TPU v7x, 256 devices: a whole 4x4x8 slice. The times are simulated.
256 devices in a mesh: seq: 32 (over x, z), head: 8 (over y, core).
Axes of the slice: x: 4, y: 4, z: 8, core: 2. Of those that a mesh axis runs over, the one named last changes fastest.
Arguments:
- queries: bfloat16 [16384, 16, 128], P('seq', 'head'), may hold values from -6 to 6
- keys: bfloat16 [16384, 16, 128], P('seq', 'head'), may hold values from -6 to 6
- values: bfloat16 [16384, 16, 256], P('seq', 'head'), may hold values from -15 to 15
- beta: float32 [16, 16384], P('head', 'seq'), may hold values from 0 to 0.9
- reset_blocks: int32 [32, 2], P('seq'), may hold values from 0 to 4, as said below
- out_weight: bfloat16 [4096, 4096], P('head'), may hold values from -0.09375 to 0.09375
Outputs:
- layer_out: bfloat16 [16384, 4096], P(('seq', 'head'))
Inputs may be any that keep to these rules, and one draw needn't show every extreme that they name: `reset_blocks`: row s lists distinct local indices (0 to 3) of the blocks of sequence shard s at which an episode begins; unused slots hold 4.
All inputs are finite; a program needn't handle non-finite values.
Results may differ from a plain program's by a relative error of at most 0.017.
Values may be sent and summed in bfloat16 or wider, within the bound.
No kernel may reach another device: no remote copies, remote signals or barrier semaphores. Data moves between devices by JAX's collectives and lax.ppermute only.
A program may use at most 64 MiB of HBM per device.

v0:
```python
import jax
import jax.numpy as jnp
from jax import lax
from jax.sharding import PartitionSpec as P

BLOCK = 128


exact_precision = lax.Precision.HIGHEST


def passed_along(x, axis, by):
    peers = lax.axis_size(axis)
    pairs = [(i, i + by) for i in range(peers) if 0 <= i + by < peers]
    return lax.ppermute(x, axis, pairs)


def unit_rows(values_in, epsilon):
    return values_in * lax.rsqrt(jnp.sum(values_in * values_in, axis=-1, keepdims=True) + epsilon)


def block_terms(query_rows, key_rows, value_rows, rate_rows):
    block_len = key_rows.shape[-2]
    key_dim = key_rows.shape[-1]
    strict = jnp.tril(jnp.ones((block_len, block_len), jnp.float32), -1)
    causal = jnp.tril(jnp.ones((block_len, block_len), jnp.float32))
    key_gram = jnp.einsum("...ik,...jk->...ij", key_rows, key_rows, precision=exact_precision)
    system = jnp.eye(block_len, dtype=jnp.float32) + rate_rows[..., :, None] * key_gram * strict
    right_side = rate_rows[..., :, None] * jnp.concatenate([key_rows, value_rows], axis=-1)
    solved = lax.linalg.triangular_solve(
        system, right_side, left_side=True, lower=True, unit_diagonal=True
    )
    attention_scores = (
        jnp.einsum("...ik,...jk->...ij", query_rows, key_rows, precision=exact_precision) * causal
    )
    return (solved[..., :key_dim], solved[..., key_dim:], attention_scores)


def body(queries, keys, values, beta, reset_blocks, out_weight):
    tok_count, head_count, key_dim = queries.shape
    value_dim = values.shape[2]
    block_count = tok_count // BLOCK
    query_rows = (
        unit_rows(queries.astype(jnp.float32), 1e-06)
        .reshape(block_count, BLOCK, head_count, key_dim)
        .transpose(0, 2, 1, 3)
    )
    key_rows = (
        unit_rows(keys.astype(jnp.float32), 1e-06)
        .reshape(block_count, BLOCK, head_count, key_dim)
        .transpose(0, 2, 1, 3)
    )
    value_rows = (
        values.astype(jnp.float32)
        .reshape(block_count, BLOCK, head_count, value_dim)
        .transpose(0, 2, 1, 3)
    )
    rate_rows = beta.reshape(head_count, block_count, BLOCK).transpose(1, 0, 2)
    local_ids = jnp.arange(block_count, dtype=jnp.int32)
    starts = jnp.any(reset_blocks[0][:, None] == local_ids[None, :], axis=0)
    retain = 1.0 - starts.astype(jnp.float32)
    decay_rows, update_rows, attention_scores = block_terms(
        query_rows, key_rows, value_rows, rate_rows
    )
    identity_key = jnp.broadcast_to(
        jnp.eye(key_dim, dtype=jnp.float32), (head_count, key_dim, key_dim)
    )
    empty_memory = jnp.zeros((head_count, key_dim, value_dim), jnp.float32)

    def step_power(power, decay_block_tile, key_block_tile):
        moved = jnp.einsum("hck,hkj->hcj", decay_block_tile, power, precision=exact_precision)
        return power - jnp.einsum("hck,hcj->hkj", key_block_tile, moved, precision=exact_precision)

    def propagate(carry, inputs):
        memory_state, power = carry
        decay_block_tile, update_block_tile, key_block_tile, kept = inputs
        memory_state = memory_state * kept
        power = power * kept
        fresh_value_rows = update_block_tile - jnp.einsum(
            "gzs,gso->gzo", decay_block_tile, memory_state, precision=exact_precision
        )
        memory_state = memory_state + jnp.einsum(
            "glq,glr->gqr", key_block_tile, fresh_value_rows, precision=exact_precision
        )
        return ((memory_state, step_power(power, decay_block_tile, key_block_tile)), None)

    (memory_state, power), _ = lax.scan(
        propagate, (empty_memory, identity_key), (decay_rows, update_rows, key_rows, retain)
    )

    def relay_step(index, carry):
        outgoing, received = carry
        received = passed_along(outgoing, "seq", 1)
        outgoing = (
            jnp.einsum("hij,hjv->hiv", power, received, precision=exact_precision) + memory_state
        )
        return (outgoing, received)

    _, incoming = lax.fori_loop(
        0, lax.axis_size("seq") - 1, relay_step, (memory_state, empty_memory)
    )

    def replay(incoming_state, inputs):
        query_block_tile, decay_block_tile, update_block_tile, key_block_tile, s_blk, kept = inputs
        incoming_state = incoming_state * kept
        fresh_value_rows = update_block_tile - jnp.einsum(
            "gzs,gso->gzo", decay_block_tile, incoming_state, precision=exact_precision
        )
        output_matrix = jnp.einsum(
            "gzs,gso->gzo", query_block_tile, incoming_state, precision=exact_precision
        ) + jnp.einsum("kra,kap->krp", s_blk, fresh_value_rows, precision=exact_precision)
        incoming_state = incoming_state + jnp.einsum(
            "glq,glr->gqr", key_block_tile, fresh_value_rows, precision=exact_precision
        )
        return (incoming_state, output_matrix)

    _, attended = lax.scan(
        replay, incoming, (query_rows, decay_rows, update_rows, key_rows, attention_scores, retain)
    )
    scaled = attended * lax.rsqrt(jnp.mean(attended * attended, axis=-1, keepdims=True) + 1e-05)
    normed = (
        scaled.astype(jnp.bfloat16).transpose(0, 2, 1, 3).reshape(tok_count, head_count * value_dim)
    )
    return lax.psum_scatter(
        jnp.dot(normed, out_weight, preferred_element_type=jnp.float32).astype(jnp.bfloat16),
        "head",
        scatter_dimension=0,
        tiled=True,
    )


def solution(mesh):
    return jax.shard_map(
        body,
        mesh=mesh,
        in_specs=(
            P("seq", "head", None),
            P("seq", "head", None),
            P("seq", "head", None),
            P("head", "seq"),
            P("seq", None),
            P("head", None),
        ),
        out_specs=P(("seq", "head"), None),
        check_vma=False,
    )
```

profile of v0, /device:TPU:4, one launch (start us, length us, event | category | flops | bytes accessed | tf_op | source)
XLA Modules:
  0.0 562.6 jit_solution(4979171304251029233)
XLA Ops:
  10.6 79.3 %custom-call.3 = f32[4,2,1,128,128]{3,4,2,1,0:T(8,128)} custom-call(f32[4,2,1,128,128]{4,3,2,1,0:T(8,128)S(1)} %fusion.45), custom_call_target="InvertDiagBlocksLowerTriangular" | custom-call | tf_op jit(solution)/shard_map/triangular_solve | solution.py:30
  96.1 16.3 %while.39 = (s32[]{:T(128)}, f32[2,128,256]{2,1,0:T(8,128)S(1)}, f32[2,128,128]{2,1,0:T(8,128)S(1)}, f32[4]{0:T(128)S(1)}, f32[4,2,128,128]{2,3,1,0:T(8,128)S(1)...) while((s32[]{:T(128)}, f32[2,128,256]{2,1,0:T(8,128)S(1)}, ...), condition=%wide.region_3.4_spmd.clone, body=%wide.region_2.0_spmd.clone.sunk | while | flops 302481408 | bytes 2754199 | solution.py:87
  112.4 367.0 %while.37 = (s32[]{:T(128)}, f32[2,128,256]{2,1,0:T(8,128)S(1)}, f32[2,128,256]{2,1,0:T(8,128)}, f32[2,128,128]{2,1,0:T(8,128)S(1)}, f32[2,128,256]{2,1,0:T(8,128)S(1)}, /*index=5*/s32[]{:T(128)}) while((s32[]{:T(128)}, f32[2,128,256]{2,1,0:T(8,128)S(1)}, f32[2,128,256]{2,1,0:T(8,128)}, f32[2,128,128]{2,1,0:T(8,128)S(1)}, ...), condition=%wide.region_5.6_spmd, body=%wide.region_4.5_spmd.sunk | while | flops 100728832 | bytes 3014793 | solution.py:99
  116.3 10.2 %collective-permute-done = f32[2,128,256]{2,1,0:T(8,128)S(1)} collective-permute-done((f32[2,128,256]{2,1,0:T(8,128)S(1)}, f32[2,128,256]{2,1,0:T(8,128)S(1)}, u32[]{:S(2)}, u32[]{:S(2)}) %collective-permute-start) | collective-permute-done | bytes 262176 | tf_op jit(solution)/shard_map/while/body/eval_jaxpr/ppermute | solution.py:15
  129.1 9.6 %collective-permute-done = f32[2,128,256]{2,1,0:T(8,128)S(1)} collective-permute-done((f32[2,128,256]{2,1,0:T(8,128)S(1)}, f32[2,128,256]{2,1,0:T(8,128)S(1)}, u32[]{:S(2)}, u32[]{:S(2)}) %collective-permute-start) | collective-permute-done | bytes 262176 | tf_op jit(solution)/shard_map/while/body/eval_jaxpr/ppermute | solution.py:15
  141.3 8.6 %collective-permute-done = f32[2,128,256]{2,1,0:T(8,128)S(1)} collective-permute-done((f32[2,128,256]{2,1,0:T(8,128)S(1)}, f32[2,128,256]{2,1,0:T(8,128)S(1)}, u32[]{:S(2)}, u32[]{:S(2)}) %collective-permute-start) | collective-permute-done | bytes 262176 | tf_op jit(solution)/shard_map/while/body/eval_jaxpr/ppermute | solution.py:15
  152.6 8.4 %collective-permute-done = f32[2,128,256]{2,1,0:T(8,128)S(1)} collective-permute-done((f32[2,128,256]{2,1,0:T(8,128)S(1)}, f32[2,128,256]{2,1,0:T(8,128)S(1)}, u32[]{:S(2)}, u32[]{:S(2)}) %collective-permute-start) | collective-permute-done | bytes 262176 | tf_op jit(solution)/shard_map/while/body/eval_jaxpr/ppermute | solution.py:15
  163.6 8.4 %collective-permute-done = f32[2,128,256]{2,1,0:T(8,128)S(1)} collective-permute-done((f32[2,128,256]{2,1,0:T(8,128)S(1)}, f32[2,128,256]{2,1,0:T(8,128)S(1)}, u32[]{:S(2)}, u32[]{:S(2)}) %collective-permute-start) | collective-permute-done | bytes 262176 | tf_op jit(solution)/shard_map/while/body/eval_jaxpr/ppermute | solution.py:15
  174.7 8.4 %collective-permute-done = f32[2,128,256]{2,1,0:T(8,128)S(1)} collective-permute-done((f32[2,128,256]{2,1,0:T(8,128)S(1)}, f32[2,128,256]{2,1,0:T(8,128)S(1)}, u32[]{:S(2)}, u32[]{:S(2)}) %collective-permute-start) | collective-permute-done | bytes 262176 | tf_op jit(solution)/shard_map/while/body/eval_jaxpr/ppermute | solution.py:15
  185.8 8.4 %collective-permute-done = f32[2,128,256]{2,1,0:T(8,128)S(1)} collective-permute-done((f32[2,128,256]{2,1,0:T(8,128)S(1)}, f32[2,128,256]{2,1,0:T(8,128)S(1)}, u32[]{:S(2)}, u32[]{:S(2)}) %collective-permute-start) | collective-permute-done | bytes 262176 | tf_op jit(solution)/shard_map/while/body/eval_jaxpr/ppermute | solution.py:15
  196.8 9.4 %collective-permute-done = f32[2,128,256]{2,1,0:T(8,128)S(1)} collective-permute-done((f32[2,128,256]{2,1,0:T(8,128)S(1)}, f32[2,128,256]{2,1,0:T(8,128)S(1)}, u32[]{:S(2)}, u32[]{:S(2)}) %collective-permute-start) | collective-permute-done | bytes 262176 | tf_op jit(solution)/shard_map/while/body/eval_jaxpr/ppermute | solution.py:15
  208.9 10.6 %collective-permute-done = f32[2,128,256]{2,1,0:T(8,128)S(1)} collective-permute-done((f32[2,128,256]{2,1,0:T(8,128)S(1)}, f32[2,128,256]{2,1,0:T(8,128)S(1)}, u32[]{:S(2)}, u32[]{:S(2)}) %collective-permute-start) | collective-permute-done | bytes 262176 | tf_op jit(solution)/shard_map/while/body/eval_jaxpr/ppermute | solution.py:15
  222.1 10.8 %collective-permute-done = f32[2,128,256]{2,1,0:T(8,128)S(1)} collective-permute-done((f32[2,128,256]{2,1,0:T(8,128)S(1)}, f32[2,128,256]{2,1,0:T(8,128)S(1)}, u32[]{:S(2)}, u32[]{:S(2)}) %collective-permute-start) | collective-permute-done | bytes 262176 | tf_op jit(solution)/shard_map/while/body/eval_jaxpr/ppermute | solution.py:15
  235.5 10.0 %collective-permute-done = f32[2,128,256]{2,1,0:T(8,128)S(1)} collective-permute-done((f32[2,128,256]{2,1,0:T(8,128)S(1)}, f32[2,128,256]{2,1,0:T(8,128)S(1)}, u32[]{:S(2)}, u32[]{:S(2)}) %collective-permute-start) | collective-permute-done | bytes 262176 | tf_op jit(solution)/shard_map/while/body/eval_jaxpr/ppermute | solution.py:15
  248.1 9.1 %collective-permute-done = f32[2,128,256]{2,1,0:T(8,128)S(1)} collective-permute-done((f32[2,128,256]{2,1,0:T(8,128)S(1)}, f32[2,128,256]{2,1,0:T(8,128)S(1)}, u32[]{:S(2)}, u32[]{:S(2)}) %collective-permute-start) | collective-permute-done | bytes 262176 | tf_op jit(solution)/shard_map/while/body/eval_jaxpr/ppermute | solution.py:15
  259.8 8.4 %collective-permute-done = f32[2,128,256]{2,1,0:T(8,128)S(1)} collective-permute-done((f32[2,128,256]{2,1,0:T(8,128)S(1)}, f32[2,128,256]{2,1,0:T(8,128)S(1)}, u32[]{:S(2)}, u32[]{:S(2)}) %collective-permute-start) | collective-permute-done | bytes 262176 | tf_op jit(solution)/shard_map/while/body/eval_jaxpr/ppermute | solution.py:15
  270.9 8.4 %collective-permute-done = f32[2,128,256]{2,1,0:T(8,128)S(1)} collective-permute-done((f32[2,128,256]{2,1,0:T(8,128)S(1)}, f32[2,128,256]{2,1,0:T(8,128)S(1)}, u32[]{:S(2)}, u32[]{:S(2)}) %collective-permute-start) | collective-permute-done | bytes 262176 | tf_op jit(solution)/shard_map/while/body/eval_jaxpr/ppermute | solution.py:15
  281.9 8.4 %collective-permute-done = f32[2,128,256]{2,1,0:T(8,128)S(1)} collective-permute-done((f32[2,128,256]{2,1,0:T(8,128)S(1)}, f32[2,128,256]{2,1,0:T(8,128)S(1)}, u32[]{:S(2)}, u32[]{:S(2)}) %collective-permute-start) | collective-permute-done | bytes 262176 | tf_op jit(solution)/shard_map/while/body/eval_jaxpr/ppermute | solution.py:15
  293.0 8.4 %collective-permute-done = f32[2,128,256]{2,1,0:T(8,128)S(1)} collective-permute-done((f32[2,128,256]{2,1,0:T(8,128)S(1)}, f32[2,128,256]{2,1,0:T(8,128)S(1)}, u32[]{:S(2)}, u32[]{:S(2)}) %collective-permute-start) | collective-permute-done | bytes 262176 | tf_op jit(solution)/shard_map/while/body/eval_jaxpr/ppermute | solution.py:15
  304.1 8.9 %collective-permute-done = f32[2,128,256]{2,1,0:T(8,128)S(1)} collective-permute-done((f32[2,128,256]{2,1,0:T(8,128)S(1)}, f32[2,128,256]{2,1,0:T(8,128)S(1)}, u32[]{:S(2)}, u32[]{:S(2)}) %collective-permute-start) | collective-permute-done | bytes 262176 | tf_op jit(solution)/shard_map/while/body/eval_jaxpr/ppermute | solution.py:15
  315.6 10.1 %collective-permute-done = f32[2,128,256]{2,1,0:T(8,128)S(1)} collective-permute-done((f32[2,128,256]{2,1,0:T(8,128)S(1)}, f32[2,128,256]{2,1,0:T(8,128)S(1)}, u32[]{:S(2)}, u32[]{:S(2)}) %collective-permute-start) | collective-permute-done | bytes 262176 | tf_op jit(solution)/shard_map/while/body/eval_jaxpr/ppermute | solution.py:15
  328.3 11.2 %collective-permute-done = f32[2,128,256]{2,1,0:T(8,128)S(1)} collective-permute-done((f32[2,128,256]{2,1,0:T(8,128)S(1)}, f32[2,128,256]{2,1,0:T(8,128)S(1)}, u32[]{:S(2)}, u32[]{:S(2)}) %collective-permute-start) | collective-permute-done | bytes 262176 | tf_op jit(solution)/shard_map/while/body/eval_jaxpr/ppermute | solution.py:15
  342.2 10.4 %collective-permute-done = f32[2,128,256]{2,1,0:T(8,128)S(1)} collective-permute-done((f32[2,128,256]{2,1,0:T(8,128)S(1)}, f32[2,128,256]{2,1,0:T(8,128)S(1)}, u32[]{:S(2)}, u32[]{:S(2)}) %collective-permute-start) | collective-permute-done | bytes 262176 | tf_op jit(solution)/shard_map/while/body/eval_jaxpr/ppermute | solution.py:15
  355.2 9.6 %collective-permute-done = f32[2,128,256]{2,1,0:T(8,128)S(1)} collective-permute-done((f32[2,128,256]{2,1,0:T(8,128)S(1)}, f32[2,128,256]{2,1,0:T(8,128)S(1)}, u32[]{:S(2)}, u32[]{:S(2)}) %collective-permute-start) | collective-permute-done | bytes 262176 | tf_op jit(solution)/shard_map/while/body/eval_jaxpr/ppermute | solution.py:15
  367.4 8.6 %collective-permute-done = f32[2,128,256]{2,1,0:T(8,128)S(1)} collective-permute-done((f32[2,128,256]{2,1,0:T(8,128)S(1)}, f32[2,128,256]{2,1,0:T(8,128)S(1)}, u32[]{:S(2)}, u32[]{:S(2)}) %collective-permute-start) | collective-permute-done | bytes 262176 | tf_op jit(solution)/shard_map/while/body/eval_jaxpr/ppermute | solution.py:15
  378.6 8.4 %collective-permute-done = f32[2,128,256]{2,1,0:T(8,128)S(1)} collective-permute-done((f32[2,128,256]{2,1,0:T(8,128)S(1)}, f32[2,128,256]{2,1,0:T(8,128)S(1)}, u32[]{:S(2)}, u32[]{:S(2)}) %collective-permute-start) | collective-permute-done | bytes 262176 | tf_op jit(solution)/shard_map/while/body/eval_jaxpr/ppermute | solution.py:15
  389.7 8.4 %collective-permute-done = f32[2,128,256]{2,1,0:T(8,128)S(1)} collective-permute-done((f32[2,128,256]{2,1,0:T(8,128)S(1)}, f32[2,128,256]{2,1,0:T(8,128)S(1)}, u32[]{:S(2)}, u32[]{:S(2)}) %collective-permute-start) | collective-permute-done | bytes 262176 | tf_op jit(solution)/shard_map/while/body/eval_jaxpr/ppermute | solution.py:15
  422.9 9.4 %collective-permute-done = f32[2,128,256]{2,1,0:T(8,128)S(1)} collective-permute-done((f32[2,128,256]{2,1,0:T(8,128)S(1)}, f32[2,128,256]{2,1,0:T(8,128)S(1)}, u32[]{:S(2)}, u32[]{:S(2)}) %collective-permute-start) | collective-permute-done | bytes 262176 | tf_op jit(solution)/shard_map/while/body/eval_jaxpr/ppermute | solution.py:15
  434.9 10.6 %collective-permute-done = f32[2,128,256]{2,1,0:T(8,128)S(1)} collective-permute-done((f32[2,128,256]{2,1,0:T(8,128)S(1)}, f32[2,128,256]{2,1,0:T(8,128)S(1)}, u32[]{:S(2)}, u32[]{:S(2)}) %collective-permute-start) | collective-permute-done | bytes 262176 | tf_op jit(solution)/shard_map/while/body/eval_jaxpr/ppermute | solution.py:15
  459.2 8.4 %collective-permute-done = f32[2,128,256]{2,1,0:T(8,128)S(1)} collective-permute-done((f32[2,128,256]{2,1,0:T(8,128)S(1)}, f32[2,128,256]{2,1,0:T(8,128)S(1)}, u32[]{:S(2)}, u32[]{:S(2)}) %collective-permute-start) | collective-permute-done | bytes 262176 | tf_op jit(solution)/shard_map/while/body/eval_jaxpr/ppermute | solution.py:15
  479.4 30.6 %while.38 = (s32[]{:T(128)}, f32[2,128,256]{2,1,0:T(8,128)}, f32[4,2,128,256]{3,2,1,0:T(8,128)}, f32[4]{0:T(128)S(1)}, f32[4,2,128,128]{2,3,1,0:T(8,128)S(1)}, /...) while((s32[]{:T(128)}, f32[2,128,256]{2,1,0:T(8,128)}, ...), condition=%wide.region_8.9_spmd, body=%wide.region_7.8_spmd.sunk | while | flops 403046400 | bytes 5507269 | solution.py:117
  518.9 36.9 %reduce-scatter.2.cloned.1.call-done = bf16[64,4096]{1,0:T(8,128)(2,1)} async-done(((bf16[512,4096]{1,0:T(8,128)(2,1)}), bf16[64,4096]{1,0:T(8,128)(2,1)}) %reduce-scatter.2.cloned.1.call-update) | async-done | bytes 524304 | tf_op jit(solution)/shard_map/reduce_scatter | solution.py:124
  (230 shorter events, 182.0 us)
Async XLA Ops:
  6.5 549.3 %reduce-scatter.2.cloned.1.call-start = ((), (), s32[]{:S(2)}) async-start(), calls=%async_computation.1 | async-start | bytes 4718592 | tf_op jit(solution)/shard_map/reduce_scatter | solution.py:124
  112.4 14.0 %collective-permute-start = (f32[2,128,256]{2,1,0:T(8,128)S(1)}, f32[2,128,256]{2,1,0:T(8,128)S(1)}, u32[]{:S(2)}, u32[]{:S(2)}) collective-permute-start(f32[2,128,256]{2,1,0:T(8,128)S(1)} %get-tuple-element.381), channel_id=1, source_target_pairs={{0,8},{8,16},{16,24},{24,32},{32,40},{40,48},{48,56},{56,64},{64,7... | collective-permute-start | bytes 786440 | tf_op jit(solution)/shard_map/while/body/eval_jaxpr/ppermute | solution.py:15
  127.2 11.5 %collective-permute-start = (f32[2,128,256]{2,1,0:T(8,128)S(1)}, f32[2,128,256]{2,1,0:T(8,128)S(1)}, u32[]{:S(2)}, u32[]{:S(2)}) collective-permute-start(f32[2,128,256]{2,1,0:T(8,128)S(1)} %get-tuple-element.381), channel_id=1, source_target_pairs={{0,8},{8,16},{16,24},{24,32},{32,40},{40,48},{48,56},{56,64},{64,7... | collective-permute-start | bytes 786440 | tf_op jit(solution)/shard_map/while/body/eval_jaxpr/ppermute | solution.py:15
  139.4 10.6 %collective-permute-start = (f32[2,128,256]{2,1,0:T(8,128)S(1)}, f32[2,128,256]{2,1,0:T(8,128)S(1)}, u32[]{:S(2)}, u32[]{:S(2)}) collective-permute-start(f32[2,128,256]{2,1,0:T(8,128)S(1)} %get-tuple-element.381), channel_id=1, source_target_pairs={{0,8},{8,16},{16,24},{24,32},{32,40},{40,48},{48,56},{56,64},{64,7... | collective-permute-start | bytes 786440 | tf_op jit(solution)/shard_map/while/body/eval_jaxpr/ppermute | solution.py:15
  150.6 10.4 %collective-permute-start = (f32[2,128,256]{2,1,0:T(8,128)S(1)}, f32[2,128,256]{2,1,0:T(8,128)S(1)}, u32[]{:S(2)}, u32[]{:S(2)}) collective-permute-start(f32[2,128,256]{2,1,0:T(8,128)S(1)} %get-tuple-element.381), channel_id=1, source_target_pairs={{0,8},{8,16},{16,24},{24,32},{32,40},{40,48},{48,56},{56,64},{64,7... | collective-permute-start | bytes 786440 | tf_op jit(solution)/shard_map/while/body/eval_jaxpr/ppermute | solution.py:15
  161.7 10.4 %collective-permute-start = (f32[2,128,256]{2,1,0:T(8,128)S(1)}, f32[2,128,256]{2,1,0:T(8,128)S(1)}, u32[]{:S(2)}, u32[]{:S(2)}) collective-permute-start(f32[2,128,256]{2,1,0:T(8,128)S(1)} %get-tuple-element.381), channel_id=1, source_target_pairs={{0,8},{8,16},{16,24},{24,32},{32,40},{40,48},{48,56},{56,64},{64,7... | collective-permute-start | bytes 786440 | tf_op jit(solution)/shard_map/while/body/eval_jaxpr/ppermute | solution.py:15
  172.8 10.4 %collective-permute-start = (f32[2,128,256]{2,1,0:T(8,128)S(1)}, f32[2,128,256]{2,1,0:T(8,128)S(1)}, u32[]{:S(2)}, u32[]{:S(2)}) collective-permute-start(f32[2,128,256]{2,1,0:T(8,128)S(1)} %get-tuple-element.381), channel_id=1, source_target_pairs={{0,8},{8,16},{16,24},{24,32},{32,40},{40,48},{48,56},{56,64},{64,7... | collective-permute-start | bytes 786440 | tf_op jit(solution)/shard_map/while/body/eval_jaxpr/ppermute | solution.py:15
  183.9 10.4 %collective-permute-start = (f32[2,128,256]{2,1,0:T(8,128)S(1)}, f32[2,128,256]{2,1,0:T(8,128)S(1)}, u32[]{:S(2)}, u32[]{:S(2)}) collective-permute-start(f32[2,128,256]{2,1,0:T(8,128)S(1)} %get-tuple-element.381), channel_id=1, source_target_pairs={{0,8},{8,16},{16,24},{24,32},{32,40},{40,48},{48,56},{56,64},{64,7... | collective-permute-start | bytes 786440 | tf_op jit(solution)/shard_map/while/body/eval_jaxpr/ppermute | solution.py:15
  194.9 11.3 %collective-permute-start = (f32[2,128,256]{2,1,0:T(8,128)S(1)}, f32[2,128,256]{2,1,0:T(8,128)S(1)}, u32[]{:S(2)}, u32[]{:S(2)}) collective-permute-start(f32[2,128,256]{2,1,0:T(8,128)S(1)} %get-tuple-element.381), channel_id=1, source_target_pairs={{0,8},{8,16},{16,24},{24,32},{32,40},{40,48},{48,56},{56,64},{64,7... | collective-permute-start | bytes 786440 | tf_op jit(solution)/shard_map/while/body/eval_jaxpr/ppermute | solution.py:15
  206.9 12.5 %collective-permute-start = (f32[2,128,256]{2,1,0:T(8,128)S(1)}, f32[2,128,256]{2,1,0:T(8,128)S(1)}, u32[]{:S(2)}, u32[]{:S(2)}) collective-permute-start(f32[2,128,256]{2,1,0:T(8,128)S(1)} %get-tuple-element.381), channel_id=1, source_target_pairs={{0,8},{8,16},{16,24},{24,32},{32,40},{40,48},{48,56},{56,64},{64,7... | collective-permute-start | bytes 786440 | tf_op jit(solution)/shard_map/while/body/eval_jaxpr/ppermute | solution.py:15
  220.1 12.7 %collective-permute-start = (f32[2,128,256]{2,1,0:T(8,128)S(1)}, f32[2,128,256]{2,1,0:T(8,128)S(1)}, u32[]{:S(2)}, u32[]{:S(2)}) collective-permute-start(f32[2,128,256]{2,1,0:T(8,128)S(1)} %get-tuple-element.381), channel_id=1, source_target_pairs={{0,8},{8,16},{16,24},{24,32},{32,40},{40,48},{48,56},{56,64},{64,7... | collective-permute-start | bytes 786440 | tf_op jit(solution)/shard_map/while/body/eval_jaxpr/ppermute | solution.py:15
  233.5 11.9 %collective-permute-start = (f32[2,128,256]{2,1,0:T(8,128)S(1)}, f32[2,128,256]{2,1,0:T(8,128)S(1)}, u32[]{:S(2)}, u32[]{:S(2)}) collective-permute-start(f32[2,128,256]{2,1,0:T(8,128)S(1)} %get-tuple-element.381), channel_id=1, source_target_pairs={{0,8},{8,16},{16,24},{24,32},{32,40},{40,48},{48,56},{56,64},{64,7... | collective-permute-start | bytes 786440 | tf_op jit(solution)/shard_map/while/body/eval_jaxpr/ppermute | solution.py:15
  246.2 11.0 %collective-permute-start = (f32[2,128,256]{2,1,0:T(8,128)S(1)}, f32[2,128,256]{2,1,0:T(8,128)S(1)}, u32[]{:S(2)}, u32[]{:S(2)}) collective-permute-start(f32[2,128,256]{2,1,0:T(8,128)S(1)} %get-tuple-element.381), channel_id=1, source_target_pairs={{0,8},{8,16},{16,24},{24,32},{32,40},{40,48},{48,56},{56,64},{64,7... | collective-permute-start | bytes 786440 | tf_op jit(solution)/shard_map/while/body/eval_jaxpr/ppermute | solution.py:15
  257.9 10.4 %collective-permute-start = (f32[2,128,256]{2,1,0:T(8,128)S(1)}, f32[2,128,256]{2,1,0:T(8,128)S(1)}, u32[]{:S(2)}, u32[]{:S(2)}) collective-permute-start(f32[2,128,256]{2,1,0:T(8,128)S(1)} %get-tuple-element.381), channel_id=1, source_target_pairs={{0,8},{8,16},{16,24},{24,32},{32,40},{40,48},{48,56},{56,64},{64,7... | collective-permute-start | bytes 786440 | tf_op jit(solution)/shard_map/while/body/eval_jaxpr/ppermute | solution.py:15
  269.0 10.4 %collective-permute-start = (f32[2,128,256]{2,1,0:T(8,128)S(1)}, f32[2,128,256]{2,1,0:T(8,128)S(1)}, u32[]{:S(2)}, u32[]{:S(2)}) collective-permute-start(f32[2,128,256]{2,1,0:T(8,128)S(1)} %get-tuple-element.381), channel_id=1, source_target_pairs={{0,8},{8,16},{16,24},{24,32},{32,40},{40,48},{48,56},{56,64},{64,7... | collective-permute-start | bytes 786440 | tf_op jit(solution)/shard_map/while/body/eval_jaxpr/ppermute | solution.py:15
  280.0 10.4 %collective-permute-start = (f32[2,128,256]{2,1,0:T(8,128)S(1)}, f32[2,128,256]{2,1,0:T(8,128)S(1)}, u32[]{:S(2)}, u32[]{:S(2)}) collective-permute-start(f32[2,128,256]{2,1,0:T(8,128)S(1)} %get-tuple-element.381), channel_id=1, source_target_pairs={{0,8},{8,16},{16,24},{24,32},{32,40},{40,48},{48,56},{56,64},{64,7... | collective-permute-start | bytes 786440 | tf_op jit(solution)/shard_map/while/body/eval_jaxpr/ppermute | solution.py:15
  291.1 10.4 %collective-permute-start = (f32[2,128,256]{2,1,0:T(8,128)S(1)}, f32[2,128,256]{2,1,0:T(8,128)S(1)}, u32[]{:S(2)}, u32[]{:S(2)}) collective-permute-start(f32[2,128,256]{2,1,0:T(8,128)S(1)} %get-tuple-element.381), channel_id=1, source_target_pairs={{0,8},{8,16},{16,24},{24,32},{32,40},{40,48},{48,56},{56,64},{64,7... | collective-permute-start | bytes 786440 | tf_op jit(solution)/shard_map/while/body/eval_jaxpr/ppermute | solution.py:15
  302.2 10.9 %collective-permute-start = (f32[2,128,256]{2,1,0:T(8,128)S(1)}, f32[2,128,256]{2,1,0:T(8,128)S(1)}, u32[]{:S(2)}, u32[]{:S(2)}) collective-permute-start(f32[2,128,256]{2,1,0:T(8,128)S(1)} %get-tuple-element.381), channel_id=1, source_target_pairs={{0,8},{8,16},{16,24},{24,32},{32,40},{40,48},{48,56},{56,64},{64,7... | collective-permute-start | bytes 786440 | tf_op jit(solution)/shard_map/while/body/eval_jaxpr/ppermute | solution.py:15
  313.7 12.0 %collective-permute-start = (f32[2,128,256]{2,1,0:T(8,128)S(1)}, f32[2,128,256]{2,1,0:T(8,128)S(1)}, u32[]{:S(2)}, u32[]{:S(2)}) collective-permute-start(f32[2,128,256]{2,1,0:T(8,128)S(1)} %get-tuple-element.381), channel_id=1, source_target_pairs={{0,8},{8,16},{16,24},{24,32},{32,40},{40,48},{48,56},{56,64},{64,7... | collective-permute-start | bytes 786440 | tf_op jit(solution)/shard_map/while/body/eval_jaxpr/ppermute | solution.py:15
  326.4 13.1 %collective-permute-start = (f32[2,128,256]{2,1,0:T(8,128)S(1)}, f32[2,128,256]{2,1,0:T(8,128)S(1)}, u32[]{:S(2)}, u32[]{:S(2)}) collective-permute-start(f32[2,128,256]{2,1,0:T(8,128)S(1)} %get-tuple-element.381), channel_id=1, source_target_pairs={{0,8},{8,16},{16,24},{24,32},{32,40},{40,48},{48,56},{56,64},{64,7... | collective-permute-start | bytes 786440 | tf_op jit(solution)/shard_map/while/body/eval_jaxpr/ppermute | solution.py:15
  340.2 12.3 %collective-permute-start = (f32[2,128,256]{2,1,0:T(8,128)S(1)}, f32[2,128,256]{2,1,0:T(8,128)S(1)}, u32[]{:S(2)}, u32[]{:S(2)}) collective-permute-start(f32[2,128,256]{2,1,0:T(8,128)S(1)} %get-tuple-element.381), channel_id=1, source_target_pairs={{0,8},{8,16},{16,24},{24,32},{32,40},{40,48},{48,56},{56,64},{64,7... | collective-permute-start | bytes 786440 | tf_op jit(solution)/shard_map/while/body/eval_jaxpr/ppermute | solution.py:15
  353.3 11.5 %collective-permute-start = (f32[2,128,256]{2,1,0:T(8,128)S(1)}, f32[2,128,256]{2,1,0:T(8,128)S(1)}, u32[]{:S(2)}, u32[]{:S(2)}) collective-permute-start(f32[2,128,256]{2,1,0:T(8,128)S(1)} %get-tuple-element.381), channel_id=1, source_target_pairs={{0,8},{8,16},{16,24},{24,32},{32,40},{40,48},{48,56},{56,64},{64,7... | collective-permute-start | bytes 786440 | tf_op jit(solution)/shard_map/while/body/eval_jaxpr/ppermute | solution.py:15
  365.4 10.6 %collective-permute-start = (f32[2,128,256]{2,1,0:T(8,128)S(1)}, f32[2,128,256]{2,1,0:T(8,128)S(1)}, u32[]{:S(2)}, u32[]{:S(2)}) collective-permute-start(f32[2,128,256]{2,1,0:T(8,128)S(1)} %get-tuple-element.381), channel_id=1, source_target_pairs={{0,8},{8,16},{16,24},{24,32},{32,40},{40,48},{48,56},{56,64},{64,7... | collective-permute-start | bytes 786440 | tf_op jit(solution)/shard_map/while/body/eval_jaxpr/ppermute | solution.py:15
  376.7 10.4 %collective-permute-start = (f32[2,128,256]{2,1,0:T(8,128)S(1)}, f32[2,128,256]{2,1,0:T(8,128)S(1)}, u32[]{:S(2)}, u32[]{:S(2)}) collective-permute-start(f32[2,128,256]{2,1,0:T(8,128)S(1)} %get-tuple-element.381), channel_id=1, source_target_pairs={{0,8},{8,16},{16,24},{24,32},{32,40},{40,48},{48,56},{56,64},{64,7... | collective-permute-start | bytes 786440 | tf_op jit(solution)/shard_map/while/body/eval_jaxpr/ppermute | solution.py:15
  387.8 10.4 %collective-permute-start = (f32[2,128,256]{2,1,0:T(8,128)S(1)}, f32[2,128,256]{2,1,0:T(8,128)S(1)}, u32[]{:S(2)}, u32[]{:S(2)}) collective-permute-start(f32[2,128,256]{2,1,0:T(8,128)S(1)} %get-tuple-element.381), channel_id=1, source_target_pairs={{0,8},{8,16},{16,24},{24,32},{32,40},{40,48},{48,56},{56,64},{64,7... | collective-permute-start | bytes 786440 | tf_op jit(solution)/shard_map/while/body/eval_jaxpr/ppermute | solution.py:15
  398.9 10.4 %collective-permute-start = (f32[2,128,256]{2,1,0:T(8,128)S(1)}, f32[2,128,256]{2,1,0:T(8,128)S(1)}, u32[]{:S(2)}, u32[]{:S(2)}) collective-permute-start(f32[2,128,256]{2,1,0:T(8,128)S(1)} %get-tuple-element.381), channel_id=1, source_target_pairs={{0,8},{8,16},{16,24},{24,32},{32,40},{40,48},{48,56},{56,64},{64,7... | collective-permute-start | bytes 786440 | tf_op jit(solution)/shard_map/while/body/eval_jaxpr/ppermute | solution.py:15
  409.9 10.4 %collective-permute-start = (f32[2,128,256]{2,1,0:T(8,128)S(1)}, f32[2,128,256]{2,1,0:T(8,128)S(1)}, u32[]{:S(2)}, u32[]{:S(2)}) collective-permute-start(f32[2,128,256]{2,1,0:T(8,128)S(1)} %get-tuple-element.381), channel_id=1, source_target_pairs={{0,8},{8,16},{16,24},{24,32},{32,40},{40,48},{48,56},{56,64},{64,7... | collective-permute-start | bytes 786440 | tf_op jit(solution)/shard_map/while/body/eval_jaxpr/ppermute | solution.py:15
  421.0 11.3 %collective-permute-start = (f32[2,128,256]{2,1,0:T(8,128)S(1)}, f32[2,128,256]{2,1,0:T(8,128)S(1)}, u32[]{:S(2)}, u32[]{:S(2)}) collective-permute-start(f32[2,128,256]{2,1,0:T(8,128)S(1)} %get-tuple-element.381), channel_id=1, source_target_pairs={{0,8},{8,16},{16,24},{24,32},{32,40},{40,48},{48,56},{56,64},{64,7... | collective-permute-start | bytes 786440 | tf_op jit(solution)/shard_map/while/body/eval_jaxpr/ppermute | solution.py:15
  433.0 12.5 %collective-permute-start = (f32[2,128,256]{2,1,0:T(8,128)S(1)}, f32[2,128,256]{2,1,0:T(8,128)S(1)}, u32[]{:S(2)}, u32[]{:S(2)}) collective-permute-start(f32[2,128,256]{2,1,0:T(8,128)S(1)} %get-tuple-element.381), channel_id=1, source_target_pairs={{0,8},{8,16},{16,24},{24,32},{32,40},{40,48},{48,56},{56,64},{64,7... | collective-permute-start | bytes 786440 | tf_op jit(solution)/shard_map/while/body/eval_jaxpr/ppermute | solution.py:15
  446.2 10.4 %collective-permute-start = (f32[2,128,256]{2,1,0:T(8,128)S(1)}, f32[2,128,256]{2,1,0:T(8,128)S(1)}, u32[]{:S(2)}, u32[]{:S(2)}) collective-permute-start(f32[2,128,256]{2,1,0:T(8,128)S(1)} %get-tuple-element.381), channel_id=1, source_target_pairs={{0,8},{8,16},{16,24},{24,32},{32,40},{40,48},{48,56},{56,64},{64,7... | collective-permute-start | bytes 786440 | tf_op jit(solution)/shard_map/while/body/eval_jaxpr/ppermute | solution.py:15
  457.3 10.4 %collective-permute-start = (f32[2,128,256]{2,1,0:T(8,128)S(1)}, f32[2,128,256]{2,1,0:T(8,128)S(1)}, u32[]{:S(2)}, u32[]{:S(2)}) collective-permute-start(f32[2,128,256]{2,1,0:T(8,128)S(1)} %get-tuple-element.381), channel_id=1, source_target_pairs={{0,8},{8,16},{16,24},{24,32},{32,40},{40,48},{48,56},{56,64},{64,7... | collective-permute-start | bytes 786440 | tf_op jit(solution)/shard_map/while/body/eval_jaxpr/ppermute | solution.py:15
  468.4 10.4 %collective-permute-start = (f32[2,128,256]{2,1,0:T(8,128)S(1)}, f32[2,128,256]{2,1,0:T(8,128)S(1)}, u32[]{:S(2)}, u32[]{:S(2)}) collective-permute-start(f32[2,128,256]{2,1,0:T(8,128)S(1)} %get-tuple-element.381), channel_id=1, source_target_pairs={{0,8},{8,16},{16,24},{24,32},{32,40},{40,48},{48,56},{56,64},{64,7... | collective-permute-start | bytes 786440 | tf_op jit(solution)/shard_map/while/body/eval_jaxpr/ppermute | solution.py:15
  (45 other events, 137.3 us)
Sparse Core Ops, SparseCore 0:
  519.0 36.7 reduce-scatter.1
where the time goes:
time: 564 us; the launch traced here: 563 us
  waiting for transfers between devices  321 us (57%)
  other arithmetic  84.1 us (15%)
  matrix products  64.5 us (11%)
  starting transfers between devices  61.1 us (11%)
  local copies, waits for them, and re-layouts  17.8 us (3%)
  between operations  13.6 us (2%)
    ppermute x31, waiting for transfers between devices, passed_along(): return lax.ppermute(x, axis, pairs)  284 us
    another operation x4, other arithmetic, block_terms(): lax.linalg.triangular_solve(system, right_side, left_side=True, lower=Tru...  79.4 us
    ppermute x31, starting transfers between devices, passed_along(): return lax.ppermute(x, axis, pairs)  61.1 us
    reduce_scatter x1, waiting for transfers between devices, body(): lax.psum_scatter(jnp.dot(normed, out_weight, preferred_element_type=jnp.f...  36.9 us
    dot_general x31, matrix products, relay_step(): jnp.einsum('hij,hjv->hiv', power, received, precision=exact_precision)  11.3 us
  transfers between devices with their start and end apart: 32, of which 32 were waited for; matrix products, arithmetic and copies ran while one was open for 0% of the time, Pallas kernels for 0%

commit v1 on v0

v1 whole, which is shorter than its diff:
```python
import jax
import jax.numpy as jnp
from jax import lax
from jax.experimental import pallas as pl
from jax.experimental.pallas import tpu as pltpu
from jax.sharding import PartitionSpec as P

BLOCK = 128
INTERPRET = False
VMEM_LIMIT = 48 << 20
F32 = jnp.float32
BF16 = jnp.bfloat16


def split(x):
    high = x.astype(BF16)
    return high, (x - high.astype(F32)).astype(BF16)


def dot(a, b):
    return jnp.dot(a, b, preferred_element_type=F32)


def dot_t(a, b):
    return lax.dot_general(a, b, (((0,), (0,)), ((), ())), preferred_element_type=F32)


def dot_nt(a, b):
    return lax.dot_general(a, b, (((1,), (1,)), ((), ())), preferred_element_type=F32)


def dot3(a, b):
    a_high, a_low = split(a)
    b_high, b_low = split(b)
    both = dot(jnp.concatenate([a_high, a_low], 1), jnp.concatenate([b_high, b_high], 0))
    return both + dot(a_high, b_low)


def dot2_right(a, b):
    b_high, b_low = split(b)
    return dot(jnp.concatenate([a, a], 1), jnp.concatenate([b_high, b_low], 0))


def dot2_left(a, b):
    a_high, a_low = split(a)
    return dot(jnp.concatenate([a_high, a_low], 1), jnp.concatenate([b, b], 0))


def square_ids(n):
    return lax.broadcasted_iota(jnp.int32, (n, n), 0), lax.broadcasted_iota(jnp.int32, (n, n), 1)


def terms_kernel(resets, k_ref, v_ref, beta_ref, wu_ref, prefix_ref, scale_ref, carry_ref):
    row, col = square_ids(BLOCK)
    eye = row == col
    identity = jnp.where(eye, 1.0, 0.0).astype(F32)
    cells = [(b, h) for b in range(4) for h in range(2)]
    ks, vs, grams = {}, {}, {}
    for b, h in cells:
        ks[b, h] = k_ref[b * BLOCK : (b + 1) * BLOCK, h * 128 : (h + 1) * 128]
        vs[b, h] = v_ref[b * BLOCK : (b + 1) * BLOCK, h * 256 : (h + 1) * 256]
        grams[b, h] = dot_nt(ks[b, h], ks[b, h])
    lower, inv, r_cols, beta_rows, c_rows = {}, {}, {}, {}, {}
    for b, h in cells:
        gram = grams[b, h]
        diagonal = jnp.where(eye, gram, 0.0)
        r_col = lax.rsqrt(jnp.sum(diagonal, axis=1, keepdims=True) + 1e-06)
        r_row = lax.rsqrt(jnp.sum(diagonal, axis=0, keepdims=True) + 1e-06)
        beta_row = beta_ref[h : h + 1, b * BLOCK : (b + 1) * BLOCK]
        beta_col = jnp.sum(jnp.where(eye, beta_row, 0.0), axis=1, keepdims=True)
        low = jnp.where(row > col, (beta_col * r_col) * gram * r_row, 0.0)
        lower[b, h] = low
        inv[b, h] = identity - jnp.where(row // 2 == col // 2, low, 0.0)
        r_cols[b, h] = r_col
        beta_rows[b, h] = beta_row
        c_rows[b, h] = beta_row * r_row
        scale_ref[b * 2 + h : b * 2 + h + 1, :] = r_row
    size = 2
    while size < BLOCK:
        joined = (row // (2 * size) == col // (2 * size)) & (row // size != col // size)
        half = {}
        for cell in cells:
            half[cell] = dot3(jnp.where(joined, lower[cell], 0.0), inv[cell])
        for cell in cells:
            inv[cell] = inv[cell] - dot3(inv[cell], half[cell])
        size *= 2
    steps = {}
    for b, h in cells:
        cell = (b, h)
        decay = dot2_left(inv[cell] * c_rows[cell], ks[cell])
        update = dot2_left(inv[cell] * beta_rows[cell], vs[cell])
        wu = jnp.concatenate([decay, update], 1)
        wu_ref[b * 2 + h] = wu
        high, low = split(wu * r_cols[cell])
        steps[cell] = dot_t(
            jnp.concatenate([ks[cell], ks[cell]], 0), jnp.concatenate([high, low], 0)
        )
    zeros = jnp.zeros((BLOCK, 256), F32)
    state = {h: jnp.concatenate([identity, zeros], 1) for h in range(2)}
    for b in range(4):
        starts = (resets[0] == b) | (resets[1] == b)
        kept = jnp.where(starts, 0.0, 1.0).astype(F32)
        for h in range(2):
            before = state[h] * kept
            prefix_ref[b * 2 + h] = before
            step = steps[b, h]
            added = jnp.concatenate([jnp.zeros((BLOCK, 128), F32), step[:, 128:]], 1)
            if b == 0:
                moved = jnp.concatenate([step[:, :128] * kept, zeros], 1)
            else:
                moved = dot3(step[:, :128], before)
            state[h] = before - moved + added
    for h in range(2):
        carry_ref[h] = jnp.concatenate(
            [state[h][:, :128] - identity, state[h][:, 128:]], 1
        ).astype(BF16)


def response_kernel(q_ref, k_ref, scale_ref, wu_ref, prefix_ref, r_ref, o_ref):
    row, col = square_ids(BLOCK)
    causal = row >= col
    for b in range(4):
        for h in range(2):
            cell = b * 2 + h
            q = q_ref[b * BLOCK : (b + 1) * BLOCK, h * 128 : (h + 1) * 128]
            k = k_ref[b * BLOCK : (b + 1) * BLOCK, h * 128 : (h + 1) * 128]
            qf = q.astype(F32)
            rq = lax.rsqrt(jnp.sum(qf * qf, axis=1, keepdims=True) + 1e-06)
            scores = jnp.where(causal, rq * dot_nt(q, k) * scale_ref[cell : cell + 1, :], 0.0)
            local = dot3(scores, wu_ref[cell])
            reach = qf * rq - local[:, :128]
            out = dot3(reach, prefix_ref[cell])
            r_ref[cell] = out[:, :128].astype(BF16)
            o_ref[cell] = out[:, 128:] + local[:, 128:]


def follow(state, element):
    moved = dot2_right(element[:, :128], state)
    width = state.shape[1]
    added = element.astype(F32)
    if width == 256:
        added = added[:, 128:]
    else:
        added = jnp.concatenate([jnp.zeros((BLOCK, 128), F32), added[:, 128:]], 1)
    return state + moved + added


def group_kernel(place, *refs):
    elements, (before_ref, total_ref) = refs[:8], refs[8:]
    row, col = square_ids(BLOCK)
    identity = jnp.where(row == col, 1.0, 0.0).astype(F32)
    empty = jnp.concatenate([identity, jnp.zeros((BLOCK, 256), F32)], 1)
    z = place[0]
    state = {h: empty for h in range(2)}
    after = {h: empty for h in range(2)}
    for step in range(1, 8):
        wraps = z + step == 8
        for h in range(2):
            if step > 1:
                after[h] = jnp.where(wraps, state[h], after[h])
                state[h] = jnp.where(wraps, empty, state[h])
            state[h] = follow(state[h], elements[step][h])
    for h in range(2):
        after[h] = jnp.where(z == 0, state[h], after[h])
        state[h] = jnp.where(z == 0, empty, state[h])
        before_ref[h] = jnp.concatenate([state[h][:, :128] - identity, state[h][:, 128:]], 1)
        through = follow(state[h], elements[0][h])
        total = dot3(after[h][:, :128], through)
        total_ref[h] = jnp.concatenate(
            [total[:, :128] - identity, total[:, 128:] + after[h][:, 128:]], 1
        ).astype(BF16)


def output_kernel(place, far_ref, mid_ref, near_ref, before_ref, r_ref, o_ref, keep_ref, send_ref):
    y, core = place[1], place[2]
    states = []
    for h in range(2):
        state = far_ref[h][:, 128:].astype(F32)
        state = follow(state, mid_ref[h])
        state = follow(state, near_ref[h])
        before = before_ref[h]
        states.append(state + dot3(before[:, :128], state) + before[:, 128:])
    for b in range(4):
        parts = []
        for h in range(2):
            cell = b * 2 + h
            out = dot2_right(r_ref[cell], states[h]) + o_ref[cell]
            mean = jnp.mean(out * out, axis=1, keepdims=True)
            parts.append((out * lax.rsqrt(mean + 1e-05)).astype(BF16))
        normed = jnp.concatenate(parts, 1)
        first, second = normed[:64], normed[64:]
        slot = pl.multiple_of(((4 - (y ^ b)) & 3) * 64, 64)
        keep_ref[pl.ds(slot, 64), :] = jnp.where(core == 0, first, second)
        send_ref[pl.ds(slot, 64), :] = jnp.where(core == 0, second, first)


SMEM = pl.BlockSpec(memory_space=pltpu.SMEM)
VMEM = pl.BlockSpec(memory_space=pltpu.VMEM)


def call(kernel, outs, scalars, arrays, flops):
    moved = sum(a.size * a.dtype.itemsize for a in list(arrays) + list(outs))
    return pl.pallas_call(
        kernel,
        out_shape=outs,
        in_specs=[SMEM] + [VMEM] * len(arrays) if scalars is not None else [VMEM] * len(arrays),
        out_specs=[VMEM] * len(outs),
        compiler_params=pltpu.CompilerParams(vmem_limit_bytes=VMEM_LIMIT),
        cost_estimate=pl.CostEstimate(flops=flops, bytes_accessed=moved, transcendentals=0),
        interpret=INTERPRET,
    )(*([scalars] if scalars is not None else []), *arrays)


def body(queries, keys, values, beta, reset_blocks, out_weight):
    q = queries.reshape(512, 256)
    k = keys.reshape(512, 256)
    v = values.reshape(512, 512)
    shard = lax.axis_index("seq")
    head = lax.axis_index("head")
    place = jnp.stack([shard % 8, head // 2, head % 2]).astype(jnp.int32)

    across = [(i, i ^ 1) for i in range(8)]
    other_weight = lax.ppermute(out_weight, "head", across)

    shaped = jax.ShapeDtypeStruct
    wu, prefix, scale, carry = call(
        terms_kernel,
        [
            shaped((8, 128, 384), F32),
            shaped((8, 128, 384), F32),
            shaped((8, 128), F32),
            shaped((2, 128, 384), BF16),
        ],
        reset_blocks.reshape(2),
        [k, v, beta],
        3_000_000_000,
    )
    up = [(i, i - i % 8 + (i + 1) % 8) for i in range(32)]
    down = [(i, i - i % 8 + (i + 7) % 8) for i in range(32)]
    below, above = [carry], [carry]
    for step in range(4):
        below.append(lax.ppermute(below[-1], "seq", up))
        if step < 3:
            above.append(lax.ppermute(above[-1], "seq", down))
    response, own_out = call(
        response_kernel,
        [shaped((8, 128, 128), BF16), shaped((8, 128, 256), F32)],
        None,
        [q, k, scale, wu, prefix],
        2_000_000_000,
    )
    before, total = call(
        group_kernel,
        [shaped((2, 128, 384), F32), shaped((2, 128, 384), BF16)],
        place,
        above + below[:0:-1],
        1_000_000_000,
    )
    received = [
        lax.ppermute(total, "seq", [(i, i + 8 * d) for i in range(32) if i + 8 * d < 32])
        for d in (3, 2, 1)
    ]
    keep, send = call(
        output_kernel,
        [shaped((256, 512), BF16), shaped((256, 512), BF16)],
        place,
        received + [before, response, own_out],
        500_000_000,
    )
    joined = lax.ppermute(send, "head", across)

    def product(first, last, low, high):
        return (
            dot(keep[first:last], out_weight[:, low:high])
            + dot(joined[first:last], other_weight[:, low:high])
        ).astype(BF16)

    near = [(i, i ^ 2) for i in range(8)]
    far = [(i, 7 - i ^ 1) for i in range(8)]
    sent_a = lax.ppermute(product(128, 256, 0, 2048), "head", near)
    sent_b = lax.ppermute(product(64, 192, 2048, 4096), "head", far)
    own_a = product(0, 128, 0, 2048)
    own_b0 = product(0, 64, 2048, 4096)
    own_b3 = product(192, 256, 2048, 4096)

    def add(x, y):
        return x.astype(F32) + y.astype(F32)

    next_a = lax.ppermute(add(own_a[64:], sent_a[:64]).astype(BF16), "head", far)
    next_b = lax.ppermute(add(own_b3, sent_b[64:]).astype(BF16), "head", near)
    out_a = (add(own_a[:64], sent_a[64:]) + next_a.astype(F32)).astype(BF16)
    out_b = (add(own_b0, sent_b[:64]) + next_b.astype(F32)).astype(BF16)
    return jnp.concatenate([out_a, out_b], 1)


def solution(mesh):
    return jax.shard_map(
        body,
        mesh=mesh,
        in_specs=(
            P("seq", "head", None),
            P("seq", "head", None),
            P("seq", "head", None),
            P("head", "seq"),
            P("seq", None),
            P("head", None),
        ),
        out_specs=P(("seq", "head"), None),
        check_vma=False,
    )
```

time: 564 us -> 98.8 us (0.18)
  waiting for transfers between devices: 321 us -> 36.2 us
  other arithmetic: 84.1 us -> 1.07 us
  matrix products: 64.5 us -> 12.7 us
  starting transfers between devices: 61.1 us -> 25.3 us
  between operations: 13.6 us -> 0.22 us
  Pallas kernels: 0 us -> 13.2 us
  local copies, waits for them, and re-layouts: 17.8 us -> 8.7 us
    ppermute x31 -> x16, waiting for transfers between devices: 284 us -> 36.2 us  [the longest x4 20.9 us: body(): below.append(lax.ppermute(below[-1], 'seq', up))]
    another operation x4 -> x1, other arithmetic: 79.4 us -> 0.08 us  [body(): place = jnp.stack([shard % 8, head // 2, head % 2]).astype(jnp.int32)]
    dot_general x66 -> x10, matrix products: 62.8 us -> 12.7 us  [dot(): return jnp.dot(a, b, preferred_element_type=F32)]
    reduce_scatter x1 -> x0, waiting for transfers between devices: 36.9 us -> none  [body(): lax.psum_scatter(jnp.dot(normed, out_weight, preferred_element_type=jnp.f...]
    ppermute x31 -> x16, starting transfers between devices: 61.1 us -> 25.3 us  [the longest x3 10.4 us: body(): above.append(lax.ppermute(above[-1], 'seq', down))]
    pallas_call x0 -> x4, Pallas kernels: none -> 13.2 us  [call(): pl.pallas_call(kernel, out_shape=outs, in_specs=[SMEM] + [VMEM] * len(arr...]
    while x79 -> x0, local copies, waits for them, and re-layouts: 10.4 us -> none
    unnamed x14 -> x15, local copies, waits for them, and re-layouts: 1.77 us -> 7.6 us
  transfers between devices with their start and end apart: 32 -> 16, of which waited for: 32 -> 10; matrix products, arithmetic and copies ran while one was open for 0% -> 10% of each run, Pallas kernels for 0% -> 14%
where the time goes in v1:
time: 98.8 us; the launch traced here: 97.4 us
  waiting for transfers between devices  36.2 us (37%)
  starting transfers between devices  25.3 us (26%)
  Pallas kernels  13.2 us (13%)
  matrix products  12.7 us (13%)
  local copies, waits for them, and re-layouts  8.7 us (9%)
  other arithmetic  1.07 us (1%)
    ppermute x4, waiting for transfers between devices, body(): below.append(lax.ppermute(below[-1], 'seq', up))  20.9 us
    pallas_call x4, Pallas kernels, call(): pl.pallas_call(kernel, out_shape=outs, in_specs=[SMEM] + [VMEM] * len(arr...  13.2 us
    dot_general x10, matrix products, dot(): return jnp.dot(a, b, preferred_element_type=F32)  12.7 us
    ppermute x3, starting transfers between devices, body(): above.append(lax.ppermute(above[-1], 'seq', down))  10.4 us
    unnamed x15, local copies, waits for them, and re-layouts  7.6 us
    ppermute x3, starting transfers between devices, body(): lax.ppermute(total, 'seq', [(i, i + 8 * d) for i in range(32) if i + 8 *...  5.65 us
    ppermute x1, waiting for transfers between devices, body(): lax.ppermute(add(own_a[64:], sent_a[:64]).astype(BF16), 'head', far)  3.89 us
    ppermute x1, waiting for transfers between devices, body(): sent_a = lax.ppermute(product(128, 256, 0, 2048), 'head', near)  3.37 us
  transfers between devices with their start and end apart: 16, of which 10 were waited for; matrix products, arithmetic and copies ran while one was open for 10% of the time, Pallas kernels for 14%

profile of v1, /device:TPU:4, one launch (start us, length us, event | category | flops | bytes accessed | tf_op | source)
XLA Modules:
  0.0 97.4 jit_solution(16078906049044233366)
XLA Ops:
  0.0 1.1 %copy.8 = bf16[64,8,2,256]{3,1,2,0:T(8,128)(2,1)S(1)} copy(bf16[64,8,2,256]{3,2,1,0:T(2,128)(2,1)} %bitcast.14) | data formatting | bytes 1048576
  3.6 5.9 %shard_map.64 = (f32[8,128,384]{2,1,0:T(8,128)S(1)}, f32[8,128,384]{2,1,0:T(8,128)S(1)}, f32[8,128]{1,0:T(8,128)S(1)}, bf16[2,128,384]{2,1,0:T(8,128)(2,1)S(1)}) custom-call(s32[2]{0:T(128)S(1)} %bitcast.13, bf16[512,256]{1,0:T(8,128)(2,1)S(1)} %get-tuple-element.26.k_ref, bf16[512,512]{1,0:T(8,128)(2,1)S(1)} %bitcast.12, f32[2,512]{1,0:T(2,128)S(1)} %copy-done), custom_call_target="tpu_custom_call" | custom-call | flops 3000000000 | bytes 4136960 | tf_op jit(solution)/shard_map/pallas_call | solution.py:203
  9.5 1.2 %copy-done.2 = f32[8,128,384]{2,1,0:T(8,128)} copy-done((f32[8,128,384]{2,1,0:T(8,128)}, f32[8,128,384]{2,1,0:T(8,128)S(1)}, u32[]{:S(2)}) %copy-start.2) | copy-done | bytes 1572888
  10.7 1.1 %copy-done.4 = f32[8,128,384]{2,1,0:T(8,128)} copy-done((f32[8,128,384]{2,1,0:T(8,128)}, f32[8,128,384]{2,1,0:T(8,128)S(1)}, u32[]{:S(2)}) %copy-start.4) | copy-done | bytes 1572888
  11.8 1.9 %collective-permute-start.3 = (bf16[2,128,384]{2,1,0:T(8,128)(2,1)S(1)}, bf16[2,128,384]{2,1,0:T(8,128)(2,1)S(1)}, u32[]{:S(2)}, u32[]{:S(2)}) collective-permute-start(bf16[2,128,384]{2,1,0:T(8,128)(2,1)S(1)} %get-tuple-element.15.refs_0_), channel_id=1, source_target_pairs={{0,8},{8,16},{16,24},{24,32},{32,40},{40,48},{48,56},{56,0},{64,72... | collective-permute-start | bytes 589832 | tf_op jit(solution)/shard_map/ppermute | solution.py:242
  13.7 3.9 %collective-permute-start = (bf16[2,128,384]{2,1,0:T(8,128)(2,1)S(1)}, bf16[2,128,384]{2,1,0:T(8,128)(2,1)S(1)}, u32[]{:S(2)}, u32[]{:S(2)}) collective-permute-start(bf16[2,128,384]{2,1,0:T(8,128)(2,1)S(1)} %get-tuple-element.15.refs_0_), channel_id=1, source_target_pairs={{0,56},{8,0},{16,8},{24,16},{32,24},{40,32},{48,40},{56,48},{64,12... | collective-permute-start | bytes 589832 | tf_op jit(solution)/shard_map/ppermute | solution.py:244
  17.7 5.6 %collective-permute-done.3.refs_7_ = bf16[2,128,384]{2,1,0:T(8,128)(2,1)S(1)} collective-permute-done((bf16[2,128,384]{2,1,0:T(8,128)(2,1)S(1)}, bf16[2,128,384]{2,1,0:T(8,128)(2,1)S(1)}, u32[]{:S(2)}, u32[]{:S(2)}) %collective-permute-start.3) | collective-permute-done | bytes 196640 | tf_op jit(solution)/shard_map/ppermute | solution.py:242
  23.2 3.2 %collective-permute-start.1 = (bf16[2,128,384]{2,1,0:T(8,128)(2,1)S(1)}, bf16[2,128,384]{2,1,0:T(8,128)(2,1)S(1)}, u32[]{:S(2)}, u32[]{:S(2)}) collective-permute-start(bf16[2,128,384]{2,1,0:T(8,128)(2,1)S(1)} %collective-permute-done.refs_1_), channel_id=1, source_target_pairs={{0,56},{8,0},{16,8},{24,16},{32,24},{40,32},{48,40},{56,48},{64,12... | collective-permute-start | bytes 589832 | tf_op jit(solution)/shard_map/ppermute | solution.py:244
  26.5 4.7 %collective-permute-done.4.refs_6_ = bf16[2,128,384]{2,1,0:T(8,128)(2,1)S(1)} collective-permute-done((bf16[2,128,384]{2,1,0:T(8,128)(2,1)S(1)}, bf16[2,128,384]{2,1,0:T(8,128)(2,1)S(1)}, u32[]{:S(2)}, u32[]{:S(2)}) %collective-permute-start.4) | collective-permute-done | bytes 196640 | tf_op jit(solution)/shard_map/ppermute | solution.py:242
  31.2 3.2 %collective-permute-start.2 = (bf16[2,128,384]{2,1,0:T(8,128)(2,1)S(1)}, bf16[2,128,384]{2,1,0:T(8,128)(2,1)S(1)}, u32[]{:S(2)}, u32[]{:S(2)}) collective-permute-start(bf16[2,128,384]{2,1,0:T(8,128)(2,1)S(1)} %collective-permute-done.1.refs_2_), channel_id=1, source_target_pairs={{0,56},{8,0},{16,8},{24,16},{32,24},{40,32},{48,40},{56,48},{64,12... | collective-permute-start | bytes 589832 | tf_op jit(solution)/shard_map/ppermute | solution.py:244
  34.4 3.9 %collective-permute-done.5.refs_5_ = bf16[2,128,384]{2,1,0:T(8,128)(2,1)S(1)} collective-permute-done((bf16[2,128,384]{2,1,0:T(8,128)(2,1)S(1)}, bf16[2,128,384]{2,1,0:T(8,128)(2,1)S(1)}, u32[]{:S(2)}, u32[]{:S(2)}) %collective-permute-start.5) | collective-permute-done | bytes 196640 | tf_op jit(solution)/shard_map/ppermute | solution.py:242
  38.4 6.8 %collective-permute-done.6.refs_4_ = bf16[2,128,384]{2,1,0:T(8,128)(2,1)S(1)} collective-permute-done((bf16[2,128,384]{2,1,0:T(8,128)(2,1)S(1)}, bf16[2,128,384]{2,1,0:T(8,128)(2,1)S(1)}, u32[]{:S(2)}, u32[]{:S(2)}) %collective-permute-start.6) | collective-permute-done | bytes 196640 | tf_op jit(solution)/shard_map/ppermute | solution.py:242
  45.2 2.4 %shard_map.65 = (f32[2,128,384]{2,1,0:T(8,128)S(1)}, bf16[2,128,384]{2,1,0:T(8,128)(2,1)S(1)}) custom-call(s32[3]{0:T(128)S(1)} %pad_add_fusion.place, bf16[2,128,384]{2,1,0:T(8,128)(2,1)S(1)} %get-tuple-element.15.refs_0_, bf16[2,128,384]{2,1,0:T(8,128)(2,1)S(1)} %collective-permute-done.refs_1_, bf16[2,128,384]{2,1,0:T(8,128)(2,1)S(1)} %collective-permute-done.1.refs_2_, ...), custom_call_target="tpu_custom_call" | custom-call | flops 1000000000 | bytes 2162688 | tf_op jit(solution)/shard_map/pallas_call | solution.py:203
  48.2 1.3 %collective-permute-start.8 = (bf16[2,128,384]{2,1,0:T(8,128)(2,1)S(1)}, bf16[2,128,384]{2,1,0:T(8,128)(2,1)S(1)}, u32[]{:S(2)}, u32[]{:S(2)}) collective-permute-start(bf16[2,128,384]{2,1,0:T(8,128)(2,1)S(1)} %get-tuple-element.16), channel_id=1, source_target_pairs={{0,128},{8,136},{16,144},{24,152},{32,160},{40,168},{48,176},{56,1... | collective-permute-start | bytes 589832 | tf_op jit(solution)/shard_map/ppermute | solution.py:260
  49.5 3.7 %collective-permute-start.9 = (bf16[2,128,384]{2,1,0:T(8,128)(2,1)S(1)}, bf16[2,128,384]{2,1,0:T(8,128)(2,1)S(1)}, u32[]{:S(2)}, u32[]{:S(2)}) collective-permute-start(bf16[2,128,384]{2,1,0:T(8,128)(2,1)S(1)} %get-tuple-element.16), channel_id=1, source_target_pairs={{0,64},{8,72},{16,80},{24,88},{32,96},{40,104},{48,112},{56,120},{... | collective-permute-start | bytes 589832 | tf_op jit(solution)/shard_map/ppermute | solution.py:260
  53.3 1.4 %copy-done.3 = f32[8,128,384]{2,1,0:T(8,128)S(1)} copy-done((f32[8,128,384]{2,1,0:T(8,128)S(1)}, f32[8,128,384]{2,1,0:T(8,128)}, u32[]{:S(2)}) %copy-start.3) | copy-done | bytes 1572888
  54.7 1.4 %copy-done.5 = f32[8,128,384]{2,1,0:T(8,128)S(1)} copy-done((f32[8,128,384]{2,1,0:T(8,128)S(1)}, f32[8,128,384]{2,1,0:T(8,128)}, u32[]{:S(2)}) %copy-start.5) | copy-done | bytes 1572888
  56.1 3.2 %shard_map.66 = (bf16[8,128,128]{2,1,0:T(8,128)(2,1)S(1)}, f32[8,128,256]{2,1,0:T(8,128)S(1)}) custom-call(bf16[512,256]{1,0:T(8,128)(2,1)S(1)} %get-tuple-element.25.q_ref, bf16[512,256]{1,0:T(8,128)(2,1)S(1)} %get-tuple-element.26.k_ref, f32[8,128]{1,0:T(8,128)S(1)} %get-tuple-element.18.scale_ref, f32[8,128,384]{2,1,0:T(8,128)S(1)} %copy-done.3, ...), custom_call_target="tpu_custom_call" | custom-call | flops 2000000000 | bytes 4984832 | tf_op jit(solution)/shard_map/pallas_call | solution.py:203
  60.4 1.7 %shard_map.67 = (bf16[256,512]{1,0:T(8,128)(2,1)S(1)}, bf16[256,512]{1,0:T(8,128)(2,1)S(1)}) custom-call(s32[3]{0:T(128)S(1)} %pad_add_fusion.place, bf16[2,128,384]{2,1,0:T(8,128)(2,1)S(1)} %collective-permute-done.7.far_ref, bf16[2,128,384]{2,1,0:T(8,128)(2,1)S(1)} %collective-permute-done.8.mid_ref, ...), custom_call_target="tpu_custom_call" | custom-call | flops 500000000 | bytes 2818048 | tf_op jit(solution)/shard_map/pallas_call | solution.py:203
  62.1 1.5 %collective-permute-done.10 = bf16[256,512]{1,0:T(8,128)(2,1)S(1)} collective-permute-done((bf16[256,512]{1,0:T(8,128)(2,1)S(1)}, bf16[256,512]{1,0:T(8,128)(2,1)S(1)}, u32[]{:S(2)}, u32[]{:S(2)}) %collective-permute-start.10) | collective-permute-done | bytes 262176 | tf_op jit(solution)/shard_map/ppermute | solution.py:270
  63.7 2.1 %fusion.14 = f32[128,2048]{1,0:T(8,128)S(1)} fusion(bf16[512,4096]{1,0:T(8,128)(2,1)} %collective-permute-done.11, bf16[256,512]{1,0:T(8,128)(2,1)S(1)} %collective-permute-done.10), kind=kOutput, calls=%fused_computation.19 | convolution fusion | flops 268435456 | bytes 3276800 | tf_op jit(solution)/shard_map/dot_general | solution.py:21
  66.2 2.1 %fusion.12 = f32[128,2048]{1,0:T(8,128)S(1)} fusion(bf16[512,4096]{1,0:T(8,128)(2,1)} %collective-permute-done.11, bf16[256,512]{1,0:T(8,128)(2,1)S(1)} %collective-permute-done.10), kind=kOutput, calls=%fused_computation.17 | convolution fusion | flops 268435456 | bytes 3276800 | tf_op jit(solution)/shard_map/dot_general | solution.py:21
  68.7 1.7 %collective-permute-start.12 = (bf16[128,2048]{1,0:T(8,128)(2,1)S(1)}, bf16[128,2048]{1,0:T(8,128)(2,1)S(1)}, u32[]{:S(2)}, u32[]{:S(2)}) collective-permute-start(bf16[128,2048]{1,0:T(8,128)(2,1)S(1)} %fusion.1), channel_id=1, source_target_pairs={{0,2},{1,3},{2,0},{3,1},{4,6},{5,7},{6,4},{7,5},{8,10},{9,11},{10,... | collective-permute-start | bytes 1572872 | tf_op jit(solution)/shard_map/ppermute | solution.py:280
  70.4 2.1 %fusion.20 = f32[128,2048]{1,0:T(8,128)S(1)} fusion(bf16[512,4096]{1,0:T(8,128)(2,1)} %collective-permute-done.11, bf16[256,512]{1,0:T(8,128)(2,1)S(1)} %collective-permute-done.10), kind=kOutput, calls=%fused_computation.25 | convolution fusion | flops 268435456 | bytes 3276800 | tf_op jit(solution)/shard_map/dot_general | solution.py:21
  72.9 2.3 %collective-permute-start.14 = (bf16[128,2048]{1,0:T(8,128)(2,1)S(1)}, bf16[128,2048]{1,0:T(8,128)(2,1)S(1)}, u32[]{:S(2)}, u32[]{:S(2)}) collective-permute-start(bf16[128,2048]{1,0:T(8,128)(2,1)S(1)} %fusion.2), channel_id=1, source_target_pairs={{0,6},{1,7},{2,4},{3,5},{4,2},{5,3},{6,0},{7,1},{8,14},{9,15},{10,... | collective-permute-start | bytes 1572872 | tf_op jit(solution)/shard_map/ppermute | solution.py:281
  75.2 2.1 %fusion.18 = f32[64,2048]{1,0:T(8,128)S(1)} fusion(bf16[512,4096]{1,0:T(8,128)(2,1)} %collective-permute-done.11, bf16[256,512]{1,0:T(8,128)(2,1)S(1)} %collective-permute-done.10), kind=kOutput, calls=%fused_computation.23 | convolution fusion | flops 134217728 | bytes 2686976 | tf_op jit(solution)/shard_map/dot_general | solution.py:21
  77.3 2.1 %fusion.22 = f32[64,2048]{1,0:T(8,128)S(1)} fusion(bf16[512,4096]{1,0:T(8,128)(2,1)} %collective-permute-done.11, bf16[256,512]{1,0:T(8,128)(2,1)S(1)} %collective-permute-done.10), kind=kOutput, calls=%fused_computation.27 | convolution fusion | flops 134217728 | bytes 2686976 | tf_op jit(solution)/shard_map/dot_general | solution.py:21
  79.4 3.4 %collective-permute-done.12 = bf16[128,2048]{1,0:T(8,128)(2,1)S(1)} collective-permute-done((bf16[128,2048]{1,0:T(8,128)(2,1)S(1)}, bf16[128,2048]{1,0:T(8,128)(2,1)S(1)}, u32[]{:S(2)}, u32[]{:S(2)}) %collective-permute-start.12) | collective-permute-done | bytes 524320 | tf_op jit(solution)/shard_map/ppermute | solution.py:280
  82.8 3.2 %collective-permute-start.13 = (bf16[64,2048]{1,0:T(8,128)(2,1)S(1)}, bf16[64,2048]{1,0:T(8,128)(2,1)S(1)}, u32[]{:S(2)}, u32[]{:S(2)}) collective-permute-start(bf16[64,2048]{1,0:T(8,128)(2,1)S(1)} %add_convert_fusion.1), channel_id=1, source_target_pairs={{0,6},{1,7},{2,4},{3,5},{4,2},{5,3},{6,0},{7,1},{8,14},{9,15},{10,... | collective-permute-start | bytes 786440 | tf_op jit(solution)/shard_map/ppermute | solution.py:289
  86.0 3.0 %collective-permute-done.14 = bf16[128,2048]{1,0:T(8,128)(2,1)S(1)} collective-permute-done((bf16[128,2048]{1,0:T(8,128)(2,1)S(1)}, bf16[128,2048]{1,0:T(8,128)(2,1)S(1)}, u32[]{:S(2)}, u32[]{:S(2)}) %collective-permute-start.14) | collective-permute-done | bytes 524320 | tf_op jit(solution)/shard_map/ppermute | solution.py:281
  89.6 3.9 %collective-permute-done.13 = bf16[64,2048]{1,0:T(8,128)(2,1)S(1)} collective-permute-done((bf16[64,2048]{1,0:T(8,128)(2,1)S(1)}, bf16[64,2048]{1,0:T(8,128)(2,1)S(1)}, u32[]{:S(2)}, u32[]{:S(2)}) %collective-permute-start.13) | collective-permute-done | bytes 262176 | tf_op jit(solution)/shard_map/ppermute | solution.py:289
  93.6 2.4 %collective-permute-done.15 = bf16[64,2048]{1,0:T(8,128)(2,1)S(1)} collective-permute-done((bf16[64,2048]{1,0:T(8,128)(2,1)S(1)}, bf16[64,2048]{1,0:T(8,128)(2,1)S(1)}, u32[]{:S(2)}, u32[]{:S(2)}) %collective-permute-start.15) | collective-permute-done | bytes 262176 | tf_op jit(solution)/shard_map/ppermute | solution.py:290
  (34 shorter events, 7.8 us)
Async XLA Ops:
  0.0 63.7 %collective-permute-start.11 = (bf16[512,4096]{1,0:T(8,128)(2,1)}, bf16[512,4096]{1,0:T(8,128)(2,1)}, u32[]{:S(2)}, u32[]{:S(2)}) collective-permute-start(bf16[512,4096]{1,0:T(8,128)(2,1)} %param.11), channel_id=1, source_target_pairs={{0,1},{1,0},{2,3},{3,2},{4,5},{5,4},{6,7},{7,6},{8,9},{9,8},{10,11... | collective-permute-start | bytes 12582920 | tf_op jit(solution)/shard_map/ppermute | solution.py:223
  2.2 0.7 copy-start
  2.9 0.7 copy-start.1
  9.5 1.2 %copy-start.2 = (f32[8,128,384]{2,1,0:T(8,128)}, f32[8,128,384]{2,1,0:T(8,128)S(1)}, u32[]{:S(2)}) copy-start(f32[8,128,384]{2,1,0:T(8,128)S(1)} %get-tuple-element.19.wu_ref) | copy-start | bytes 4718596
  10.7 1.1 %copy-start.4 = (f32[8,128,384]{2,1,0:T(8,128)}, f32[8,128,384]{2,1,0:T(8,128)S(1)}, u32[]{:S(2)}) copy-start(f32[8,128,384]{2,1,0:T(8,128)S(1)} %get-tuple-element.20.prefix_ref) | copy-start | bytes 4718596
  11.8 11.4 %collective-permute-start.3 = (bf16[2,128,384]{2,1,0:T(8,128)(2,1)S(1)}, bf16[2,128,384]{2,1,0:T(8,128)(2,1)S(1)}, u32[]{:S(2)}, u32[]{:S(2)}) collective-permute-start(bf16[2,128,384]{2,1,0:T(8,128)(2,1)S(1)} %get-tuple-element.15.refs_0_), channel_id=1, source_target_pairs={{0,8},{8,16},{16,24},{24,32},{32,40},{40,48},{48,56},{56,0},{64,72... | collective-permute-start | bytes 589832 | tf_op jit(solution)/shard_map/ppermute | solution.py:242
  13.7 9.5 %collective-permute-start = (bf16[2,128,384]{2,1,0:T(8,128)(2,1)S(1)}, bf16[2,128,384]{2,1,0:T(8,128)(2,1)S(1)}, u32[]{:S(2)}, u32[]{:S(2)}) collective-permute-start(bf16[2,128,384]{2,1,0:T(8,128)(2,1)S(1)} %get-tuple-element.15.refs_0_), channel_id=1, source_target_pairs={{0,56},{8,0},{16,8},{24,16},{32,24},{40,32},{48,40},{56,48},{64,12... | collective-permute-start | bytes 589832 | tf_op jit(solution)/shard_map/ppermute | solution.py:244
  23.2 8.0 %collective-permute-start.4 = (bf16[2,128,384]{2,1,0:T(8,128)(2,1)S(1)}, bf16[2,128,384]{2,1,0:T(8,128)(2,1)S(1)}, u32[]{:S(2)}, u32[]{:S(2)}) collective-permute-start(bf16[2,128,384]{2,1,0:T(8,128)(2,1)S(1)} %collective-permute-done.3.refs_7_), channel_id=1, source_target_pairs={{0,8},{8,16},{16,24},{24,32},{32,40},{40,48},{48,56},{56,0},{64,72... | collective-permute-start | bytes 589832 | tf_op jit(solution)/shard_map/ppermute | solution.py:242
  23.2 8.0 %collective-permute-start.1 = (bf16[2,128,384]{2,1,0:T(8,128)(2,1)S(1)}, bf16[2,128,384]{2,1,0:T(8,128)(2,1)S(1)}, u32[]{:S(2)}, u32[]{:S(2)}) collective-permute-start(bf16[2,128,384]{2,1,0:T(8,128)(2,1)S(1)} %collective-permute-done.refs_1_), channel_id=1, source_target_pairs={{0,56},{8,0},{16,8},{24,16},{32,24},{40,32},{48,40},{56,48},{64,12... | collective-permute-start | bytes 589832 | tf_op jit(solution)/shard_map/ppermute | solution.py:244
  31.2 7.1 %collective-permute-start.5 = (bf16[2,128,384]{2,1,0:T(8,128)(2,1)S(1)}, bf16[2,128,384]{2,1,0:T(8,128)(2,1)S(1)}, u32[]{:S(2)}, u32[]{:S(2)}) collective-permute-start(bf16[2,128,384]{2,1,0:T(8,128)(2,1)S(1)} %collective-permute-done.4.refs_6_), channel_id=1, source_target_pairs={{0,8},{8,16},{16,24},{24,32},{32,40},{40,48},{48,56},{56,0},{64,72... | collective-permute-start | bytes 589832 | tf_op jit(solution)/shard_map/ppermute | solution.py:242
  31.2 7.2 %collective-permute-start.2 = (bf16[2,128,384]{2,1,0:T(8,128)(2,1)S(1)}, bf16[2,128,384]{2,1,0:T(8,128)(2,1)S(1)}, u32[]{:S(2)}, u32[]{:S(2)}) collective-permute-start(bf16[2,128,384]{2,1,0:T(8,128)(2,1)S(1)} %collective-permute-done.1.refs_2_), channel_id=1, source_target_pairs={{0,56},{8,0},{16,8},{24,16},{32,24},{40,32},{48,40},{56,48},{64,12... | collective-permute-start | bytes 589832 | tf_op jit(solution)/shard_map/ppermute | solution.py:244
  38.3 6.9 %collective-permute-start.6 = (bf16[2,128,384]{2,1,0:T(8,128)(2,1)S(1)}, bf16[2,128,384]{2,1,0:T(8,128)(2,1)S(1)}, u32[]{:S(2)}, u32[]{:S(2)}) collective-permute-start(bf16[2,128,384]{2,1,0:T(8,128)(2,1)S(1)} %collective-permute-done.5.refs_5_), channel_id=1, source_target_pairs={{0,8},{8,16},{16,24},{24,32},{32,40},{40,48},{48,56},{56,0},{64,72... | collective-permute-start | bytes 589832 | tf_op jit(solution)/shard_map/ppermute | solution.py:242
  47.6 11.7 %collective-permute-start.7 = (bf16[2,128,384]{2,1,0:T(8,128)(2,1)S(1)}, bf16[2,128,384]{2,1,0:T(8,128)(2,1)S(1)}, u32[]{:S(2)}, u32[]{:S(2)}) collective-permute-start(bf16[2,128,384]{2,1,0:T(8,128)(2,1)S(1)} %get-tuple-element.16), channel_id=1, source_target_pairs={{0,192},{8,200},{16,208},{24,216},{32,224},{40,232},{48,240},{56,2... | collective-permute-start | bytes 589832 | tf_op jit(solution)/shard_map/ppermute | solution.py:260
  48.2 11.1 %collective-permute-start.8 = (bf16[2,128,384]{2,1,0:T(8,128)(2,1)S(1)}, bf16[2,128,384]{2,1,0:T(8,128)(2,1)S(1)}, u32[]{:S(2)}, u32[]{:S(2)}) collective-permute-start(bf16[2,128,384]{2,1,0:T(8,128)(2,1)S(1)} %get-tuple-element.16), channel_id=1, source_target_pairs={{0,128},{8,136},{16,144},{24,152},{32,160},{40,168},{48,176},{56,1... | collective-permute-start | bytes 589832 | tf_op jit(solution)/shard_map/ppermute | solution.py:260
  49.5 10.8 %collective-permute-start.9 = (bf16[2,128,384]{2,1,0:T(8,128)(2,1)S(1)}, bf16[2,128,384]{2,1,0:T(8,128)(2,1)S(1)}, u32[]{:S(2)}, u32[]{:S(2)}) collective-permute-start(bf16[2,128,384]{2,1,0:T(8,128)(2,1)S(1)} %get-tuple-element.16), channel_id=1, source_target_pairs={{0,64},{8,72},{16,80},{24,88},{32,96},{40,104},{48,112},{56,120},{... | collective-permute-start | bytes 589832 | tf_op jit(solution)/shard_map/ppermute | solution.py:260
  53.2 1.4 %copy-start.3 = (f32[8,128,384]{2,1,0:T(8,128)S(1)}, f32[8,128,384]{2,1,0:T(8,128)}, u32[]{:S(2)}) copy-start(f32[8,128,384]{2,1,0:T(8,128)} %copy-done.2) | copy-start | bytes 4718596
  54.7 1.4 %copy-start.5 = (f32[8,128,384]{2,1,0:T(8,128)S(1)}, f32[8,128,384]{2,1,0:T(8,128)}, u32[]{:S(2)}) copy-start(f32[8,128,384]{2,1,0:T(8,128)} %copy-done.4) | copy-start | bytes 4718596
  59.3 6.5 %copy-start.6 = (bf16[512,4096]{1,0:T(8,128)(2,1)S(1)}, bf16[512,4096]{1,0:T(8,128)(2,1)}, u32[]{:S(2)}) copy-start(bf16[512,4096]{1,0:T(8,128)(2,1)} %param.11) | copy-start | bytes 12582916
  62.0 1.6 %collective-permute-start.10 = (bf16[256,512]{1,0:T(8,128)(2,1)S(1)}, bf16[256,512]{1,0:T(8,128)(2,1)S(1)}, u32[]{:S(2)}, u32[]{:S(2)}) collective-permute-start(bf16[256,512]{1,0:T(8,128)(2,1)S(1)} %get-tuple-element.24), channel_id=1, source_target_pairs={{0,1},{1,0},{2,3},{3,2},{4,5},{5,4},{6,7},{7,6},{8,9},{9,8},{10,11... | collective-permute-start | bytes 786440 | tf_op jit(solution)/shard_map/ppermute | solution.py:270
  68.7 14.0 %collective-permute-start.12 = (bf16[128,2048]{1,0:T(8,128)(2,1)S(1)}, bf16[128,2048]{1,0:T(8,128)(2,1)S(1)}, u32[]{:S(2)}, u32[]{:S(2)}) collective-permute-start(bf16[128,2048]{1,0:T(8,128)(2,1)S(1)} %fusion.1), channel_id=1, source_target_pairs={{0,2},{1,3},{2,0},{3,1},{4,6},{5,7},{6,4},{7,5},{8,10},{9,11},{10,... | collective-permute-start | bytes 1572872 | tf_op jit(solution)/shard_map/ppermute | solution.py:280
  72.9 16.1 %collective-permute-start.14 = (bf16[128,2048]{1,0:T(8,128)(2,1)S(1)}, bf16[128,2048]{1,0:T(8,128)(2,1)S(1)}, u32[]{:S(2)}, u32[]{:S(2)}) collective-permute-start(bf16[128,2048]{1,0:T(8,128)(2,1)S(1)} %fusion.2), channel_id=1, source_target_pairs={{0,6},{1,7},{2,4},{3,5},{4,2},{5,3},{6,0},{7,1},{8,14},{9,15},{10,... | collective-permute-start | bytes 1572872 | tf_op jit(solution)/shard_map/ppermute | solution.py:281
  82.8 10.7 %collective-permute-start.13 = (bf16[64,2048]{1,0:T(8,128)(2,1)S(1)}, bf16[64,2048]{1,0:T(8,128)(2,1)S(1)}, u32[]{:S(2)}, u32[]{:S(2)}) collective-permute-start(bf16[64,2048]{1,0:T(8,128)(2,1)S(1)} %add_convert_fusion.1), channel_id=1, source_target_pairs={{0,6},{1,7},{2,4},{3,5},{4,2},{5,3},{6,0},{7,1},{8,14},{9,15},{10,... | collective-permute-start | bytes 786440 | tf_op jit(solution)/shard_map/ppermute | solution.py:289
  89.5 6.5 %collective-permute-start.15 = (bf16[64,2048]{1,0:T(8,128)(2,1)S(1)}, bf16[64,2048]{1,0:T(8,128)(2,1)S(1)}, u32[]{:S(2)}, u32[]{:S(2)}) collective-permute-start(bf16[64,2048]{1,0:T(8,128)(2,1)S(1)} %fusion.11), channel_id=1, source_target_pairs={{0,2},{1,3},{2,0},{3,1},{4,6},{5,7},{6,4},{7,5},{8,10},{9,11},{10,... | collective-permute-start | bytes 786440 | tf_op jit(solution)/shard_map/ppermute | solution.py:290

commit v2 on v1

--- a/solution.py
+++ b/solution.py
@@ -1,3 +1,5 @@
+import functools
+
 import jax
 import jax.numpy as jnp
 from jax import lax
@@ -7,7 +9,7 @@
 
 BLOCK = 128
 INTERPRET = False
-VMEM_LIMIT = 48 << 20
+VMEM_LIMIT = 12 << 20
 F32 = jnp.float32
 BF16 = jnp.bfloat16
 
@@ -145,12 +147,12 @@
     return state + moved + added
 
 
-def group_kernel(place, *refs):
+def group_kernel(*refs):
     elements, (before_ref, total_ref) = refs[:8], refs[8:]
     row, col = square_ids(BLOCK)
     identity = jnp.where(row == col, 1.0, 0.0).astype(F32)
     empty = jnp.concatenate([identity, jnp.zeros((BLOCK, 256), F32)], 1)
-    z = place[0]
+    z = lax.axis_index("seq") % 8
     state = {h: empty for h in range(2)}
     after = {h: empty for h in range(2)}
     for step in range(1, 8):
@@ -171,8 +173,9 @@
         ).astype(BF16)
 
 
-def output_kernel(place, far_ref, mid_ref, near_ref, before_ref, r_ref, o_ref, keep_ref, send_ref):
-    y, core = place[1], place[2]
+def output_kernel(far_ref, mid_ref, near_ref, before_ref, r_ref, o_ref, keep_ref, send_ref):
+    head = lax.axis_index("head")
+    y, core = head // 2, head % 2
     states = []
     for h in range(2):
         state = far_ref[h][:, 128:].astype(F32)
@@ -211,14 +214,42 @@
     )(*([scalars] if scalars is not None else []), *arrays)
 
 
+def product_kernel(crossed, keep_ref, joined_ref, own_w_ref, other_w_ref, send_ref, own_ref):
+    out = dot(keep_ref[...], own_w_ref[...]) + dot(joined_ref[...], other_w_ref[...])
+    out = out.astype(BF16)
+    if crossed:
+        send_ref[...] = out[64:192]
+        own_ref[:64] = out[:64]
+        own_ref[64:] = out[192:]
+    else:
+        send_ref[...] = out[128:]
+        own_ref[...] = out[:128]
+
+
+def product(crossed, keep, joined, own_weight, other_weight):
+    tile = 512
+    first = 2048 // tile if crossed else 0
+    rows = pl.BlockSpec((256, 512), lambda i: (0, 0))
+    columns = pl.BlockSpec((512, tile), lambda i: (0, i + first))
+    out = pl.BlockSpec((128, tile), lambda i: (0, i))
+    return pl.pallas_call(
+        functools.partial(product_kernel, crossed),
+        grid=(2048 // tile,),
+        out_shape=[jax.ShapeDtypeStruct((128, 2048), BF16)] * 2,
+        in_specs=[rows, rows, columns, columns],
+        out_specs=[out, out],
+        compiler_params=pltpu.CompilerParams(vmem_limit_bytes=VMEM_LIMIT),
+        cost_estimate=pl.CostEstimate(
+            flops=1_000_000_000, bytes_accessed=6_000_000, transcendentals=0
+        ),
+        interpret=INTERPRET,
+    )(keep, joined, own_weight, other_weight)
+
+
 def body(queries, keys, values, beta, reset_blocks, out_weight):
     q = queries.reshape(512, 256)
     k = keys.reshape(512, 256)
     v = values.reshape(512, 512)
-    shard = lax.axis_index("seq")
-    head = lax.axis_index("head")
-    place = jnp.stack([shard % 8, head // 2, head % 2]).astype(jnp.int32)
-
     across = [(i, i ^ 1) for i in range(8)]
     other_weight = lax.ppermute(out_weight, "head", across)
 
@@ -235,13 +266,6 @@
         [k, v, beta],
         3_000_000_000,
     )
-    up = [(i, i - i % 8 + (i + 1) % 8) for i in range(32)]
-    down = [(i, i - i % 8 + (i + 7) % 8) for i in range(32)]
-    below, above = [carry], [carry]
-    for step in range(4):
-        below.append(lax.ppermute(below[-1], "seq", up))
-        if step < 3:
-            above.append(lax.ppermute(above[-1], "seq", down))
     response, own_out = call(
         response_kernel,
         [shaped((8, 128, 128), BF16), shaped((8, 128, 256), F32)],
@@ -249,10 +273,22 @@
         [q, k, scale, wu, prefix],
         2_000_000_000,
     )
+    up = [(i, i - i % 8 + (i + 1) % 8) for i in range(32)]
+    down = [(i, i - i % 8 + (i + 7) % 8) for i in range(32)]
+    below, above = [carry], [carry]
+    for step in range(4):
+        lower = lax.ppermute(below[-1], "seq", up)
+        below.append(lower)
+        if step < 3:
+            above.append(lax.ppermute(above[-1], "seq", down))
+        if step == 0:
+            below[1], above[1], response, own_out = lax.optimization_barrier(
+                (below[1], above[1], response, own_out)
+            )
     before, total = call(
         group_kernel,
         [shaped((2, 128, 384), F32), shaped((2, 128, 384), BF16)],
-        place,
+        None,
         above + below[:0:-1],
         1_000_000_000,
     )
@@ -263,33 +299,26 @@
     keep, send = call(
         output_kernel,
         [shaped((256, 512), BF16), shaped((256, 512), BF16)],
-        place,
+        None,
         received + [before, response, own_out],
         500_000_000,
     )
     joined = lax.ppermute(send, "head", across)
 
-    def product(first, last, low, high):
-        return (
-            dot(keep[first:last], out_weight[:, low:high])
-            + dot(joined[first:last], other_weight[:, low:high])
-        ).astype(BF16)
-
     near = [(i, i ^ 2) for i in range(8)]
-    far = [(i, 7 - i ^ 1) for i in range(8)]
-    sent_a = lax.ppermute(product(128, 256, 0, 2048), "head", near)
-    sent_b = lax.ppermute(product(64, 192, 2048, 4096), "head", far)
-    own_a = product(0, 128, 0, 2048)
-    own_b0 = product(0, 64, 2048, 4096)
-    own_b3 = product(192, 256, 2048, 4096)
+    far = [(i, i ^ 6) for i in range(8)]
+    send_a, own_a = product(False, keep, joined, out_weight, other_weight)
+    sent_a = lax.ppermute(send_a, "head", near)
+    send_b, own_b = product(True, keep, joined, out_weight, other_weight)
+    sent_b = lax.ppermute(send_b, "head", far)
 
     def add(x, y):
         return x.astype(F32) + y.astype(F32)
 
     next_a = lax.ppermute(add(own_a[64:], sent_a[:64]).astype(BF16), "head", far)
-    next_b = lax.ppermute(add(own_b3, sent_b[64:]).astype(BF16), "head", near)
+    next_b = lax.ppermute(add(own_b[64:], sent_b[64:]).astype(BF16), "head", near)
     out_a = (add(own_a[:64], sent_a[64:]) + next_a.astype(F32)).astype(BF16)
-    out_b = (add(own_b0, sent_b[:64]) + next_b.astype(F32)).astype(BF16)
+    out_b = (add(own_b[:64], sent_b[:64]) + next_b.astype(F32)).astype(BF16)
     return jnp.concatenate([out_a, out_b], 1)
 
 

time: 98.8 us -> 90.3 us (0.914); the launches traced: 97.4 us -> 90 us
  matrix products: 12.7 us -> 0 us
  waiting for transfers between devices: 36.2 us -> 43.2 us
  local copies, waits for them, and re-layouts: 8.7 us -> 3.57 us
  Pallas kernels: 13.2 us -> 16.5 us
    dot_general x10 -> x0, matrix products: 12.7 us -> none  [dot(): return jnp.dot(a, b, preferred_element_type=F32)]
    ppermute x3, waiting for transfers between devices: 1.06 us -> 7.11 us  [body(): lax.ppermute(total, 'seq', [(i, i + 8 * d) for i in range(32) if i + 8 *...]
    unnamed x15 -> x7, local copies, waits for them, and re-layouts: 7.6 us -> 2.47 us
    pallas_call x0 -> x2, Pallas kernels: none -> 4.42 us  [product(): pl.pallas_call(functools.partial(product_kernel, crossed), grid=(2048 //...]
    pallas_call x4, Pallas kernels: 13.2 us -> 12.1 us  [call(): pl.pallas_call(kernel, out_shape=outs, in_specs=[SMEM] + [VMEM] * len(arr...]
  transfers between devices with their start and end apart: 16 -> 16, of which waited for: 10 -> 11; matrix products, arithmetic and copies ran while one was open for 10% -> 3% of each run, Pallas kernels for 14% -> 16%
where the time goes in v2:
time: 90.3 us; the launch traced here: 90 us
  waiting for transfers between devices  43.2 us (48%)
  starting transfers between devices  25.4 us (28%)
  Pallas kernels  16.5 us (18%)
  local copies, waits for them, and re-layouts  3.57 us (4%)
  other arithmetic  1.15 us (1%)
    ppermute x4, waiting for transfers between devices, body(): lower = lax.ppermute(below[-1], 'seq', up)  17.7 us
    pallas_call x4, Pallas kernels, call(): pl.pallas_call(kernel, out_shape=outs, in_specs=[SMEM] + [VMEM] * len(arr...  12.1 us
    ppermute x3, starting transfers between devices, body(): above.append(lax.ppermute(above[-1], 'seq', down))  10.5 us
    ppermute x1, waiting for transfers between devices, body(): sent_a = lax.ppermute(send_a, 'head', near)  7.92 us
    ppermute x3, waiting for transfers between devices, body(): lax.ppermute(total, 'seq', [(i, i + 8 * d) for i in range(32) if i + 8 *...  7.11 us
    ppermute x3, starting transfers between devices, body(): lax.ppermute(total, 'seq', [(i, i + 8 * d) for i in range(32) if i + 8 *...  5.66 us
    pallas_call x2, Pallas kernels, product(): pl.pallas_call(functools.partial(product_kernel, crossed), grid=(2048 //...  4.42 us
    ppermute x1, waiting for transfers between devices, body(): lax.ppermute(add(own_a[64:], sent_a[:64]).astype(BF16), 'head', far)  4.33 us
  transfers between devices with their start and end apart: 16, of which 11 were waited for; matrix products, arithmetic and copies ran while one was open for 3% of the time, Pallas kernels for 16%

profile of v2, /device:TPU:4, one launch (start us, length us, event | category | flops | bytes accessed | tf_op | source)
XLA Modules:
  0.0 90.0 jit_solution(6506941875086592104)
XLA Ops:
  0.0 1.1 %copy.8 = bf16[64,8,2,256]{3,1,2,0:T(8,128)(2,1)S(1)} copy(bf16[64,8,2,256]{3,2,1,0:T(2,128)(2,1)} %bitcast.11) | data formatting | bytes 1048576
  1.1 1.1 %copy_bitcast_fusion = (bf16[512,256]{1,0:T(8,128)(2,1)S(1)}, bf16[512,256]{1,0:T(8,128)(2,1)S(1)}) fusion(bf16[64,8,2,128]{3,2,1,0:T(2,128)(2,1)} %bitcast.12, bf16[64,8,2,128]{3,2,1,0:T(2,128)(2,1)} %bitcast.13), kind=kLoop, calls=%fused_computation.5 | loop fusion | bytes 1048576 | tf_op jit(solution)/shard_map/reshape | solution.py:250
  2.3 0.7 copy-done.1
  2.9 0.7 copy-done.2
  3.6 5.9 %shard_map.64 = (f32[8,128,384]{2,1,0:T(8,128)S(1)}, f32[8,128,384]{2,1,0:T(8,128)S(1)}, f32[8,128]{1,0:T(8,128)S(1)}, bf16[2,128,384]{2,1,0:T(8,128)(2,1)S(1)}) custom-call(s32[2]{0:T(128)S(1)} %bitcast.10, bf16[512,256]{1,0:T(8,128)(2,1)S(1)} %get-tuple-element.42.k_ref, bf16[512,512]{1,0:T(8,128)(2,1)S(1)} %bitcast.9, f32[2,512]{1,0:T(2,128)S(1)} %copy-done.1), custom_call_target="tpu_custom_call" | custom-call | flops 3000000000 | bytes 4136960 | tf_op jit(solution)/shard_map/pallas_call | solution.py:206
  9.5 2.0 %collective-permute-start = (bf16[2,128,384]{2,1,0:T(8,128)(2,1)S(1)}, bf16[2,128,384]{2,1,0:T(8,128)(2,1)S(1)}, u32[]{:S(2)}, u32[]{:S(2)}) collective-permute-start(bf16[2,128,384]{2,1,0:T(8,128)(2,1)S(1)} %get-tuple-element.23.refs_0_), channel_id=1, source_target_pairs={{0,8},{8,16},{16,24},{24,32},{32,40},{40,48},{48,56},{56,0},{64,72... | collective-permute-start | bytes 589832 | tf_op jit(solution)/shard_map/ppermute | solution.py:280
  11.5 4.0 %collective-permute-start.1 = (bf16[2,128,384]{2,1,0:T(8,128)(2,1)S(1)}, bf16[2,128,384]{2,1,0:T(8,128)(2,1)S(1)}, u32[]{:S(2)}, u32[]{:S(2)}) collective-permute-start(bf16[2,128,384]{2,1,0:T(8,128)(2,1)S(1)} %get-tuple-element.23.refs_0_), channel_id=1, source_target_pairs={{0,56},{8,0},{16,8},{24,16},{32,24},{40,32},{48,40},{56,48},{64,12... | collective-permute-start | bytes 589832 | tf_op jit(solution)/shard_map/ppermute | solution.py:283
  15.5 3.2 %shard_map.65 = (bf16[8,128,128]{2,1,0:T(8,128)(2,1)S(1)}, f32[8,128,256]{2,1,0:T(8,128)S(1)}) custom-call(bf16[512,256]{1,0:T(8,128)(2,1)S(1)} %get-tuple-element.41.q_ref, bf16[512,256]{1,0:T(8,128)(2,1)S(1)} %get-tuple-element.42.k_ref, f32[8,128]{1,0:T(8,128)S(1)} %get-tuple-element.24.scale_ref, f32[8,128,384]{2,1,0:T(8,128)S(1)} %get-tuple-element.25.wu_ref, ...), custom_call_target="tpu_custom_call" | custom-call | flops 2000000000 | bytes 4984832 | tf_op jit(solution)/shard_map/pallas_call | solution.py:206
  18.8 2.2 %collective-permute-done.refs_7_ = bf16[2,128,384]{2,1,0:T(8,128)(2,1)S(1)} collective-permute-done((bf16[2,128,384]{2,1,0:T(8,128)(2,1)S(1)}, bf16[2,128,384]{2,1,0:T(8,128)(2,1)S(1)}, u32[]{:S(2)}, u32[]{:S(2)}) %collective-permute-start) | collective-permute-done | bytes 196640 | tf_op jit(solution)/shard_map/ppermute | solution.py:280
  21.0 3.2 %collective-permute-start.2 = (bf16[2,128,384]{2,1,0:T(8,128)(2,1)S(1)}, bf16[2,128,384]{2,1,0:T(8,128)(2,1)S(1)}, u32[]{:S(2)}, u32[]{:S(2)}) collective-permute-start(bf16[2,128,384]{2,1,0:T(8,128)(2,1)S(1)} %collective-permute-done.1.refs_1_), channel_id=1, source_target_pairs={{0,56},{8,0},{16,8},{24,16},{32,24},{40,32},{48,40},{56,48},{64,12... | collective-permute-start | bytes 589832 | tf_op jit(solution)/shard_map/ppermute | solution.py:283
  24.2 4.7 %collective-permute-done.4.refs_6_ = bf16[2,128,384]{2,1,0:T(8,128)(2,1)S(1)} collective-permute-done((bf16[2,128,384]{2,1,0:T(8,128)(2,1)S(1)}, bf16[2,128,384]{2,1,0:T(8,128)(2,1)S(1)}, u32[]{:S(2)}, u32[]{:S(2)}) %collective-permute-start.4) | collective-permute-done | bytes 196640 | tf_op jit(solution)/shard_map/ppermute | solution.py:280
  29.0 3.2 %collective-permute-start.3 = (bf16[2,128,384]{2,1,0:T(8,128)(2,1)S(1)}, bf16[2,128,384]{2,1,0:T(8,128)(2,1)S(1)}, u32[]{:S(2)}, u32[]{:S(2)}) collective-permute-start(bf16[2,128,384]{2,1,0:T(8,128)(2,1)S(1)} %collective-permute-done.2.refs_2_), channel_id=1, source_target_pairs={{0,56},{8,0},{16,8},{24,16},{32,24},{40,32},{48,40},{56,48},{64,12... | collective-permute-start | bytes 589832 | tf_op jit(solution)/shard_map/ppermute | solution.py:283
  32.2 3.9 %collective-permute-done.5.refs_5_ = bf16[2,128,384]{2,1,0:T(8,128)(2,1)S(1)} collective-permute-done((bf16[2,128,384]{2,1,0:T(8,128)(2,1)S(1)}, bf16[2,128,384]{2,1,0:T(8,128)(2,1)S(1)}, u32[]{:S(2)}, u32[]{:S(2)}) %collective-permute-start.5) | collective-permute-done | bytes 196640 | tf_op jit(solution)/shard_map/ppermute | solution.py:280
  36.1 6.9 %collective-permute-done.6.refs_4_ = bf16[2,128,384]{2,1,0:T(8,128)(2,1)S(1)} collective-permute-done((bf16[2,128,384]{2,1,0:T(8,128)(2,1)S(1)}, bf16[2,128,384]{2,1,0:T(8,128)(2,1)S(1)}, u32[]{:S(2)}, u32[]{:S(2)}) %collective-permute-start.6) | collective-permute-done | bytes 196640 | tf_op jit(solution)/shard_map/ppermute | solution.py:280
  42.9 1.9 %shard_map.66 = (f32[2,128,384]{2,1,0:T(8,128)S(1)}, bf16[2,128,384]{2,1,0:T(8,128)(2,1)S(1)}) custom-call(bf16[2,128,384]{2,1,0:T(8,128)(2,1)S(1)} %get-tuple-element.23.refs_0_, bf16[2,128,384]{2,1,0:T(8,128)(2,1)S(1)} %collective-permute-done.1.refs_1_, bf16[2,128,384]{2,1,0:T(8,128)(2,1)S(1)} %collective-permute-done.2.refs_2_, ...), custom_call_target="tpu_custom_call" | custom-call | flops 1000000000 | bytes 2162688 | tf_op jit(solution)/shard_map/pallas_call | solution.py:206
  44.8 0.7 collective-permute-start.7
  45.5 1.3 %collective-permute-start.8 = (bf16[2,128,384]{2,1,0:T(8,128)(2,1)S(1)}, bf16[2,128,384]{2,1,0:T(8,128)(2,1)S(1)}, u32[]{:S(2)}, u32[]{:S(2)}) collective-permute-start(bf16[2,128,384]{2,1,0:T(8,128)(2,1)S(1)} %get-tuple-element.31), channel_id=1, source_target_pairs={{0,128},{8,136},{16,144},{24,152},{32,160},{40,168},{48,176},{56,1... | collective-permute-start | bytes 589832 | tf_op jit(solution)/shard_map/ppermute | solution.py:296
  46.8 3.7 %collective-permute-start.9 = (bf16[2,128,384]{2,1,0:T(8,128)(2,1)S(1)}, bf16[2,128,384]{2,1,0:T(8,128)(2,1)S(1)}, u32[]{:S(2)}, u32[]{:S(2)}) collective-permute-start(bf16[2,128,384]{2,1,0:T(8,128)(2,1)S(1)} %get-tuple-element.31), channel_id=1, source_target_pairs={{0,64},{8,72},{16,80},{24,88},{32,96},{40,104},{48,112},{56,120},{... | collective-permute-start | bytes 589832 | tf_op jit(solution)/shard_map/ppermute | solution.py:296
  50.5 5.1 %collective-permute-done.8.mid_ref = bf16[2,128,384]{2,1,0:T(8,128)(2,1)S(1)} collective-permute-done((bf16[2,128,384]{2,1,0:T(8,128)(2,1)S(1)}, bf16[2,128,384]{2,1,0:T(8,128)(2,1)S(1)}, u32[]{:S(2)}, u32[]{:S(2)}) %collective-permute-start.8) | collective-permute-done | bytes 196640 | tf_op jit(solution)/shard_map/ppermute | solution.py:296
  55.6 2.0 %collective-permute-done.9.near_ref = bf16[2,128,384]{2,1,0:T(8,128)(2,1)S(1)} collective-permute-done((bf16[2,128,384]{2,1,0:T(8,128)(2,1)S(1)}, bf16[2,128,384]{2,1,0:T(8,128)(2,1)S(1)}, u32[]{:S(2)}, u32[]{:S(2)}) %collective-permute-start.9) | collective-permute-done | bytes 196640 | tf_op jit(solution)/shard_map/ppermute | solution.py:296
  57.6 1.1 %shard_map.67 = (bf16[256,512]{1,0:T(8,128)(2,1)S(1)}, bf16[256,512]{1,0:T(8,128)(2,1)S(1)}) custom-call(bf16[2,128,384]{2,1,0:T(8,128)(2,1)S(1)} %collective-permute-done.7.far_ref, bf16[2,128,384]{2,1,0:T(8,128)(2,1)S(1)} %collective-permute-done.8.mid_ref, bf16[2,128,384]{2,1,0:T(8,128)(2,1)S(1)} %collective-permute-done.9.near_ref, ...), custom_call_target="tpu_custom_call" | custom-call | flops 500000000 | bytes 2818048 | tf_op jit(solution)/shard_map/pallas_call | solution.py:206
  58.8 1.5 %collective-permute-done.10.joined_ref = bf16[256,512]{1,0:T(8,128)(2,1)S(1)} collective-permute-done((bf16[256,512]{1,0:T(8,128)(2,1)S(1)}, bf16[256,512]{1,0:T(8,128)(2,1)S(1)}, u32[]{:S(2)}, u32[]{:S(2)}) %collective-permute-start.10) | collective-permute-done | bytes 262176 | tf_op jit(solution)/shard_map/ppermute | solution.py:306
  60.4 2.2 %shard_map.68 = (bf16[128,2048]{1,0:T(8,128)(2,1)S(1)}, bf16[128,2048]{1,0:T(8,128)(2,1)S(1)}) custom-call(bf16[256,512]{1,0:T(8,128)(2,1)S(1)} %get-tuple-element.35.keep_ref, bf16[256,512]{1,0:T(8,128)(2,1)S(1)} %collective-permute-done.10.joined_ref, bf16[512,4096]{1,0:T(8,128)(2,1)S(1)} %copy-done, bf16[512,4096]{1,0:T(8,128)(2,1)S(1)} %collective-permute-done.11.other_w_ref), custom_call_target="tpu_custom_call" | custom-call | flops 1000000000 | bytes 6000000 | tf_op jit(solution)/shard_map/pallas_call | solution.py:235
  62.6 1.7 %collective-permute-start.12 = (bf16[128,2048]{1,0:T(8,128)(2,1)S(1)}, bf16[128,2048]{1,0:T(8,128)(2,1)S(1)}, u32[]{:S(2)}, u32[]{:S(2)}) collective-permute-start(bf16[128,2048]{1,0:T(8,128)(2,1)S(1)} %get-tuple-element.38), channel_id=1, source_target_pairs={{0,2},{1,3},{2,0},{3,1},{4,6},{5,7},{6,4},{7,5},{8,10},{9,11},{10,... | collective-permute-start | bytes 1572872 | tf_op jit(solution)/shard_map/ppermute | solution.py:311
  64.3 2.2 %shard_map.69 = (bf16[128,2048]{1,0:T(8,128)(2,1)S(1)}, bf16[128,2048]{1,0:T(8,128)(2,1)S(1)}) custom-call(bf16[256,512]{1,0:T(8,128)(2,1)S(1)} %get-tuple-element.35.keep_ref, bf16[256,512]{1,0:T(8,128)(2,1)S(1)} %collective-permute-done.10.joined_ref, bf16[512,4096]{1,0:T(8,128)(2,1)S(1)} %copy-done, bf16[512,4096]{1,0:T(8,128)(2,1)S(1)} %collective-permute-done.11.other_w_ref), custom_call_target="tpu_custom_call" | custom-call | flops 1000000000 | bytes 6000000 | tf_op jit(solution)/shard_map/pallas_call | solution.py:235
  66.5 2.3 %collective-permute-start.14 = (bf16[128,2048]{1,0:T(8,128)(2,1)S(1)}, bf16[128,2048]{1,0:T(8,128)(2,1)S(1)}, u32[]{:S(2)}, u32[]{:S(2)}) collective-permute-start(bf16[128,2048]{1,0:T(8,128)(2,1)S(1)} %get-tuple-element.40), channel_id=1, source_target_pairs={{0,6},{1,7},{2,4},{3,5},{4,2},{5,3},{6,0},{7,1},{8,14},{9,15},{10,... | collective-permute-start | bytes 1572872 | tf_op jit(solution)/shard_map/ppermute | solution.py:313
  68.7 7.9 %collective-permute-done.12 = bf16[128,2048]{1,0:T(8,128)(2,1)S(1)} collective-permute-done((bf16[128,2048]{1,0:T(8,128)(2,1)S(1)}, bf16[128,2048]{1,0:T(8,128)(2,1)S(1)}, u32[]{:S(2)}, u32[]{:S(2)}) %collective-permute-start.12) | collective-permute-done | bytes 524320 | tf_op jit(solution)/shard_map/ppermute | solution.py:311
  76.7 3.1 %collective-permute-start.13 = (bf16[64,2048]{1,0:T(8,128)(2,1)S(1)}, bf16[64,2048]{1,0:T(8,128)(2,1)S(1)}, u32[]{:S(2)}, u32[]{:S(2)}) collective-permute-start(bf16[64,2048]{1,0:T(8,128)(2,1)S(1)} %add_convert_fusion.3), channel_id=1, source_target_pairs={{0,6},{1,7},{2,4},{3,5},{4,2},{5,3},{6,0},{7,1},{8,14},{9,15},{10,... | collective-permute-start | bytes 786440 | tf_op jit(solution)/shard_map/ppermute | solution.py:318
  79.8 2.7 %collective-permute-done.14 = bf16[128,2048]{1,0:T(8,128)(2,1)S(1)} collective-permute-done((bf16[128,2048]{1,0:T(8,128)(2,1)S(1)}, bf16[128,2048]{1,0:T(8,128)(2,1)S(1)}, u32[]{:S(2)}, u32[]{:S(2)}) %collective-permute-start.14) | collective-permute-done | bytes 524320 | tf_op jit(solution)/shard_map/ppermute | solution.py:313
  82.7 4.3 %collective-permute-done.13 = bf16[64,2048]{1,0:T(8,128)(2,1)S(1)} collective-permute-done((bf16[64,2048]{1,0:T(8,128)(2,1)S(1)}, bf16[64,2048]{1,0:T(8,128)(2,1)S(1)}, u32[]{:S(2)}, u32[]{:S(2)}) %collective-permute-start.13) | collective-permute-done | bytes 262176 | tf_op jit(solution)/shard_map/ppermute | solution.py:318
  87.2 1.9 %collective-permute-done.15 = bf16[64,2048]{1,0:T(8,128)(2,1)S(1)} collective-permute-done((bf16[64,2048]{1,0:T(8,128)(2,1)S(1)}, bf16[64,2048]{1,0:T(8,128)(2,1)S(1)}, u32[]{:S(2)}, u32[]{:S(2)}) %collective-permute-start.15) | collective-permute-done | bytes 262176 | tf_op jit(solution)/shard_map/ppermute | solution.py:319
  89.2 0.8 pad_maximum_fusion
  (19 shorter events, 0.5 us)
Async XLA Ops:
  0.0 60.4 %collective-permute-start.11 = (bf16[512,4096]{1,0:T(8,128)(2,1)}, bf16[512,4096]{1,0:T(8,128)(2,1)S(1)}, u32[]{:S(2)}, u32[]{:S(2)}) collective-permute-start(bf16[512,4096]{1,0:T(8,128)(2,1)} %own_w_ref.3), channel_id=1, source_target_pairs={{0,1},{1,0},{2,3},{3,2},{4,5},{5,4},{6,7},{7,6},{8,9},{9,8},{10,11... | collective-permute-start | bytes 12582920 | tf_op jit(solution)/shard_map/ppermute | solution.py:254
  2.2 0.7 copy-start.1
  2.9 0.7 copy-start.2
  9.5 11.5 %collective-permute-start = (bf16[2,128,384]{2,1,0:T(8,128)(2,1)S(1)}, bf16[2,128,384]{2,1,0:T(8,128)(2,1)S(1)}, u32[]{:S(2)}, u32[]{:S(2)}) collective-permute-start(bf16[2,128,384]{2,1,0:T(8,128)(2,1)S(1)} %get-tuple-element.23.refs_0_), channel_id=1, source_target_pairs={{0,8},{8,16},{16,24},{24,32},{32,40},{40,48},{48,56},{56,0},{64,72... | collective-permute-start | bytes 589832 | tf_op jit(solution)/shard_map/ppermute | solution.py:280
  11.5 9.5 %collective-permute-start.1 = (bf16[2,128,384]{2,1,0:T(8,128)(2,1)S(1)}, bf16[2,128,384]{2,1,0:T(8,128)(2,1)S(1)}, u32[]{:S(2)}, u32[]{:S(2)}) collective-permute-start(bf16[2,128,384]{2,1,0:T(8,128)(2,1)S(1)} %get-tuple-element.23.refs_0_), channel_id=1, source_target_pairs={{0,56},{8,0},{16,8},{24,16},{32,24},{40,32},{48,40},{56,48},{64,12... | collective-permute-start | bytes 589832 | tf_op jit(solution)/shard_map/ppermute | solution.py:283
  18.7 41.6 %copy-start = (bf16[512,4096]{1,0:T(8,128)(2,1)S(1)}, bf16[512,4096]{1,0:T(8,128)(2,1)}, u32[]{:S(2)}) copy-start(bf16[512,4096]{1,0:T(8,128)(2,1)} %own_w_ref.3) | copy-start | bytes 12582916
  21.0 8.0 %collective-permute-start.4 = (bf16[2,128,384]{2,1,0:T(8,128)(2,1)S(1)}, bf16[2,128,384]{2,1,0:T(8,128)(2,1)S(1)}, u32[]{:S(2)}, u32[]{:S(2)}) collective-permute-start(bf16[2,128,384]{2,1,0:T(8,128)(2,1)S(1)} %collective-permute-done.refs_7_), channel_id=1, source_target_pairs={{0,8},{8,16},{16,24},{24,32},{32,40},{40,48},{48,56},{56,0},{64,72... | collective-permute-start | bytes 589832 | tf_op jit(solution)/shard_map/ppermute | solution.py:280
  21.0 8.0 %collective-permute-start.2 = (bf16[2,128,384]{2,1,0:T(8,128)(2,1)S(1)}, bf16[2,128,384]{2,1,0:T(8,128)(2,1)S(1)}, u32[]{:S(2)}, u32[]{:S(2)}) collective-permute-start(bf16[2,128,384]{2,1,0:T(8,128)(2,1)S(1)} %collective-permute-done.1.refs_1_), channel_id=1, source_target_pairs={{0,56},{8,0},{16,8},{24,16},{32,24},{40,32},{48,40},{56,48},{64,12... | collective-permute-start | bytes 589832 | tf_op jit(solution)/shard_map/ppermute | solution.py:283
  28.9 7.1 %collective-permute-start.5 = (bf16[2,128,384]{2,1,0:T(8,128)(2,1)S(1)}, bf16[2,128,384]{2,1,0:T(8,128)(2,1)S(1)}, u32[]{:S(2)}, u32[]{:S(2)}) collective-permute-start(bf16[2,128,384]{2,1,0:T(8,128)(2,1)S(1)} %collective-permute-done.4.refs_6_), channel_id=1, source_target_pairs={{0,8},{8,16},{16,24},{24,32},{32,40},{40,48},{48,56},{56,0},{64,72... | collective-permute-start | bytes 589832 | tf_op jit(solution)/shard_map/ppermute | solution.py:280
  29.0 7.1 %collective-permute-start.3 = (bf16[2,128,384]{2,1,0:T(8,128)(2,1)S(1)}, bf16[2,128,384]{2,1,0:T(8,128)(2,1)S(1)}, u32[]{:S(2)}, u32[]{:S(2)}) collective-permute-start(bf16[2,128,384]{2,1,0:T(8,128)(2,1)S(1)} %collective-permute-done.2.refs_2_), channel_id=1, source_target_pairs={{0,56},{8,0},{16,8},{24,16},{32,24},{40,32},{48,40},{56,48},{64,12... | collective-permute-start | bytes 589832 | tf_op jit(solution)/shard_map/ppermute | solution.py:283
  36.0 6.9 %collective-permute-start.6 = (bf16[2,128,384]{2,1,0:T(8,128)(2,1)S(1)}, bf16[2,128,384]{2,1,0:T(8,128)(2,1)S(1)}, u32[]{:S(2)}, u32[]{:S(2)}) collective-permute-start(bf16[2,128,384]{2,1,0:T(8,128)(2,1)S(1)} %collective-permute-done.5.refs_5_), channel_id=1, source_target_pairs={{0,8},{8,16},{16,24},{24,32},{32,40},{40,48},{48,56},{56,0},{64,72... | collective-permute-start | bytes 589832 | tf_op jit(solution)/shard_map/ppermute | solution.py:280
  44.8 5.7 %collective-permute-start.7 = (bf16[2,128,384]{2,1,0:T(8,128)(2,1)S(1)}, bf16[2,128,384]{2,1,0:T(8,128)(2,1)S(1)}, u32[]{:S(2)}, u32[]{:S(2)}) collective-permute-start(bf16[2,128,384]{2,1,0:T(8,128)(2,1)S(1)} %get-tuple-element.31), channel_id=1, source_target_pairs={{0,192},{8,200},{16,208},{24,216},{32,224},{40,232},{48,240},{56,2... | collective-permute-start | bytes 589832 | tf_op jit(solution)/shard_map/ppermute | solution.py:296
  45.5 10.1 %collective-permute-start.8 = (bf16[2,128,384]{2,1,0:T(8,128)(2,1)S(1)}, bf16[2,128,384]{2,1,0:T(8,128)(2,1)S(1)}, u32[]{:S(2)}, u32[]{:S(2)}) collective-permute-start(bf16[2,128,384]{2,1,0:T(8,128)(2,1)S(1)} %get-tuple-element.31), channel_id=1, source_target_pairs={{0,128},{8,136},{16,144},{24,152},{32,160},{40,168},{48,176},{56,1... | collective-permute-start | bytes 589832 | tf_op jit(solution)/shard_map/ppermute | solution.py:296
  46.8 10.8 %collective-permute-start.9 = (bf16[2,128,384]{2,1,0:T(8,128)(2,1)S(1)}, bf16[2,128,384]{2,1,0:T(8,128)(2,1)S(1)}, u32[]{:S(2)}, u32[]{:S(2)}) collective-permute-start(bf16[2,128,384]{2,1,0:T(8,128)(2,1)S(1)} %get-tuple-element.31), channel_id=1, source_target_pairs={{0,64},{8,72},{16,80},{24,88},{32,96},{40,104},{48,112},{56,120},{... | collective-permute-start | bytes 589832 | tf_op jit(solution)/shard_map/ppermute | solution.py:296
  58.7 1.6 %collective-permute-start.10 = (bf16[256,512]{1,0:T(8,128)(2,1)S(1)}, bf16[256,512]{1,0:T(8,128)(2,1)S(1)}, u32[]{:S(2)}, u32[]{:S(2)}) collective-permute-start(bf16[256,512]{1,0:T(8,128)(2,1)S(1)} %get-tuple-element.36), channel_id=1, source_target_pairs={{0,1},{1,0},{2,3},{3,2},{4,5},{5,4},{6,7},{7,6},{8,9},{9,8},{10,11... | collective-permute-start | bytes 786440 | tf_op jit(solution)/shard_map/ppermute | solution.py:306
  62.6 14.1 %collective-permute-start.12 = (bf16[128,2048]{1,0:T(8,128)(2,1)S(1)}, bf16[128,2048]{1,0:T(8,128)(2,1)S(1)}, u32[]{:S(2)}, u32[]{:S(2)}) collective-permute-start(bf16[128,2048]{1,0:T(8,128)(2,1)S(1)} %get-tuple-element.38), channel_id=1, source_target_pairs={{0,2},{1,3},{2,0},{3,1},{4,6},{5,7},{6,4},{7,5},{8,10},{9,11},{10,... | collective-permute-start | bytes 1572872 | tf_op jit(solution)/shard_map/ppermute | solution.py:311
  66.5 16.1 %collective-permute-start.14 = (bf16[128,2048]{1,0:T(8,128)(2,1)S(1)}, bf16[128,2048]{1,0:T(8,128)(2,1)S(1)}, u32[]{:S(2)}, u32[]{:S(2)}) collective-permute-start(bf16[128,2048]{1,0:T(8,128)(2,1)S(1)} %get-tuple-element.40), channel_id=1, source_target_pairs={{0,6},{1,7},{2,4},{3,5},{4,2},{5,3},{6,0},{7,1},{8,14},{9,15},{10,... | collective-permute-start | bytes 1572872 | tf_op jit(solution)/shard_map/ppermute | solution.py:313
  76.7 10.3 %collective-permute-start.13 = (bf16[64,2048]{1,0:T(8,128)(2,1)S(1)}, bf16[64,2048]{1,0:T(8,128)(2,1)S(1)}, u32[]{:S(2)}, u32[]{:S(2)}) collective-permute-start(bf16[64,2048]{1,0:T(8,128)(2,1)S(1)} %add_convert_fusion.3), channel_id=1, source_target_pairs={{0,6},{1,7},{2,4},{3,5},{4,2},{5,3},{6,0},{7,1},{8,14},{9,15},{10,... | collective-permute-start | bytes 786440 | tf_op jit(solution)/shard_map/ppermute | solution.py:318
  82.6 6.5 %collective-permute-start.15 = (bf16[64,2048]{1,0:T(8,128)(2,1)S(1)}, bf16[64,2048]{1,0:T(8,128)(2,1)S(1)}, u32[]{:S(2)}, u32[]{:S(2)}) collective-permute-start(bf16[64,2048]{1,0:T(8,128)(2,1)S(1)} %add_convert_fusion.1), channel_id=1, source_target_pairs={{0,2},{1,3},{2,0},{3,1},{4,6},{5,7},{6,4},{7,5},{8,10},{9,11},{10,... | collective-permute-start | bytes 786440 | tf_op jit(solution)/shard_map/ppermute | solution.py:319

commit v3 on v2

--- a/solution.py
+++ b/solution.py
@@ -10,6 +10,7 @@
 BLOCK = 128
 INTERPRET = False
 VMEM_LIMIT = 12 << 20
+CHUNK = 1024
 F32 = jnp.float32
 BF16 = jnp.bfloat16
 
@@ -52,7 +53,13 @@
     return lax.broadcasted_iota(jnp.int32, (n, n), 0), lax.broadcasted_iota(jnp.int32, (n, n), 1)
 
 
-def terms_kernel(resets, k_ref, v_ref, beta_ref, wu_ref, prefix_ref, scale_ref, carry_ref):
+def terms_kernel(
+    resets_hbm, beta_hbm, k_ref, v_ref, wu_ref, prefix_ref, scale_ref, carry_ref, resets, beta_ref, sems
+):
+    resets_copy = pltpu.make_async_copy(resets_hbm, resets, sems.at[0])
+    beta_copy = pltpu.make_async_copy(beta_hbm, beta_ref, sems.at[1])
+    beta_copy.start()
+    resets_copy.start()
     row, col = square_ids(BLOCK)
     eye = row == col
     identity = jnp.where(eye, 1.0, 0.0).astype(F32)
@@ -62,6 +69,7 @@
         ks[b, h] = k_ref[b * BLOCK : (b + 1) * BLOCK, h * 128 : (h + 1) * 128]
         vs[b, h] = v_ref[b * BLOCK : (b + 1) * BLOCK, h * 256 : (h + 1) * 256]
         grams[b, h] = dot_nt(ks[b, h], ks[b, h])
+    beta_copy.wait()
     lower, inv, r_cols, beta_rows, c_rows = {}, {}, {}, {}, {}
     for b, h in cells:
         gram = grams[b, h]
@@ -99,8 +107,9 @@
         )
     zeros = jnp.zeros((BLOCK, 256), F32)
     state = {h: jnp.concatenate([identity, zeros], 1) for h in range(2)}
+    resets_copy.wait()
     for b in range(4):
-        starts = (resets[0] == b) | (resets[1] == b)
+        starts = (resets[0, 0] == b) | (resets[0, 1] == b)
         kept = jnp.where(starts, 0.0, 1.0).astype(F32)
         for h in range(2):
             before = state[h] * kept
@@ -148,7 +157,9 @@
 
 
 def group_kernel(*refs):
-    elements, (before_ref, total_ref) = refs[:8], refs[8:]
+    refs, (before_ref, total_ref) = refs[:9], refs[9:]
+    elements = [(ref.at[0], ref.at[1]) for ref in refs[:4] + refs[6:]]
+    elements.insert(4, refs[4:6])
     row, col = square_ids(BLOCK)
     identity = jnp.where(row == col, 1.0, 0.0).astype(F32)
     empty = jnp.concatenate([identity, jnp.zeros((BLOCK, 256), F32)], 1)
@@ -161,12 +172,12 @@
             if step > 1:
                 after[h] = jnp.where(wraps, state[h], after[h])
                 state[h] = jnp.where(wraps, empty, state[h])
-            state[h] = follow(state[h], elements[step][h])
+            state[h] = follow(state[h], elements[step][h][...])
     for h in range(2):
         after[h] = jnp.where(z == 0, state[h], after[h])
         state[h] = jnp.where(z == 0, empty, state[h])
         before_ref[h] = jnp.concatenate([state[h][:, :128] - identity, state[h][:, 128:]], 1)
-        through = follow(state[h], elements[0][h])
+        through = follow(state[h], elements[0][h][...])
         total = dot3(after[h][:, :128], through)
         total_ref[h] = jnp.concatenate(
             [total[:, :128] - identity, total[:, 128:] + after[h][:, 128:]], 1
@@ -197,59 +208,70 @@
         send_ref[pl.ds(slot, 64), :] = jnp.where(core == 0, second, first)
 
 
-SMEM = pl.BlockSpec(memory_space=pltpu.SMEM)
+HBM = pl.BlockSpec(memory_space=pltpu.HBM)
 VMEM = pl.BlockSpec(memory_space=pltpu.VMEM)
 
 
-def call(kernel, outs, scalars, arrays, flops):
-    moved = sum(a.size * a.dtype.itemsize for a in list(arrays) + list(outs))
+def call(kernel, outs, arrays, flops, in_hbm=(), scratch=()):
+    moved = sum(a.size * a.dtype.itemsize for a in (*in_hbm, *arrays, *outs))
     return pl.pallas_call(
         kernel,
-        out_shape=outs,
-        in_specs=[SMEM] + [VMEM] * len(arrays) if scalars is not None else [VMEM] * len(arrays),
+        out_shape=[jax.ShapeDtypeStruct(a.shape, a.dtype) for a in outs],
+        in_specs=[HBM] * len(in_hbm) + [VMEM] * len(arrays),
         out_specs=[VMEM] * len(outs),
+        scratch_shapes=scratch,
         compiler_params=pltpu.CompilerParams(vmem_limit_bytes=VMEM_LIMIT),
         cost_estimate=pl.CostEstimate(flops=flops, bytes_accessed=moved, transcendentals=0),
         interpret=INTERPRET,
-    )(*([scalars] if scalars is not None else []), *arrays)
-
-
-def product_kernel(crossed, keep_ref, joined_ref, own_w_ref, other_w_ref, send_ref, own_ref):
-    out = dot(keep_ref[...], own_w_ref[...]) + dot(joined_ref[...], other_w_ref[...])
-    out = out.astype(BF16)
-    if crossed:
-        send_ref[...] = out[64:192]
-        own_ref[:64] = out[:64]
-        own_ref[64:] = out[192:]
-    else:
-        send_ref[...] = out[128:]
-        own_ref[...] = out[:128]
-
-
-def product(crossed, keep, joined, own_weight, other_weight):
-    tile = 512
-    first = 2048 // tile if crossed else 0
-    rows = pl.BlockSpec((256, 512), lambda i: (0, 0))
-    columns = pl.BlockSpec((512, tile), lambda i: (0, i + first))
-    out = pl.BlockSpec((128, tile), lambda i: (0, i))
-    return pl.pallas_call(
-        functools.partial(product_kernel, crossed),
-        grid=(2048 // tile,),
-        out_shape=[jax.ShapeDtypeStruct((128, 2048), BF16)] * 2,
-        in_specs=[rows, rows, columns, columns],
-        out_specs=[out, out],
-        compiler_params=pltpu.CompilerParams(vmem_limit_bytes=VMEM_LIMIT),
-        cost_estimate=pl.CostEstimate(
-            flops=1_000_000_000, bytes_accessed=6_000_000, transcendentals=0
-        ),
-        interpret=INTERPRET,
-    )(keep, joined, own_weight, other_weight)
+    )(*[pltpu.with_memory_space_constraint(a, pltpu.HBM) for a in in_hbm], *arrays)
+
+
+def rows_product(own_rows, other_rows, own_w_ref, other_w_ref, first):
+    columns = slice(first, first + CHUNK)
+    out = dot(own_rows, own_w_ref[:, columns]) + dot(other_rows, other_w_ref[:, columns])
+    return out.astype(BF16)
+
+
+def send_kernel(part, keep_ref, joined_ref, own_w_ref, other_w_ref, near_ref, far_ref):
+    weights = own_w_ref, other_w_ref, part * CHUNK
+    near_ref[...] = rows_product(keep_ref[128:], joined_ref[128:], *weights)
+    weights = own_w_ref, other_w_ref, 2048 + part * CHUNK
+    far_ref[...] = rows_product(keep_ref[64:192], joined_ref[64:192], *weights)
+
+
+def own_kernel(keep_ref, joined_ref, own_w_ref, other_w_ref, final_ref, passed_ref):
+    for part in range(4):
+        columns = slice(part * CHUNK, (part + 1) * CHUNK)
+        weights = own_w_ref, other_w_ref, part * CHUNK
+        if part < 2:
+            out = rows_product(keep_ref[:128], joined_ref[:128], *weights)
+        else:
+            own_rows = jnp.concatenate([keep_ref[:64], keep_ref[192:]], 0)
+            other_rows = jnp.concatenate([joined_ref[:64], joined_ref[192:]], 0)
+            out = rows_product(own_rows, other_rows, *weights)
+        final_ref[:, columns] = out[:64]
+        passed_ref[:, columns] = out[64:]
+
+
+def pair_kernel(part, passed_ref, sent_ref, out_ref):
+    half = slice(0, 64) if part < 2 else slice(64, 128)
+    own = passed_ref[:, part * CHUNK : (part + 1) * CHUNK].astype(F32)
+    out_ref[...] = (own + sent_ref[half].astype(F32)).astype(BF16)
+
+
+def sum_kernel(*refs):
+    final_ref, out_ref = refs[0], refs[9]
+    for part in range(4):
+        columns = slice(part * CHUNK, (part + 1) * CHUNK)
+        half = slice(64, 128) if part < 2 else slice(0, 64)
+        total = final_ref[:, columns].astype(F32) + refs[1 + part][half].astype(F32)
+        out_ref[:, columns] = (total + refs[5 + part][...].astype(F32)).astype(BF16)
 
 
 def body(queries, keys, values, beta, reset_blocks, out_weight):
-    q = queries.reshape(512, 256)
     k = keys.reshape(512, 256)
     v = values.reshape(512, 512)
+
     across = [(i, i ^ 1) for i in range(8)]
     other_weight = lax.ppermute(out_weight, "head", across)
 
@@ -262,34 +284,40 @@
             shaped((8, 128), F32),
             shaped((2, 128, 384), BF16),
         ],
-        reset_blocks.reshape(2),
-        [k, v, beta],
+        [k, v],
         3_000_000_000,
-    )
+        in_hbm=[reset_blocks, beta],
+        scratch=[
+            pltpu.SMEM((1, 2), jnp.int32),
+            pltpu.VMEM((2, 512), F32),
+            pltpu.SemaphoreType.DMA((2,)),
+        ],
+    )
+    queries, carry = lax.optimization_barrier((queries, carry))
     response, own_out = call(
         response_kernel,
         [shaped((8, 128, 128), BF16), shaped((8, 128, 256), F32)],
-        None,
-        [q, k, scale, wu, prefix],
+        [queries.reshape(512, 256), k, scale, wu, prefix],
         2_000_000_000,
     )
     up = [(i, i - i % 8 + (i + 1) % 8) for i in range(32)]
     down = [(i, i - i % 8 + (i + 7) % 8) for i in range(32)]
     below, above = [carry], [carry]
-    for step in range(4):
-        lower = lax.ppermute(below[-1], "seq", up)
-        below.append(lower)
-        if step < 3:
-            above.append(lax.ppermute(above[-1], "seq", down))
+    for step in range(3):
+        below.append(lax.ppermute(below[-1], "seq", up))
+        above.append(lax.ppermute(above[-1], "seq", down))
         if step == 0:
             below[1], above[1], response, own_out = lax.optimization_barrier(
                 (below[1], above[1], response, own_out)
             )
+    opposite = [
+        lax.ppermute(below[3][0], "seq", up),
+        lax.ppermute(above[3][1], "seq", down),
+    ]
     before, total = call(
         group_kernel,
         [shaped((2, 128, 384), F32), shaped((2, 128, 384), BF16)],
-        None,
-        above + below[:0:-1],
+        above + opposite + below[:0:-1],
         1_000_000_000,
     )
     received = [
@@ -299,27 +327,36 @@
     keep, send = call(
         output_kernel,
         [shaped((256, 512), BF16), shaped((256, 512), BF16)],
-        None,
         received + [before, response, own_out],
         500_000_000,
     )
     joined = lax.ppermute(send, "head", across)
-
+    operands = [keep, joined, out_weight, other_weight]
     near = [(i, i ^ 2) for i in range(8)]
     far = [(i, i ^ 6) for i in range(8)]
-    send_a, own_a = product(False, keep, joined, out_weight, other_weight)
-    sent_a = lax.ppermute(send_a, "head", near)
-    send_b, own_b = product(True, keep, joined, out_weight, other_weight)
-    sent_b = lax.ppermute(send_b, "head", far)
-
-    def add(x, y):
-        return x.astype(F32) + y.astype(F32)
-
-    next_a = lax.ppermute(add(own_a[64:], sent_a[:64]).astype(BF16), "head", far)
-    next_b = lax.ppermute(add(own_b[64:], sent_b[64:]).astype(BF16), "head", near)
-    out_a = (add(own_a[:64], sent_a[64:]) + next_a.astype(F32)).astype(BF16)
-    out_b = (add(own_b[:64], sent_b[:64]) + next_b.astype(F32)).astype(BF16)
-    return jnp.concatenate([out_a, out_b], 1)
+    half = [shaped((128, CHUNK), BF16)] * 2
+    routes = [near, near, far, far]
+    sent = [None] * 4
+    for part in range(2):
+        to_near, to_far = call(
+            functools.partial(send_kernel, part), half, operands, 500_000_000
+        )
+        operands[0], to_near, to_far = lax.optimization_barrier((operands[0], to_near, to_far))
+        sent[part] = lax.ppermute(to_near, "head", near)
+        sent[part + 2] = lax.ppermute(to_far, "head", far)
+    final, passed = call(
+        own_kernel, [shaped((64, 4096), BF16)] * 2, operands, 1_000_000_000
+    )
+    received = [None] * 4
+    for part in (0, 2, 1, 3):
+        (summed,) = call(
+            functools.partial(pair_kernel, part),
+            [shaped((64, CHUNK), BF16)],
+            [passed, sent[part]],
+            100_000,
+        )
+        received[part] = lax.ppermute(summed, "head", routes[3 - part])
+    return call(sum_kernel, [shaped((64, 4096), BF16)], [final, *sent, *received], 1_000_000)[0]
 
 
 def solution(mesh):

time: 90.3 us -> 86.6 us (0.959); the launches traced: 90 us -> 85.1 us
  waiting for transfers between devices: 43.2 us -> 36.2 us
  starting transfers between devices: 25.4 us -> 30.3 us
  local copies, waits for them, and re-layouts: 3.57 us -> 2.18 us
  other arithmetic: 1.15 us -> 0 us
    ppermute x8 -> x13, waiting for transfers between devices: 34.6 us -> 18.2 us  [the longest x4 4.83 us: body(): received[part] = lax.ppermute(summed, 'head', routes[3 - part])]
    ppermute x3, waiting for transfers between devices: 0.01 us -> 9.38 us  [body(): above.append(lax.ppermute(above[-1], 'seq', down))]
    ppermute x8 -> x13, starting transfers between devices: 9.14 us -> 17.2 us  [the longest x4 6.8 us: body(): received[part] = lax.ppermute(summed, 'head', routes[3 - part])]
    ppermute x3, starting transfers between devices: 10.5 us -> 8.03 us  [body(): above.append(lax.ppermute(above[-1], 'seq', down))]
    reshape x1 -> x0, local copies, waits for them, and re-layouts: 1.1 us -> none  [body(): q = queries.reshape(512, 256)]
    pallas_call x6 -> x12, Pallas kernels: 16.5 us -> 16.3 us  [call(): pl.pallas_call(kernel, out_shape=[jax.ShapeDtypeStruct(a.shape, a.dtype)...]
  transfers between devices with their start and end apart: 16 -> 21, of which waited for: 11 -> 14; matrix products, arithmetic and copies ran while one was open for 3% -> 3% of each run, Pallas kernels for 16% -> 17%
where the time goes in v3:
time: 86.6 us; the launch traced here: 85.1 us
  waiting for transfers between devices  36.2 us (42%)
  starting transfers between devices  30.3 us (35%)
  Pallas kernels  16.3 us (19%)
  local copies, waits for them, and re-layouts  2.18 us (3%)
    pallas_call x12, Pallas kernels, call(): pl.pallas_call(kernel, out_shape=[jax.ShapeDtypeStruct(a.shape, a.dtype)...  16.3 us
    ppermute x3, waiting for transfers between devices, body(): above.append(lax.ppermute(above[-1], 'seq', down))  9.38 us
    ppermute x3, starting transfers between devices, body(): above.append(lax.ppermute(above[-1], 'seq', down))  8.03 us
    ppermute x3, waiting for transfers between devices, body(): lax.ppermute(total, 'seq', [(i, i + 8 * d) for i in range(32) if i + 8 *...  7.09 us
    ppermute x4, starting transfers between devices, body(): received[part] = lax.ppermute(summed, 'head', routes[3 - part])  6.8 us
    ppermute x3, starting transfers between devices, body(): lax.ppermute(total, 'seq', [(i, i + 8 * d) for i in range(32) if i + 8 *...  5.05 us
    ppermute x4, waiting for transfers between devices, body(): received[part] = lax.ppermute(summed, 'head', routes[3 - part])  4.83 us
    ppermute x2, waiting for transfers between devices, body(): sent[part] = lax.ppermute(to_near, 'head', near)  4.1 us
  transfers between devices with their start and end apart: 21, of which 14 were waited for; matrix products, arithmetic and copies ran while one was open for 3% of the time, Pallas kernels for 17%

profile of v3, /device:TPU:4, one launch (start us, length us, event | category | flops | bytes accessed | tf_op | source)
XLA Modules:
  0.0 85.1 jit_solution(116645364666023589)
XLA Ops:
  0.0 1.0 %copy.13 = bf16[64,8,2,128]{3,1,2,0:T(8,128)(2,1)S(1)} copy(bf16[64,8,2,128]{3,2,1,0:T(2,128)(2,1)} %bitcast.19) | data formatting | bytes 524288
  1.0 1.1 %copy.8 = bf16[64,8,2,256]{3,1,2,0:T(8,128)(2,1)S(1)} copy(bf16[64,8,2,256]{3,2,1,0:T(2,128)(2,1)} %bitcast.18) | data formatting | bytes 1048576
  2.1 6.3 %shard_map.64 = (f32[8,128,384]{2,1,0:T(8,128)S(1)}, f32[8,128,384]{2,1,0:T(8,128)S(1)}, f32[8,128]{1,0:T(8,128)S(1)}, bf16[2,128,384]{2,1,0:T(8,128)(2,1)S(1)}) custom-call(s32[1,2]{1,0:T(1,128)} %resets_hbm.1, f32[2,512]{1,0:T(2,128)} %beta_hbm.1, bf16[512,256]{1,0:T(8,128)(2,1)S(1)} %bitcast.15, bf16[512,512]{1,0:T(8,128)(2,1)S(1)} %bitcast.14), custom_call_target="tpu_custom_call" | custom-call | flops 3000000000 | bytes 4136968 | tf_op jit(solution)/shard_map/pallas_call | solution.py:217
  8.4 5.9 %collective-permute-start.1 = (bf16[2,128,384]{2,1,0:T(8,128)(2,1)S(1)}, bf16[2,128,384]{2,1,0:T(8,128)(2,1)S(1)}, u32[]{:S(2)}, u32[]{:S(2)}) collective-permute-start(bf16[2,128,384]{2,1,0:T(8,128)(2,1)S(1)} %get-tuple-element.34.refs_0_), channel_id=1, source_target_pairs={{0,56},{8,0},{16,8},{24,16},{32,24},{40,32},{48,40},{56,48},{64,12... | collective-permute-start | bytes 589832 | tf_op jit(solution)/shard_map/ppermute | solution.py:308
  14.4 3.2 %shard_map.65 = (bf16[8,128,128]{2,1,0:T(8,128)(2,1)S(1)}, f32[8,128,256]{2,1,0:T(8,128)S(1)}) custom-call(bf16[512,256]{1,0:T(8,128)(2,1)S(1)} %bitcast.17, bf16[512,256]{1,0:T(8,128)(2,1)S(1)} %bitcast.16, f32[8,128]{1,0:T(8,128)S(1)} %get-tuple-element.36.scale_ref, f32[8,128,384]{2,1,0:T(8,128)S(1)} %get-tuple-element.37.wu_ref, ...), custom_call_target="tpu_custom_call" | custom-call | flops 2000000000 | bytes 4984832 | tf_op jit(solution)/shard_map/pallas_call | solution.py:217
  17.6 1.6 %collective-permute-done.1.refs_1_ = bf16[2,128,384]{2,1,0:T(8,128)(2,1)S(1)} collective-permute-done((bf16[2,128,384]{2,1,0:T(8,128)(2,1)S(1)}, bf16[2,128,384]{2,1,0:T(8,128)(2,1)S(1)}, u32[]{:S(2)}, u32[]{:S(2)}) %collective-permute-start.1) | collective-permute-done | bytes 196640 | tf_op jit(solution)/shard_map/ppermute | solution.py:308
  19.2 3.4 %collective-permute-done.refs_8_ = bf16[2,128,384]{2,1,0:T(8,128)(2,1)S(1)} collective-permute-done((bf16[2,128,384]{2,1,0:T(8,128)(2,1)S(1)}, bf16[2,128,384]{2,1,0:T(8,128)(2,1)S(1)}, u32[]{:S(2)}, u32[]{:S(2)}) %collective-permute-start) | collective-permute-done | bytes 196640 | tf_op jit(solution)/shard_map/ppermute | solution.py:307
  22.9 1.7 %collective-permute-start.4 = (bf16[2,128,384]{2,1,0:T(8,128)(2,1)S(1)}, bf16[2,128,384]{2,1,0:T(8,128)(2,1)S(1)}, u32[]{:S(2)}, u32[]{:S(2)}) collective-permute-start(bf16[2,128,384]{2,1,0:T(8,128)(2,1)S(1)} %collective-permute-done.refs_8_), channel_id=1, source_target_pairs={{0,8},{8,16},{16,24},{24,32},{32,40},{40,48},{48,56},{56,0},{64,72... | collective-permute-start | bytes 589832 | tf_op jit(solution)/shard_map/ppermute | solution.py:307
  24.6 4.2 %collective-permute-done.2.refs_2_ = bf16[2,128,384]{2,1,0:T(8,128)(2,1)S(1)} collective-permute-done((bf16[2,128,384]{2,1,0:T(8,128)(2,1)S(1)}, bf16[2,128,384]{2,1,0:T(8,128)(2,1)S(1)}, u32[]{:S(2)}, u32[]{:S(2)}) %collective-permute-start.2) | collective-permute-done | bytes 196640 | tf_op jit(solution)/shard_map/ppermute | solution.py:308
  28.8 1.8 %collective-permute-start.3 = (bf16[2,128,384]{2,1,0:T(8,128)(2,1)S(1)}, bf16[2,128,384]{2,1,0:T(8,128)(2,1)S(1)}, u32[]{:S(2)}, u32[]{:S(2)}) collective-permute-start(bf16[2,128,384]{2,1,0:T(8,128)(2,1)S(1)} %collective-permute-done.2.refs_2_), channel_id=1, source_target_pairs={{0,56},{8,0},{16,8},{24,16},{32,24},{40,32},{48,40},{56,48},{64,12... | collective-permute-start | bytes 589832 | tf_op jit(solution)/shard_map/ppermute | solution.py:308
  30.8 3.6 %collective-permute-done.3.refs_3_ = bf16[2,128,384]{2,1,0:T(8,128)(2,1)S(1)} collective-permute-done((bf16[2,128,384]{2,1,0:T(8,128)(2,1)S(1)}, bf16[2,128,384]{2,1,0:T(8,128)(2,1)S(1)}, u32[]{:S(2)}, u32[]{:S(2)}) %collective-permute-start.3) | collective-permute-done | bytes 196640 | tf_op jit(solution)/shard_map/ppermute | solution.py:308
  34.5 3.1 %collective-permute-start.7 = (bf16[128,384]{1,0:T(8,128)(2,1)S(1)}, bf16[128,384]{1,0:T(8,128)(2,1)S(1)}, u32[]{:S(2)}, u32[]{:S(2)}) collective-permute-start(bf16[128,384]{1,0:T(8,128)(2,1)S(1)} %slice_bitcast_fusion), channel_id=1, source_target_pairs={{0,56},{8,0},{16,8},{24,16},{32,24},{40,32},{48,40},{56,48},{64,12... | collective-permute-start | bytes 294920 | tf_op jit(solution)/shard_map/ppermute | solution.py:315
  37.7 2.1 %collective-permute-done.7.refs_5_ = bf16[128,384]{1,0:T(8,128)(2,1)S(1)} collective-permute-done((bf16[128,384]{1,0:T(8,128)(2,1)S(1)}, bf16[128,384]{1,0:T(8,128)(2,1)S(1)}, u32[]{:S(2)}, u32[]{:S(2)}) %collective-permute-start.7) | collective-permute-done | bytes 98336 | tf_op jit(solution)/shard_map/ppermute | solution.py:315
  39.8 3.7 %collective-permute-done.6.refs_4_ = bf16[128,384]{1,0:T(8,128)(2,1)S(1)} collective-permute-done((bf16[128,384]{1,0:T(8,128)(2,1)S(1)}, bf16[128,384]{1,0:T(8,128)(2,1)S(1)}, u32[]{:S(2)}, u32[]{:S(2)}) %collective-permute-start.6) | collective-permute-done | bytes 98336 | tf_op jit(solution)/shard_map/ppermute | solution.py:314
  43.5 1.9 %shard_map.66 = (f32[2,128,384]{2,1,0:T(8,128)S(1)}, bf16[2,128,384]{2,1,0:T(8,128)(2,1)S(1)}) custom-call(bf16[2,128,384]{2,1,0:T(8,128)(2,1)S(1)} %get-tuple-element.34.refs_0_, bf16[2,128,384]{2,1,0:T(8,128)(2,1)S(1)} %collective-permute-done.1.refs_1_, bf16[2,128,384]{2,1,0:T(8,128)(2,1)S(1)} %collective-permute-done.2.refs_2_, ...), custom_call_target="tpu_custom_call" | custom-call | flops 1000000000 | bytes 2162688 | tf_op jit(solution)/shard_map/pallas_call | solution.py:217
  45.4 3.1 %collective-permute-start.10 = (bf16[2,128,384]{2,1,0:T(8,128)(2,1)S(1)}, bf16[2,128,384]{2,1,0:T(8,128)(2,1)S(1)}, u32[]{:S(2)}, u32[]{:S(2)}) collective-permute-start(bf16[2,128,384]{2,1,0:T(8,128)(2,1)S(1)} %get-tuple-element.43), channel_id=1, source_target_pairs={{0,64},{8,72},{16,80},{24,88},{32,96},{40,104},{48,112},{56,120},{... | collective-permute-start | bytes 589832 | tf_op jit(solution)/shard_map/ppermute | solution.py:324
  48.5 1.3 %collective-permute-start.9 = (bf16[2,128,384]{2,1,0:T(8,128)(2,1)S(1)}, bf16[2,128,384]{2,1,0:T(8,128)(2,1)S(1)}, u32[]{:S(2)}, u32[]{:S(2)}) collective-permute-start(bf16[2,128,384]{2,1,0:T(8,128)(2,1)S(1)} %get-tuple-element.43), channel_id=1, source_target_pairs={{0,128},{8,136},{16,144},{24,152},{32,160},{40,168},{48,176},{56,1... | collective-permute-start | bytes 589832 | tf_op jit(solution)/shard_map/ppermute | solution.py:324
  50.5 4.2 %collective-permute-done.10.near_ref = bf16[2,128,384]{2,1,0:T(8,128)(2,1)S(1)} collective-permute-done((bf16[2,128,384]{2,1,0:T(8,128)(2,1)S(1)}, bf16[2,128,384]{2,1,0:T(8,128)(2,1)S(1)}, u32[]{:S(2)}, u32[]{:S(2)}) %collective-permute-start.10) | collective-permute-done | bytes 196640 | tf_op jit(solution)/shard_map/ppermute | solution.py:324
  54.7 2.9 %collective-permute-done.9.mid_ref = bf16[2,128,384]{2,1,0:T(8,128)(2,1)S(1)} collective-permute-done((bf16[2,128,384]{2,1,0:T(8,128)(2,1)S(1)}, bf16[2,128,384]{2,1,0:T(8,128)(2,1)S(1)}, u32[]{:S(2)}, u32[]{:S(2)}) %collective-permute-start.9) | collective-permute-done | bytes 196640 | tf_op jit(solution)/shard_map/ppermute | solution.py:324
  57.6 1.1 %shard_map.67 = (bf16[256,512]{1,0:T(8,128)(2,1)S(1)}, bf16[256,512]{1,0:T(8,128)(2,1)S(1)}) custom-call(bf16[2,128,384]{2,1,0:T(8,128)(2,1)S(1)} %collective-permute-done.8.far_ref, bf16[2,128,384]{2,1,0:T(8,128)(2,1)S(1)} %collective-permute-done.9.mid_ref, bf16[2,128,384]{2,1,0:T(8,128)(2,1)S(1)} %collective-permute-done.10.near_ref, ...), custom_call_target="tpu_custom_call" | custom-call | flops 500000000 | bytes 2818048 | tf_op jit(solution)/shard_map/pallas_call | solution.py:217
  58.8 1.5 %collective-permute-done.11.joined_ref = bf16[256,512]{1,0:T(8,128)(2,1)S(1)} collective-permute-done((bf16[256,512]{1,0:T(8,128)(2,1)S(1)}, bf16[256,512]{1,0:T(8,128)(2,1)S(1)}, u32[]{:S(2)}, u32[]{:S(2)}) %collective-permute-start.11) | collective-permute-done | bytes 262176 | tf_op jit(solution)/shard_map/ppermute | solution.py:333
  61.1 1.7 %collective-permute-start.13 = (bf16[128,1024]{1,0:T(8,128)(2,1)S(1)}, bf16[128,1024]{1,0:T(8,128)(2,1)S(1)}, u32[]{:S(2)}, u32[]{:S(2)}) collective-permute-start(bf16[128,1024]{1,0:T(8,128)(2,1)S(1)} %get-tuple-element.56), channel_id=1, source_target_pairs={{0,2},{1,3},{2,0},{3,1},{4,6},{5,7},{6,4},{7,5},{8,10},{9,11},{10,... | collective-permute-start | bytes 786440 | tf_op jit(solution)/shard_map/ppermute | solution.py:345
  62.7 2.2 %collective-permute-start.15 = (bf16[128,1024]{1,0:T(8,128)(2,1)S(1)}, bf16[128,1024]{1,0:T(8,128)(2,1)S(1)}, u32[]{:S(2)}, u32[]{:S(2)}) collective-permute-start(bf16[128,1024]{1,0:T(8,128)(2,1)S(1)} %get-tuple-element.58), channel_id=1, source_target_pairs={{0,6},{1,7},{2,4},{3,5},{4,2},{5,3},{6,0},{7,1},{8,14},{9,15},{10,... | collective-permute-start | bytes 786440 | tf_op jit(solution)/shard_map/ppermute | solution.py:346
  67.0 1.3 %shard_map.70 = (bf16[64,4096]{1,0:T(8,128)(2,1)S(1)}, bf16[64,4096]{1,0:T(8,128)(2,1)S(1)}) custom-call(bf16[256,512]{1,0:T(8,128)(2,1)S(1)} %get-tuple-element.54.keep_ref, bf16[256,512]{1,0:T(8,128)(2,1)S(1)} %collective-permute-done.11.joined_ref, bf16[512,4096]{1,0:T(8,128)(2,1)S(1)} %copy-done, bf16[512,4096]{1,0:T(8,128)(2,1)S(1)} %collective-permute-done.12.other_w_ref), custom_call_target="tpu_custom_call" | custom-call | flops 1000000000 | bytes 9961472 | tf_op jit(solution)/shard_map/pallas_call | solution.py:217
  68.3 2.0 %collective-permute-done.13.sent_ref.refs_1_ = bf16[128,1024]{1,0:T(8,128)(2,1)S(1)} collective-permute-done((bf16[128,1024]{1,0:T(8,128)(2,1)S(1)}, bf16[128,1024]{1,0:T(8,128)(2,1)S(1)}, u32[]{:S(2)}, u32[]{:S(2)}) %collective-permute-start.13) | collective-permute-done | bytes 262176 | tf_op jit(solution)/shard_map/ppermute | solution.py:345
  70.3 3.1 %collective-permute-start.17 = (bf16[64,1024]{1,0:T(8,128)(2,1)S(1)}, bf16[64,1024]{1,0:T(8,128)(2,1)S(1)}, u32[]{:S(2)}, u32[]{:S(2)}) collective-permute-start(bf16[64,1024]{1,0:T(8,128)(2,1)S(1)} %shard_map.71), channel_id=1, source_target_pairs={{0,6},{1,7},{2,4},{3,5},{4,2},{5,3},{6,0},{7,1},{8,14},{9,15},{10,... | collective-permute-start | bytes 393224 | tf_op jit(solution)/shard_map/ppermute | solution.py:358
  73.7 2.1 %collective-permute-done.14.sent_ref.refs_2_ = bf16[128,1024]{1,0:T(8,128)(2,1)S(1)} collective-permute-done((bf16[128,1024]{1,0:T(8,128)(2,1)S(1)}, bf16[128,1024]{1,0:T(8,128)(2,1)S(1)}, u32[]{:S(2)}, u32[]{:S(2)}) %collective-permute-start.14) | collective-permute-done | bytes 262176 | tf_op jit(solution)/shard_map/ppermute | solution.py:345
  75.8 3.2 %collective-permute-start.18 = (bf16[64,1024]{1,0:T(8,128)(2,1)S(1)}, bf16[64,1024]{1,0:T(8,128)(2,1)S(1)}, u32[]{:S(2)}, u32[]{:S(2)}) collective-permute-start(bf16[64,1024]{1,0:T(8,128)(2,1)S(1)} %shard_map.72), channel_id=1, source_target_pairs={{0,6},{1,7},{2,4},{3,5},{4,2},{5,3},{6,0},{7,1},{8,14},{9,15},{10,... | collective-permute-start | bytes 393224 | tf_op jit(solution)/shard_map/ppermute | solution.py:358
  79.3 2.2 %collective-permute-done.17.refs_5_ = bf16[64,1024]{1,0:T(8,128)(2,1)S(1)} collective-permute-done((bf16[64,1024]{1,0:T(8,128)(2,1)S(1)}, bf16[64,1024]{1,0:T(8,128)(2,1)S(1)}, u32[]{:S(2)}, u32[]{:S(2)}) %collective-permute-start.17) | collective-permute-done | bytes 131104 | tf_op jit(solution)/shard_map/ppermute | solution.py:358
  81.6 1.7 %collective-permute-done.18.refs_6_ = bf16[64,1024]{1,0:T(8,128)(2,1)S(1)} collective-permute-done((bf16[64,1024]{1,0:T(8,128)(2,1)S(1)}, bf16[64,1024]{1,0:T(8,128)(2,1)S(1)}, u32[]{:S(2)}, u32[]{:S(2)}) %collective-permute-start.18) | collective-permute-done | bytes 131104 | tf_op jit(solution)/shard_map/ppermute | solution.py:358
  83.2 0.9 %collective-permute-done.20.refs_8_ = bf16[64,1024]{1,0:T(8,128)(2,1)S(1)} collective-permute-done((bf16[64,1024]{1,0:T(8,128)(2,1)S(1)}, bf16[64,1024]{1,0:T(8,128)(2,1)S(1)}, u32[]{:S(2)}, u32[]{:S(2)}) %collective-permute-start.20) | collective-permute-done | bytes 131104 | tf_op jit(solution)/shard_map/ppermute | solution.py:358
  84.1 1.0 %shard_map.75 = bf16[64,4096]{1,0:T(8,128)(2,1)} custom-call(bf16[64,4096]{1,0:T(8,128)(2,1)S(1)} %get-tuple-element.55.refs_0_, bf16[128,1024]{1,0:T(8,128)(2,1)S(1)} %collective-permute-done.13.sent_ref.refs_1_, bf16[128,1024]{1,0:T(8,128)(2,1)S(1)} %collective-permute-done.14.sent_ref.refs_2_, ...), custom_call_target="tpu_custom_call" | custom-call | flops 1000000 | bytes 2621440 | tf_op jit(solution)/shard_map/pallas_call | solution.py:217
  (31 shorter events, 4.8 us)
Async XLA Ops:
  0.0 60.3 %collective-permute-start.12 = (bf16[512,4096]{1,0:T(8,128)(2,1)}, bf16[512,4096]{1,0:T(8,128)(2,1)S(1)}, u32[]{:S(2)}, u32[]{:S(2)}) collective-permute-start(bf16[512,4096]{1,0:T(8,128)(2,1)} %own_w_ref.5), channel_id=1, source_target_pairs={{0,1},{1,0},{2,3},{3,2},{4,5},{5,4},{6,7},{7,6},{8,9},{9,8},{10,11... | collective-permute-start | bytes 12582920 | tf_op jit(solution)/shard_map/ppermute | solution.py:276
  2.1 12.2 %copy-start.1 = (bf16[512,2,128]{2,1,0:T(2,128)(2,1)S(1)}, bf16[512,2,128]{2,1,0:T(2,128)(2,1)}, u32[]{:S(2)}) copy-start(bf16[512,2,128]{2,1,0:T(2,128)(2,1)} %param.6) | copy-start | bytes 786436
  8.4 10.8 %collective-permute-start.1 = (bf16[2,128,384]{2,1,0:T(8,128)(2,1)S(1)}, bf16[2,128,384]{2,1,0:T(8,128)(2,1)S(1)}, u32[]{:S(2)}, u32[]{:S(2)}) collective-permute-start(bf16[2,128,384]{2,1,0:T(8,128)(2,1)S(1)} %get-tuple-element.34.refs_0_), channel_id=1, source_target_pairs={{0,56},{8,0},{16,8},{24,16},{32,24},{40,32},{48,40},{56,48},{64,12... | collective-permute-start | bytes 589832 | tf_op jit(solution)/shard_map/ppermute | solution.py:308
  14.3 8.2 %collective-permute-start = (bf16[2,128,384]{2,1,0:T(8,128)(2,1)S(1)}, bf16[2,128,384]{2,1,0:T(8,128)(2,1)S(1)}, u32[]{:S(2)}, u32[]{:S(2)}) collective-permute-start(bf16[2,128,384]{2,1,0:T(8,128)(2,1)S(1)} %get-tuple-element.34.refs_0_), channel_id=1, source_target_pairs={{0,8},{8,16},{16,24},{24,32},{32,40},{40,48},{48,56},{56,0},{64,72... | collective-permute-start | bytes 589832 | tf_op jit(solution)/shard_map/ppermute | solution.py:307
  17.6 42.7 %copy-start = (bf16[512,4096]{1,0:T(8,128)(2,1)S(1)}, bf16[512,4096]{1,0:T(8,128)(2,1)}, u32[]{:S(2)}) copy-start(bf16[512,4096]{1,0:T(8,128)(2,1)} %own_w_ref.5) | copy-start | bytes 12582916
  22.6 6.2 %collective-permute-start.2 = (bf16[2,128,384]{2,1,0:T(8,128)(2,1)S(1)}, bf16[2,128,384]{2,1,0:T(8,128)(2,1)S(1)}, u32[]{:S(2)}, u32[]{:S(2)}) collective-permute-start(bf16[2,128,384]{2,1,0:T(8,128)(2,1)S(1)} %collective-permute-done.1.refs_1_), channel_id=1, source_target_pairs={{0,56},{8,0},{16,8},{24,16},{32,24},{40,32},{48,40},{56,48},{64,12... | collective-permute-start | bytes 589832 | tf_op jit(solution)/shard_map/ppermute | solution.py:308
  22.9 7.8 %collective-permute-start.4 = (bf16[2,128,384]{2,1,0:T(8,128)(2,1)S(1)}, bf16[2,128,384]{2,1,0:T(8,128)(2,1)S(1)}, u32[]{:S(2)}, u32[]{:S(2)}) collective-permute-start(bf16[2,128,384]{2,1,0:T(8,128)(2,1)S(1)} %collective-permute-done.refs_8_), channel_id=1, source_target_pairs={{0,8},{8,16},{16,24},{24,32},{32,40},{40,48},{48,56},{56,0},{64,72... | collective-permute-start | bytes 589832 | tf_op jit(solution)/shard_map/ppermute | solution.py:307
  28.8 5.7 %collective-permute-start.3 = (bf16[2,128,384]{2,1,0:T(8,128)(2,1)S(1)}, bf16[2,128,384]{2,1,0:T(8,128)(2,1)S(1)}, u32[]{:S(2)}, u32[]{:S(2)}) collective-permute-start(bf16[2,128,384]{2,1,0:T(8,128)(2,1)S(1)} %collective-permute-done.2.refs_2_), channel_id=1, source_target_pairs={{0,56},{8,0},{16,8},{24,16},{32,24},{40,32},{48,40},{56,48},{64,12... | collective-permute-start | bytes 589832 | tf_op jit(solution)/shard_map/ppermute | solution.py:308
  30.6 7.0 %collective-permute-start.5 = (bf16[2,128,384]{2,1,0:T(8,128)(2,1)S(1)}, bf16[2,128,384]{2,1,0:T(8,128)(2,1)S(1)}, u32[]{:S(2)}, u32[]{:S(2)}) collective-permute-start(bf16[2,128,384]{2,1,0:T(8,128)(2,1)S(1)} %collective-permute-done.4.refs_7_), channel_id=1, source_target_pairs={{0,8},{8,16},{16,24},{24,32},{32,40},{40,48},{48,56},{56,0},{64,72... | collective-permute-start | bytes 589832 | tf_op jit(solution)/shard_map/ppermute | solution.py:307
  34.5 5.3 %collective-permute-start.7 = (bf16[128,384]{1,0:T(8,128)(2,1)S(1)}, bf16[128,384]{1,0:T(8,128)(2,1)S(1)}, u32[]{:S(2)}, u32[]{:S(2)}) collective-permute-start(bf16[128,384]{1,0:T(8,128)(2,1)S(1)} %slice_bitcast_fusion), channel_id=1, source_target_pairs={{0,56},{8,0},{16,8},{24,16},{32,24},{40,32},{48,40},{56,48},{64,12... | collective-permute-start | bytes 294920 | tf_op jit(solution)/shard_map/ppermute | solution.py:315
  37.6 5.9 %collective-permute-start.6 = (bf16[128,384]{1,0:T(8,128)(2,1)S(1)}, bf16[128,384]{1,0:T(8,128)(2,1)S(1)}, u32[]{:S(2)}, u32[]{:S(2)}) collective-permute-start(bf16[128,384]{1,0:T(8,128)(2,1)S(1)} %slice_bitcast_fusion.1), channel_id=1, source_target_pairs={{0,8},{8,16},{16,24},{24,32},{32,40},{40,48},{48,56},{56,0},{64,72... | collective-permute-start | bytes 294920 | tf_op jit(solution)/shard_map/ppermute | solution.py:314
  45.4 9.3 %collective-permute-start.10 = (bf16[2,128,384]{2,1,0:T(8,128)(2,1)S(1)}, bf16[2,128,384]{2,1,0:T(8,128)(2,1)S(1)}, u32[]{:S(2)}, u32[]{:S(2)}) collective-permute-start(bf16[2,128,384]{2,1,0:T(8,128)(2,1)S(1)} %get-tuple-element.43), channel_id=1, source_target_pairs={{0,64},{8,72},{16,80},{24,88},{32,96},{40,104},{48,112},{56,120},{... | collective-permute-start | bytes 589832 | tf_op jit(solution)/shard_map/ppermute | solution.py:324
  48.5 9.1 %collective-permute-start.9 = (bf16[2,128,384]{2,1,0:T(8,128)(2,1)S(1)}, bf16[2,128,384]{2,1,0:T(8,128)(2,1)S(1)}, u32[]{:S(2)}, u32[]{:S(2)}) collective-permute-start(bf16[2,128,384]{2,1,0:T(8,128)(2,1)S(1)} %get-tuple-element.43), channel_id=1, source_target_pairs={{0,128},{8,136},{16,144},{24,152},{32,160},{40,168},{48,176},{56,1... | collective-permute-start | bytes 589832 | tf_op jit(solution)/shard_map/ppermute | solution.py:324
  49.8 7.8 %collective-permute-start.8 = (bf16[2,128,384]{2,1,0:T(8,128)(2,1)S(1)}, bf16[2,128,384]{2,1,0:T(8,128)(2,1)S(1)}, u32[]{:S(2)}, u32[]{:S(2)}) collective-permute-start(bf16[2,128,384]{2,1,0:T(8,128)(2,1)S(1)} %get-tuple-element.43), channel_id=1, source_target_pairs={{0,192},{8,200},{16,208},{24,216},{32,224},{40,232},{48,240},{56,2... | collective-permute-start | bytes 589832 | tf_op jit(solution)/shard_map/ppermute | solution.py:324
  58.7 1.6 %collective-permute-start.11 = (bf16[256,512]{1,0:T(8,128)(2,1)S(1)}, bf16[256,512]{1,0:T(8,128)(2,1)S(1)}, u32[]{:S(2)}, u32[]{:S(2)}) collective-permute-start(bf16[256,512]{1,0:T(8,128)(2,1)S(1)} %get-tuple-element.48), channel_id=1, source_target_pairs={{0,1},{1,0},{2,3},{3,2},{4,5},{5,4},{6,7},{7,6},{8,9},{9,8},{10,11... | collective-permute-start | bytes 786440 | tf_op jit(solution)/shard_map/ppermute | solution.py:333
  61.1 9.2 %collective-permute-start.13 = (bf16[128,1024]{1,0:T(8,128)(2,1)S(1)}, bf16[128,1024]{1,0:T(8,128)(2,1)S(1)}, u32[]{:S(2)}, u32[]{:S(2)}) collective-permute-start(bf16[128,1024]{1,0:T(8,128)(2,1)S(1)} %get-tuple-element.56), channel_id=1, source_target_pairs={{0,2},{1,3},{2,0},{3,1},{4,6},{5,7},{6,4},{7,5},{8,10},{9,11},{10,... | collective-permute-start | bytes 786440 | tf_op jit(solution)/shard_map/ppermute | solution.py:345
  62.7 10.7 %collective-permute-start.15 = (bf16[128,1024]{1,0:T(8,128)(2,1)S(1)}, bf16[128,1024]{1,0:T(8,128)(2,1)S(1)}, u32[]{:S(2)}, u32[]{:S(2)}) collective-permute-start(bf16[128,1024]{1,0:T(8,128)(2,1)S(1)} %get-tuple-element.58), channel_id=1, source_target_pairs={{0,6},{1,7},{2,4},{3,5},{4,2},{5,3},{6,0},{7,1},{8,14},{9,15},{10,... | collective-permute-start | bytes 786440 | tf_op jit(solution)/shard_map/ppermute | solution.py:346
  65.6 10.1 %collective-permute-start.14 = (bf16[128,1024]{1,0:T(8,128)(2,1)S(1)}, bf16[128,1024]{1,0:T(8,128)(2,1)S(1)}, u32[]{:S(2)}, u32[]{:S(2)}) collective-permute-start(bf16[128,1024]{1,0:T(8,128)(2,1)S(1)} %get-tuple-element.57), channel_id=1, source_target_pairs={{0,2},{1,3},{2,0},{3,1},{4,6},{5,7},{6,4},{7,5},{8,10},{9,11},{10,... | collective-permute-start | bytes 786440 | tf_op jit(solution)/shard_map/ppermute | solution.py:345
  66.4 12.7 %collective-permute-start.16 = (bf16[128,1024]{1,0:T(8,128)(2,1)S(1)}, bf16[128,1024]{1,0:T(8,128)(2,1)S(1)}, u32[]{:S(2)}, u32[]{:S(2)}) collective-permute-start(bf16[128,1024]{1,0:T(8,128)(2,1)S(1)} %get-tuple-element.59), channel_id=1, source_target_pairs={{0,6},{1,7},{2,4},{3,5},{4,2},{5,3},{6,0},{7,1},{8,14},{9,15},{10,... | collective-permute-start | bytes 786440 | tf_op jit(solution)/shard_map/ppermute | solution.py:346
  70.3 11.2 %collective-permute-start.17 = (bf16[64,1024]{1,0:T(8,128)(2,1)S(1)}, bf16[64,1024]{1,0:T(8,128)(2,1)S(1)}, u32[]{:S(2)}, u32[]{:S(2)}) collective-permute-start(bf16[64,1024]{1,0:T(8,128)(2,1)S(1)} %shard_map.71), channel_id=1, source_target_pairs={{0,6},{1,7},{2,4},{3,5},{4,2},{5,3},{6,0},{7,1},{8,14},{9,15},{10,... | collective-permute-start | bytes 393224 | tf_op jit(solution)/shard_map/ppermute | solution.py:358
  73.5 8.1 %collective-permute-start.19 = (bf16[64,1024]{1,0:T(8,128)(2,1)S(1)}, bf16[64,1024]{1,0:T(8,128)(2,1)S(1)}, u32[]{:S(2)}, u32[]{:S(2)}) collective-permute-start(bf16[64,1024]{1,0:T(8,128)(2,1)S(1)} %shard_map.73), channel_id=1, source_target_pairs={{0,2},{1,3},{2,0},{3,1},{4,6},{5,7},{6,4},{7,5},{8,10},{9,11},{10,... | collective-permute-start | bytes 393224 | tf_op jit(solution)/shard_map/ppermute | solution.py:358
  75.8 7.4 %collective-permute-start.18 = (bf16[64,1024]{1,0:T(8,128)(2,1)S(1)}, bf16[64,1024]{1,0:T(8,128)(2,1)S(1)}, u32[]{:S(2)}, u32[]{:S(2)}) collective-permute-start(bf16[64,1024]{1,0:T(8,128)(2,1)S(1)} %shard_map.72), channel_id=1, source_target_pairs={{0,6},{1,7},{2,4},{3,5},{4,2},{5,3},{6,0},{7,1},{8,14},{9,15},{10,... | collective-permute-start | bytes 393224 | tf_op jit(solution)/shard_map/ppermute | solution.py:358
  79.1 5.1 %collective-permute-start.20 = (bf16[64,1024]{1,0:T(8,128)(2,1)S(1)}, bf16[64,1024]{1,0:T(8,128)(2,1)S(1)}, u32[]{:S(2)}, u32[]{:S(2)}) collective-permute-start(bf16[64,1024]{1,0:T(8,128)(2,1)S(1)} %shard_map.74), channel_id=1, source_target_pairs={{0,2},{1,3},{2,0},{3,1},{4,6},{5,7},{6,4},{7,5},{8,10},{9,11},{10,... | collective-permute-start | bytes 393224 | tf_op jit(solution)/shard_map/ppermute | solution.py:358

commit v4 on v3

v4 whole, which is shorter than its diff:
```python
import functools

import jax
import jax.numpy as jnp
from jax import lax
from jax.experimental import pallas as pl
from jax.experimental.pallas import tpu as pltpu
from jax.sharding import PartitionSpec as P

BLOCK = 128
INTERPRET = False
VMEM_LIMIT = 12 << 20
CHUNK = 1024
F32 = jnp.float32
BF16 = jnp.bfloat16


def split(x):
    high = x.astype(BF16)
    return high, (x - high.astype(F32)).astype(BF16)


def dot(a, b):
    return jnp.dot(a, b, preferred_element_type=F32)


def dot_t(a, b):
    return lax.dot_general(a, b, (((0,), (0,)), ((), ())), preferred_element_type=F32)


def dot_nt(a, b):
    return lax.dot_general(a, b, (((1,), (1,)), ((), ())), preferred_element_type=F32)


def dot3(a, b):
    a_high, a_low = split(a)
    b_high, b_low = split(b)
    left = jnp.concatenate([a_high, a_low], 1)
    right = jnp.concatenate([b_high, b_low], 1)
    both = dot(left, jnp.concatenate([right, right], 0))
    width = b.shape[1]
    return both[:, :width] + both[:, width:]


def dot2_right(a, b):
    b_high, b_low = split(b)
    return dot(jnp.concatenate([a, a], 1), jnp.concatenate([b_high, b_low], 0))


def dot2_left(a, b):
    a_high, a_low = split(a)
    return dot(jnp.concatenate([a_high, a_low], 1), jnp.concatenate([b, b], 0))


def square_ids(n):
    return lax.broadcasted_iota(jnp.int32, (n, n), 0), lax.broadcasted_iota(jnp.int32, (n, n), 1)


def head_rows(ref, b, head):
    row = lax.broadcasted_iota(jnp.int32, (BLOCK, 2 * BLOCK), 0)
    col = lax.broadcasted_iota(jnp.int32, (BLOCK, 2 * BLOCK), 1)
    chosen = jnp.where(col == 2 * row + head, 1.0, 0.0).astype(BF16)
    return dot(chosen, ref[b * 2 * BLOCK : (b + 1) * 2 * BLOCK]).astype(BF16)


def terms_kernel(head, resets_hbm, beta_hbm, k_ref, v_ref, *refs):
    wu_ref, prefix_ref, scale_ref, rows_ref, carry_ref, resets, beta_ref, sems = refs
    resets_copy = pltpu.make_async_copy(resets_hbm, resets, sems.at[0])
    beta_copy = pltpu.make_async_copy(beta_hbm, beta_ref, sems.at[1])
    beta_copy.start()
    resets_copy.start()
    row, col = square_ids(BLOCK)
    eye = row == col
    identity = jnp.where(eye, 1.0, 0.0).astype(F32)
    blocks = range(4)
    ks = [head_rows(k_ref, b, head) for b in blocks]
    vs = [head_rows(v_ref, b, head) for b in blocks]
    grams = [dot_nt(k, k) for k in ks]
    beta_copy.wait()
    lower, inv, r_cols, beta_rows, c_rows = [], [], [], [], []
    for b in blocks:
        gram = grams[b]
        diagonal = jnp.where(eye, gram, 0.0)
        r_col = lax.rsqrt(jnp.sum(diagonal, axis=1, keepdims=True) + 1e-06)
        r_row = lax.rsqrt(jnp.sum(diagonal, axis=0, keepdims=True) + 1e-06)
        beta_row = beta_ref[head : head + 1, b * BLOCK : (b + 1) * BLOCK]
        beta_col = jnp.sum(jnp.where(eye, beta_row, 0.0), axis=1, keepdims=True)
        low = jnp.where(row > col, (beta_col * r_col) * gram * r_row, 0.0)
        lower.append(low)
        inv.append(identity - jnp.where(row // 2 == col // 2, low, 0.0))
        r_cols.append(r_col)
        beta_rows.append(beta_row)
        c_rows.append(beta_row * r_row)
        scale_ref[b : b + 1, :] = r_row
        rows_ref[b] = ks[b]
    size = 2
    while size < BLOCK:
        joined = (row // (2 * size) == col // (2 * size)) & (row // size != col // size)
        half = [dot3(jnp.where(joined, lower[b], 0.0), inv[b]) for b in blocks]
        inv = [inv[b] - dot3(inv[b], half[b]) for b in blocks]
        size *= 2
    steps = []
    for b in blocks:
        decay = dot2_left(inv[b] * c_rows[b], ks[b])
        update = dot2_left(inv[b] * beta_rows[b], vs[b])
        wu = jnp.concatenate([decay, update], 1)
        wu_ref[b] = wu
        high, low = split(wu * r_cols[b])
        steps.append(
            dot_t(jnp.concatenate([ks[b], ks[b]], 0), jnp.concatenate([high, low], 0))
        )
    zeros = jnp.zeros((BLOCK, 256), F32)
    state = jnp.concatenate([identity, zeros], 1)
    resets_copy.wait()
    for b in blocks:
        starts = (resets[0, 0] == b) | (resets[0, 1] == b)
        kept = jnp.where(starts, 0.0, 1.0).astype(F32)
        before = state * kept
        prefix_ref[b] = before
        step = steps[b]
        added = jnp.concatenate([jnp.zeros((BLOCK, 128), F32), step[:, 128:]], 1)
        if b == 0:
            moved = jnp.concatenate([step[:, :128] * kept, zeros], 1)
        else:
            moved = dot3(step[:, :128], before)
        state = before - moved + added
    carry_ref[...] = jnp.concatenate([state[:, :128] - identity, state[:, 128:]], 1).astype(BF16)


def response_kernel(head, q_ref, k_ref, scale_ref, wu_ref, prefix_ref, r_ref, o_ref):
    row, col = square_ids(BLOCK)
    causal = row >= col
    for b in range(4):
        q = head_rows(q_ref, b, head)
        qf = q.astype(F32)
        rq = lax.rsqrt(jnp.sum(qf * qf, axis=1, keepdims=True) + 1e-06)
        scores = jnp.where(causal, rq * dot_nt(q, k_ref[b]) * scale_ref[b : b + 1, :], 0.0)
        local = dot3(scores, wu_ref[b])
        reach = qf * rq - local[:, :128]
        out = dot3(reach, prefix_ref[b])
        r_ref[b] = out[:, :128].astype(BF16)
        o_ref[b] = out[:, 128:] + local[:, 128:]


def follow(state, element):
    moved = dot2_right(element[:, :128], state)
    width = state.shape[1]
    added = element.astype(F32)
    if width == 256:
        added = added[:, 128:]
    else:
        added = jnp.concatenate([jnp.zeros((BLOCK, 128), F32), added[:, 128:]], 1)
    return state + moved + added


def group_kernel(*refs):
    elements, (before_ref, total_ref) = refs[:8], refs[8:]
    z = lax.axis_index("seq") % 8
    row, col = square_ids(BLOCK)
    identity = jnp.where(row == col, 1.0, 0.0).astype(F32)
    empty = jnp.concatenate([identity, jnp.zeros((BLOCK, 256), F32)], 1)
    state = after = empty
    for step in range(1, 8):
        wraps = z + step == 8
        if step > 1:
            after = jnp.where(wraps, state, after)
            state = jnp.where(wraps, empty, state)
        state = follow(state, elements[step][...])
    after = jnp.where(z == 0, state, after)
    state = jnp.where(z == 0, empty, state)
    before_ref[...] = jnp.concatenate([state[:, :128] - identity, state[:, 128:]], 1)
    through = follow(state, elements[0][...])
    total = dot3(after[:, :128], through)
    total_ref[...] = jnp.concatenate(
        [total[:, :128] - identity, total[:, 128:] + after[:, 128:]], 1
    ).astype(BF16)


def output_kernel(far_ref, mid_ref, near_ref, *refs):
    before_refs, r_refs, o_refs, (keep_ref, send_ref) = refs[:2], refs[2:4], refs[4:6], refs[6:]
    head = lax.axis_index("head")
    y, core = head // 2, head % 2
    states = []
    for h in range(2):
        state = far_ref[h][:, 128:].astype(F32)
        state = follow(state, mid_ref[h])
        state = follow(state, near_ref[h])
        before = before_refs[h][...]
        states.append(state + dot3(before[:, :128], state) + before[:, 128:])
    for b in range(4):
        parts = []
        for h in range(2):
            out = dot2_right(r_refs[h][b], states[h]) + o_refs[h][b]
            mean = jnp.mean(out * out, axis=1, keepdims=True)
            parts.append((out * lax.rsqrt(mean + 1e-05)).astype(BF16))
        normed = jnp.concatenate(parts, 1)
        first, second = normed[:64], normed[64:]
        slot = pl.multiple_of(((4 - (y ^ b)) & 3) * 64, 64)
        keep_ref[pl.ds(slot, 64), :] = jnp.where(core == 0, first, second)
        send_ref[pl.ds(slot, 64), :] = jnp.where(core == 0, second, first)


HBM = pl.BlockSpec(memory_space=pltpu.HBM)
VMEM = pl.BlockSpec(memory_space=pltpu.VMEM)


def call(kernel, outs, arrays, flops, in_hbm=(), scratch=()):
    moved = sum(a.size * a.dtype.itemsize for a in (*in_hbm, *arrays, *outs))
    return pl.pallas_call(
        kernel,
        out_shape=[jax.ShapeDtypeStruct(a.shape, a.dtype) for a in outs],
        in_specs=[HBM] * len(in_hbm) + [VMEM] * len(arrays),
        out_specs=[VMEM] * len(outs),
        scratch_shapes=scratch,
        compiler_params=pltpu.CompilerParams(vmem_limit_bytes=VMEM_LIMIT),
        cost_estimate=pl.CostEstimate(flops=flops, bytes_accessed=moved, transcendentals=0),
        interpret=INTERPRET,
    )(*[pltpu.with_memory_space_constraint(a, pltpu.HBM) for a in in_hbm], *arrays)


def rows_product(own_rows, other_rows, own_w_ref, other_w_ref, first):
    columns = slice(first, first + CHUNK)
    out = dot(own_rows, own_w_ref[:, columns]) + dot(other_rows, other_w_ref[:, columns])
    return out.astype(BF16)


def send_kernel(part, keep_ref, joined_ref, own_w_ref, other_w_ref, near_ref, far_ref):
    weights = own_w_ref, other_w_ref, part * CHUNK
    near_ref[...] = rows_product(keep_ref[128:], joined_ref[128:], *weights)
    weights = own_w_ref, other_w_ref, 2048 + part * CHUNK
    far_ref[...] = rows_product(keep_ref[64:192], joined_ref[64:192], *weights)


def own_kernel(keep_ref, joined_ref, own_w_ref, other_w_ref, final_ref, passed_ref):
    for part in range(4):
        columns = slice(part * CHUNK, (part + 1) * CHUNK)
        weights = own_w_ref, other_w_ref, part * CHUNK
        if part < 2:
            out = rows_product(keep_ref[:128], joined_ref[:128], *weights)
        else:
            own_rows = jnp.concatenate([keep_ref[:64], keep_ref[192:]], 0)
            other_rows = jnp.concatenate([joined_ref[:64], joined_ref[192:]], 0)
            out = rows_product(own_rows, other_rows, *weights)
        final_ref[:, columns] = out[:64]
        passed_ref[:, columns] = out[64:]


def pair_kernel(part, passed_ref, sent_ref, out_ref):
    half = slice(0, 64) if part < 2 else slice(64, 128)
    own = passed_ref[:, part * CHUNK : (part + 1) * CHUNK].astype(F32)
    out_ref[...] = (own + sent_ref[half].astype(F32)).astype(BF16)


def sum_kernel(*refs):
    final_ref, out_ref = refs[0], refs[9]
    for part in range(4):
        columns = slice(part * CHUNK, (part + 1) * CHUNK)
        half = slice(64, 128) if part < 2 else slice(0, 64)
        total = final_ref[:, columns].astype(F32) + refs[1 + part][half].astype(F32)
        out_ref[:, columns] = (total + refs[5 + part][...].astype(F32)).astype(BF16)


def body(queries, keys, values, beta, reset_blocks, out_weight):
    q = queries.reshape(1024, 128)
    k = keys.reshape(1024, 128)
    v = values.reshape(1024, 256)

    across = [(i, i ^ 1) for i in range(8)]
    shaped = jax.ShapeDtypeStruct
    terms = []
    for h in range(2):
        terms.append(
            list(call(
                functools.partial(terms_kernel, h),
                [
                    shaped((4, 128, 384), F32),
                    shaped((4, 128, 384), F32),
                    shaped((4, 128), F32),
                    shaped((4, 128, 128), BF16),
                    shaped((128, 384), BF16),
                ],
                [k, v],
                1_500_000_000,
                in_hbm=[reset_blocks, beta],
                scratch=[
                    pltpu.SMEM((1, 2), jnp.int32),
                    pltpu.VMEM((2, 512), F32),
                    pltpu.SemaphoreType.DMA((2,)),
                ],
            ))
        )
        if h == 0:
            k, swapped, terms[0][4] = lax.optimization_barrier((k, out_weight, terms[0][4]))
            other_weight = lax.ppermute(swapped, "head", across)
    up = [(i, i - i % 8 + (i + 1) % 8) for i in range(32)]
    down = [(i, i - i % 8 + (i + 7) % 8) for i in range(32)]
    below = [[terms[h][4]] for h in range(2)]
    above = [[terms[h][4]] for h in range(2)]
    for step in range(3):
        for h in range(2):
            below[h].append(lax.ppermute(below[h][-1], "seq", up))
            above[h].append(lax.ppermute(above[h][-1], "seq", down))
    opposite = [
        lax.ppermute(below[0][3], "seq", up),
        lax.ppermute(above[1][3], "seq", down),
    ]
    befores, totals = [], []
    for h in range(2):
        before, total = call(
            group_kernel,
            [shaped((128, 384), F32), shaped((128, 384), BF16)],
            above[h] + [opposite[h]] + below[h][:0:-1],
            500_000_000,
        )
        befores.append(before)
        totals.append(total)
    total = jnp.stack(totals)
    received = [
        lax.ppermute(total, "seq", [(i, i + 8 * d) for i in range(32) if i + 8 * d < 32])
        for d in (3, 2, 1)
    ]
    responses = []
    for h in range(2):
        wu, prefix, scale, rows, _ = terms[h]
        responses.append(
            call(
                functools.partial(response_kernel, h),
                [shaped((4, 128, 128), BF16), shaped((4, 128, 256), F32)],
                [q, rows, scale, wu, prefix],
                1_000_000_000,
            )
        )
    keep, send = call(
        output_kernel,
        [shaped((256, 512), BF16), shaped((256, 512), BF16)],
        received + befores + [r[0] for r in responses] + [r[1] for r in responses],
        500_000_000,
    )
    joined = lax.ppermute(send, "head", across)
    operands = [keep, joined, out_weight, other_weight]
    near = [(i, i ^ 2) for i in range(8)]
    far = [(i, i ^ 6) for i in range(8)]
    half = [shaped((128, CHUNK), BF16)] * 2
    routes = [near, near, far, far]
    sent = [None] * 4
    for part in range(2):
        to_near, to_far = call(
            functools.partial(send_kernel, part), half, operands, 500_000_000
        )
        operands[0], to_near, to_far = lax.optimization_barrier((operands[0], to_near, to_far))
        sent[part] = lax.ppermute(to_near, "head", near)
        sent[part + 2] = lax.ppermute(to_far, "head", far)
    final, passed = call(
        own_kernel, [shaped((64, 4096), BF16)] * 2, operands, 1_000_000_000
    )
    received = [None] * 4
    for part in (0, 2, 1, 3):
        (summed,) = call(
            functools.partial(pair_kernel, part),
            [shaped((64, CHUNK), BF16)],
            [passed, sent[part]],
            100_000,
        )
        received[part] = lax.ppermute(summed, "head", routes[3 - part])
    return call(sum_kernel, [shaped((64, 4096), BF16)], [final, *sent, *received], 1_000_000)[0]


def solution(mesh):
    return jax.shard_map(
        body,
        mesh=mesh,
        in_specs=(
            P("seq", "head", None),
            P("seq", "head", None),
            P("seq", "head", None),
            P("head", "seq"),
            P("seq", None),
            P("head", None),
        ),
        out_specs=P(("seq", "head"), None),
        check_vma=False,
    )
```

time: 86.6 us -> 84.6 us (0.977)
  the two profiles are of different devices: /device:TPU:4 before, /device:TPU:6 now
where the time goes in v4:
time: 84.6 us; the launch traced here: 84.4 us
  starting transfers between devices  39.4 us (47%)
  Pallas kernels  21.8 us (26%)
  waiting for transfers between devices  20.7 us (24%)
  local copies, waits for them, and re-layouts  2.35 us (3%)
    pallas_call x15, Pallas kernels, call(): pl.pallas_call(kernel, out_shape=[jax.ShapeDtypeStruct(a.shape, a.dtype)...  21.8 us
    ppermute x6, starting transfers between devices, body(): above[h].append(lax.ppermute(above[h][-1], 'seq', down))  16.4 us
    ppermute x4, starting transfers between devices, body(): received[part] = lax.ppermute(summed, 'head', routes[3 - part])  6.8 us
    ppermute x3, waiting for transfers between devices, body(): lax.ppermute(total, 'seq', [(i, i + 8 * d) for i in range(32) if i + 8 *...  6.5 us
    ppermute x4, waiting for transfers between devices, body(): received[part] = lax.ppermute(summed, 'head', routes[3 - part])  4.83 us
    ppermute x2, waiting for transfers between devices, body(): sent[part] = lax.ppermute(to_near, 'head', near)  4.09 us
    ppermute x3, starting transfers between devices, body(): lax.ppermute(total, 'seq', [(i, i + 8 * d) for i in range(32) if i + 8 *...  3.88 us
    ppermute x1, starting transfers between devices, body(): lax.ppermute(above[1][3], 'seq', down)  3.69 us
  transfers between devices with their start and end apart: 27, of which 15 were waited for; matrix products, arithmetic and copies ran while one was open for 0% of the time, Pallas kernels for 18%

profile of v4, /device:TPU:6, one launch (start us, length us, event | category | flops | bytes accessed | tf_op | source)
XLA Modules:
  0.0 84.4 jit_solution(15892374246177720076)
XLA Ops:
  0.0 1.2 %reshape.10.v_ref = bf16[1024,256]{1,0:T(8,128)(2,1)S(1)} reshape(bf16[512,2,256]{2,1,0:T(2,128)(2,1)} %param.8) | data formatting | bytes 1048576 | tf_op jit(solution)/shard_map/reshape | solution.py:266
  1.3 1.1 %copy-done.1 = bf16[512,2,128]{2,1,0:T(2,128)(2,1)S(1)} copy-done((bf16[512,2,128]{2,1,0:T(2,128)(2,1)S(1)}, bf16[512,2,128]{2,1,0:T(2,128)(2,1)}, u32[]{:S(2)}) %copy-start.1) | copy-done | bytes 262168
  2.4 5.0 %shard_map.64 = (f32[4,128,384]{2,1,0:T(8,128)S(1)}, f32[4,128,384]{2,1,0:T(8,128)S(1)}, f32[4,128]{1,0:T(4,128)S(1)}, bf16[4,128,128]{2,1,0:T(8,128)(2,1)S(1)}, bf16[128,384]{1,0:T(8,128)(2,1)S(1)}) custom-call(s32[1,2]{1,0:T(1,128)} %resets_hbm.3, f32[2,512]{1,0:T(2,128)} %beta_hbm.3, bf16[1024,128]{1,0:T(8,128)(2,1)S(1)} %bitcast.6, ...), custom_call_target="tpu_custom_call" | custom-call | flops 1500000000 | bytes 2594824 | tf_op jit(solution)/shard_map/pallas_call | solution.py:209
  7.5 2.0 %collective-permute-start.3 = (bf16[128,384]{1,0:T(8,128)(2,1)S(1)}, bf16[128,384]{1,0:T(8,128)(2,1)S(1)}, u32[]{:S(2)}, u32[]{:S(2)}) collective-permute-start(bf16[128,384]{1,0:T(8,128)(2,1)S(1)} %get-tuple-element.41.refs_0_), channel_id=1, source_target_pairs={{0,8},{8,16},{16,24},{24,32},{32,40},{40,48},{48,56},{56,0},{64,72... | collective-permute-start | bytes 294920 | tf_op jit(solution)/shard_map/ppermute | solution.py:301
  9.5 4.9 %shard_map.66 = (f32[4,128,384]{2,1,0:T(8,128)S(1)}, f32[4,128,384]{2,1,0:T(8,128)S(1)}, f32[4,128]{1,0:T(4,128)S(1)}, bf16[4,128,128]{2,1,0:T(8,128)(2,1)S(1)}, bf16[128,384]{1,0:T(8,128)(2,1)S(1)}) custom-call(s32[1,2]{1,0:T(1,128)} %resets_hbm.3, f32[2,512]{1,0:T(2,128)} %beta_hbm.3, bf16[1024,128]{1,0:T(8,128)(2,1)S(1)} %bitcast.7, ...), custom_call_target="tpu_custom_call" | custom-call | flops 1500000000 | bytes 2594824 | tf_op jit(solution)/shard_map/pallas_call | solution.py:209
  14.4 4.0 %collective-permute-start.7 = (bf16[128,384]{1,0:T(8,128)(2,1)S(1)}, bf16[128,384]{1,0:T(8,128)(2,1)S(1)}, u32[]{:S(2)}, u32[]{:S(2)}) collective-permute-start(bf16[128,384]{1,0:T(8,128)(2,1)S(1)} %get-tuple-element.44.refs_0_), channel_id=1, source_target_pairs={{0,56},{8,0},{16,8},{24,16},{32,24},{40,32},{48,40},{56,48},{64,12... | collective-permute-start | bytes 294920 | tf_op jit(solution)/shard_map/ppermute | solution.py:302
  18.4 2.0 %collective-permute-start = (bf16[128,384]{1,0:T(8,128)(2,1)S(1)}, bf16[128,384]{1,0:T(8,128)(2,1)S(1)}, u32[]{:S(2)}, u32[]{:S(2)}) collective-permute-start(bf16[128,384]{1,0:T(8,128)(2,1)S(1)} %get-tuple-element.41.refs_0_), channel_id=1, source_target_pairs={{0,56},{8,0},{16,8},{24,16},{32,24},{40,32},{48,40},{56,48},{64,12... | collective-permute-start | bytes 294920 | tf_op jit(solution)/shard_map/ppermute | solution.py:302
  21.6 3.7 %collective-permute-start.8 = (bf16[128,384]{1,0:T(8,128)(2,1)S(1)}, bf16[128,384]{1,0:T(8,128)(2,1)S(1)}, u32[]{:S(2)}, u32[]{:S(2)}) collective-permute-start(bf16[128,384]{1,0:T(8,128)(2,1)S(1)} %collective-permute-done.7.refs_1_), channel_id=1, source_target_pairs={{0,56},{8,0},{16,8},{24,16},{32,24},{40,32},{48,40},{56,48},{64,12... | collective-permute-start | bytes 294920 | tf_op jit(solution)/shard_map/ppermute | solution.py:302
  25.3 1.6 %collective-permute-start.1 = (bf16[128,384]{1,0:T(8,128)(2,1)S(1)}, bf16[128,384]{1,0:T(8,128)(2,1)S(1)}, u32[]{:S(2)}, u32[]{:S(2)}) collective-permute-start(bf16[128,384]{1,0:T(8,128)(2,1)S(1)} %collective-permute-done.refs_1_), channel_id=1, source_target_pairs={{0,56},{8,0},{16,8},{24,16},{32,24},{40,32},{48,40},{56,48},{64,12... | collective-permute-start | bytes 294920 | tf_op jit(solution)/shard_map/ppermute | solution.py:302
  28.1 3.7 %collective-permute-start.9 = (bf16[128,384]{1,0:T(8,128)(2,1)S(1)}, bf16[128,384]{1,0:T(8,128)(2,1)S(1)}, u32[]{:S(2)}, u32[]{:S(2)}) collective-permute-start(bf16[128,384]{1,0:T(8,128)(2,1)S(1)} %collective-permute-done.8.refs_2_), channel_id=1, source_target_pairs={{0,56},{8,0},{16,8},{24,16},{32,24},{40,32},{48,40},{56,48},{64,12... | collective-permute-start | bytes 294920 | tf_op jit(solution)/shard_map/ppermute | solution.py:302
  31.8 1.4 %collective-permute-start.2 = (bf16[128,384]{1,0:T(8,128)(2,1)S(1)}, bf16[128,384]{1,0:T(8,128)(2,1)S(1)}, u32[]{:S(2)}, u32[]{:S(2)}) collective-permute-start(bf16[128,384]{1,0:T(8,128)(2,1)S(1)} %collective-permute-done.1.refs_2_), channel_id=1, source_target_pairs={{0,56},{8,0},{16,8},{24,16},{32,24},{40,32},{48,40},{56,48},{64,12... | collective-permute-start | bytes 294920 | tf_op jit(solution)/shard_map/ppermute | solution.py:302
  34.8 3.7 %collective-permute-start.10 = (bf16[128,384]{1,0:T(8,128)(2,1)S(1)}, bf16[128,384]{1,0:T(8,128)(2,1)S(1)}, u32[]{:S(2)}, u32[]{:S(2)}) collective-permute-start(bf16[128,384]{1,0:T(8,128)(2,1)S(1)} %collective-permute-done.9.refs_3_), channel_id=1, source_target_pairs={{0,56},{8,0},{16,8},{24,16},{32,24},{40,32},{48,40},{56,48},{64,12... | collective-permute-start | bytes 294920 | tf_op jit(solution)/shard_map/ppermute | solution.py:305
  39.2 1.6 %shard_map.65 = (f32[128,384]{1,0:T(8,128)S(1)}, bf16[128,384]{1,0:T(8,128)(2,1)S(1)}) custom-call(bf16[128,384]{1,0:T(8,128)(2,1)S(1)} %get-tuple-element.41.refs_0_, bf16[128,384]{1,0:T(8,128)(2,1)S(1)} %collective-permute-done.refs_1_, bf16[128,384]{1,0:T(8,128)(2,1)S(1)} %collective-permute-done.1.refs_2_, ...), custom_call_target="tpu_custom_call" | custom-call | flops 500000000 | bytes 1081344 | tf_op jit(solution)/shard_map/pallas_call | solution.py:209
  40.9 1.6 %shard_map.67 = (f32[128,384]{1,0:T(8,128)S(1)}, bf16[128,384]{1,0:T(8,128)(2,1)S(1)}) custom-call(bf16[128,384]{1,0:T(8,128)(2,1)S(1)} %get-tuple-element.44.refs_0_, bf16[128,384]{1,0:T(8,128)(2,1)S(1)} %collective-permute-done.7.refs_1_, bf16[128,384]{1,0:T(8,128)(2,1)S(1)} %collective-permute-done.8.refs_2_, ...), custom_call_target="tpu_custom_call" | custom-call | flops 500000000 | bytes 1081344 | tf_op jit(solution)/shard_map/pallas_call | solution.py:209
  42.5 1.3 %collective-permute-start.16 = (bf16[2,128,384]{2,1,0:T(8,128)(2,1)S(1)}, bf16[2,128,384]{2,1,0:T(8,128)(2,1)S(1)}, u32[]{:S(2)}, u32[]{:S(2)}) collective-permute-start(bf16[2,128,384]{2,1,0:T(8,128)(2,1)S(1)} %pad_maximum_fusion), channel_id=1, source_target_pairs={{0,64},{8,72},{16,80},{24,88},{32,96},{40,104},{48,112},{56,120},{... | collective-permute-start | bytes 589832 | tf_op jit(solution)/shard_map/ppermute | solution.py:319
  43.8 1.3 %collective-permute-start.15 = (bf16[2,128,384]{2,1,0:T(8,128)(2,1)S(1)}, bf16[2,128,384]{2,1,0:T(8,128)(2,1)S(1)}, u32[]{:S(2)}, u32[]{:S(2)}) collective-permute-start(bf16[2,128,384]{2,1,0:T(8,128)(2,1)S(1)} %pad_maximum_fusion), channel_id=1, source_target_pairs={{0,128},{8,136},{16,144},{24,152},{32,160},{40,168},{48,176},{56,1... | collective-permute-start | bytes 589832 | tf_op jit(solution)/shard_map/ppermute | solution.py:319
  45.1 1.3 %collective-permute-start.14 = (bf16[2,128,384]{2,1,0:T(8,128)(2,1)S(1)}, bf16[2,128,384]{2,1,0:T(8,128)(2,1)S(1)}, u32[]{:S(2)}, u32[]{:S(2)}) collective-permute-start(bf16[2,128,384]{2,1,0:T(8,128)(2,1)S(1)} %pad_maximum_fusion), channel_id=1, source_target_pairs={{0,192},{8,200},{16,208},{24,216},{32,224},{40,232},{48,240},{56,2... | collective-permute-start | bytes 589832 | tf_op jit(solution)/shard_map/ppermute | solution.py:319
  46.4 1.9 %shard_map.68 = (bf16[4,128,128]{2,1,0:T(8,128)(2,1)S(1)}, f32[4,128,256]{2,1,0:T(8,128)S(1)}) custom-call(bf16[1024,128]{1,0:T(8,128)(2,1)S(1)} %bitcast.8, bf16[4,128,128]{2,1,0:T(8,128)(2,1)S(1)} %get-tuple-element.48.k_ref, f32[4,128]{1,0:T(4,128)S(1)} %get-tuple-element.49.scale_ref, f32[4,128,384]{2,1,0:T(8,128)S(1)} %get-tuple-element.50.wu_ref, ...), custom_call_target="tpu_custom_call" | custom-call | flops 1000000000 | bytes 2623488 | tf_op jit(solution)/shard_map/pallas_call | solution.py:209
  48.3 1.9 %shard_map.69 = (bf16[4,128,128]{2,1,0:T(8,128)(2,1)S(1)}, f32[4,128,256]{2,1,0:T(8,128)S(1)}) custom-call(bf16[1024,128]{1,0:T(8,128)(2,1)S(1)} %bitcast.9, bf16[4,128,128]{2,1,0:T(8,128)(2,1)S(1)} %get-tuple-element.53.k_ref, f32[4,128]{1,0:T(4,128)S(1)} %get-tuple-element.54.scale_ref, f32[4,128,384]{2,1,0:T(8,128)S(1)} %get-tuple-element.55.wu_ref, ...), custom_call_target="tpu_custom_call" | custom-call | flops 1000000000 | bytes 2623488 | tf_op jit(solution)/shard_map/pallas_call | solution.py:209
  50.1 2.8 %collective-permute-done.15.mid_ref = bf16[2,128,384]{2,1,0:T(8,128)(2,1)S(1)} collective-permute-done((bf16[2,128,384]{2,1,0:T(8,128)(2,1)S(1)}, bf16[2,128,384]{2,1,0:T(8,128)(2,1)S(1)}, u32[]{:S(2)}, u32[]{:S(2)}) %collective-permute-start.15) | collective-permute-done | bytes 196640 | tf_op jit(solution)/shard_map/ppermute | solution.py:319
  53.0 3.7 %collective-permute-done.14.far_ref = bf16[2,128,384]{2,1,0:T(8,128)(2,1)S(1)} collective-permute-done((bf16[2,128,384]{2,1,0:T(8,128)(2,1)S(1)}, bf16[2,128,384]{2,1,0:T(8,128)(2,1)S(1)}, u32[]{:S(2)}, u32[]{:S(2)}) %collective-permute-start.14) | collective-permute-done | bytes 196640 | tf_op jit(solution)/shard_map/ppermute | solution.py:319
  56.6 1.2 %shard_map.70 = (bf16[256,512]{1,0:T(8,128)(2,1)S(1)}, bf16[256,512]{1,0:T(8,128)(2,1)S(1)}) custom-call(bf16[2,128,384]{2,1,0:T(8,128)(2,1)S(1)} %collective-permute-done.14.far_ref, bf16[2,128,384]{2,1,0:T(8,128)(2,1)S(1)} %collective-permute-done.15.mid_ref, bf16[2,128,384]{2,1,0:T(8,128)(2,1)S(1)} %collective-permute-done.16.near_ref, ...), custom_call_target="tpu_custom_call" | custom-call | flops 500000000 | bytes 2818048 | tf_op jit(solution)/shard_map/pallas_call | solution.py:209
  58.1 1.5 %collective-permute-done.17.joined_ref = bf16[256,512]{1,0:T(8,128)(2,1)S(1)} collective-permute-done((bf16[256,512]{1,0:T(8,128)(2,1)S(1)}, bf16[256,512]{1,0:T(8,128)(2,1)S(1)}, u32[]{:S(2)}, u32[]{:S(2)}) %collective-permute-start.17) | collective-permute-done | bytes 262176 | tf_op jit(solution)/shard_map/ppermute | solution.py:339
  60.4 1.7 %collective-permute-start.19 = (bf16[128,1024]{1,0:T(8,128)(2,1)S(1)}, bf16[128,1024]{1,0:T(8,128)(2,1)S(1)}, u32[]{:S(2)}, u32[]{:S(2)}) collective-permute-start(bf16[128,1024]{1,0:T(8,128)(2,1)S(1)} %get-tuple-element.70), channel_id=1, source_target_pairs={{0,2},{1,3},{2,0},{3,1},{4,6},{5,7},{6,4},{7,5},{8,10},{9,11},{10,... | collective-permute-start | bytes 786440 | tf_op jit(solution)/shard_map/ppermute | solution.py:351
  62.0 2.2 %collective-permute-start.21 = (bf16[128,1024]{1,0:T(8,128)(2,1)S(1)}, bf16[128,1024]{1,0:T(8,128)(2,1)S(1)}, u32[]{:S(2)}, u32[]{:S(2)}) collective-permute-start(bf16[128,1024]{1,0:T(8,128)(2,1)S(1)} %get-tuple-element.72), channel_id=1, source_target_pairs={{0,6},{1,7},{2,4},{3,5},{4,2},{5,3},{6,0},{7,1},{8,14},{9,15},{10,... | collective-permute-start | bytes 786440 | tf_op jit(solution)/shard_map/ppermute | solution.py:352
  66.3 1.3 %shard_map.73 = (bf16[64,4096]{1,0:T(8,128)(2,1)S(1)}, bf16[64,4096]{1,0:T(8,128)(2,1)S(1)}) custom-call(bf16[256,512]{1,0:T(8,128)(2,1)S(1)} %get-tuple-element.68.keep_ref, bf16[256,512]{1,0:T(8,128)(2,1)S(1)} %collective-permute-done.17.joined_ref, bf16[512,4096]{1,0:T(8,128)(2,1)S(1)} %copy-done, bf16[512,4096]{1,0:T(8,128)(2,1)S(1)} %collective-permute-done.18.other_w_ref), custom_call_target="tpu_custom_call" | custom-call | flops 1000000000 | bytes 9961472 | tf_op jit(solution)/shard_map/pallas_call | solution.py:209
  67.6 2.0 %collective-permute-done.19.sent_ref.refs_1_ = bf16[128,1024]{1,0:T(8,128)(2,1)S(1)} collective-permute-done((bf16[128,1024]{1,0:T(8,128)(2,1)S(1)}, bf16[128,1024]{1,0:T(8,128)(2,1)S(1)}, u32[]{:S(2)}, u32[]{:S(2)}) %collective-permute-start.19) | collective-permute-done | bytes 262176 | tf_op jit(solution)/shard_map/ppermute | solution.py:351
  69.6 3.1 %collective-permute-start.23 = (bf16[64,1024]{1,0:T(8,128)(2,1)S(1)}, bf16[64,1024]{1,0:T(8,128)(2,1)S(1)}, u32[]{:S(2)}, u32[]{:S(2)}) collective-permute-start(bf16[64,1024]{1,0:T(8,128)(2,1)S(1)} %shard_map.74), channel_id=1, source_target_pairs={{0,6},{1,7},{2,4},{3,5},{4,2},{5,3},{6,0},{7,1},{8,14},{9,15},{10,... | collective-permute-start | bytes 393224 | tf_op jit(solution)/shard_map/ppermute | solution.py:364
  73.0 2.1 %collective-permute-done.20.sent_ref.refs_2_ = bf16[128,1024]{1,0:T(8,128)(2,1)S(1)} collective-permute-done((bf16[128,1024]{1,0:T(8,128)(2,1)S(1)}, bf16[128,1024]{1,0:T(8,128)(2,1)S(1)}, u32[]{:S(2)}, u32[]{:S(2)}) %collective-permute-start.20) | collective-permute-done | bytes 262176 | tf_op jit(solution)/shard_map/ppermute | solution.py:351
  75.1 3.2 %collective-permute-start.24 = (bf16[64,1024]{1,0:T(8,128)(2,1)S(1)}, bf16[64,1024]{1,0:T(8,128)(2,1)S(1)}, u32[]{:S(2)}, u32[]{:S(2)}) collective-permute-start(bf16[64,1024]{1,0:T(8,128)(2,1)S(1)} %shard_map.75), channel_id=1, source_target_pairs={{0,6},{1,7},{2,4},{3,5},{4,2},{5,3},{6,0},{7,1},{8,14},{9,15},{10,... | collective-permute-start | bytes 393224 | tf_op jit(solution)/shard_map/ppermute | solution.py:364
  78.6 2.2 %collective-permute-done.23.refs_5_ = bf16[64,1024]{1,0:T(8,128)(2,1)S(1)} collective-permute-done((bf16[64,1024]{1,0:T(8,128)(2,1)S(1)}, bf16[64,1024]{1,0:T(8,128)(2,1)S(1)}, u32[]{:S(2)}, u32[]{:S(2)}) %collective-permute-start.23) | collective-permute-done | bytes 131104 | tf_op jit(solution)/shard_map/ppermute | solution.py:364
  80.9 1.7 %collective-permute-done.24.refs_6_ = bf16[64,1024]{1,0:T(8,128)(2,1)S(1)} collective-permute-done((bf16[64,1024]{1,0:T(8,128)(2,1)S(1)}, bf16[64,1024]{1,0:T(8,128)(2,1)S(1)}, u32[]{:S(2)}, u32[]{:S(2)}) %collective-permute-start.24) | collective-permute-done | bytes 131104 | tf_op jit(solution)/shard_map/ppermute | solution.py:364
  (45 shorter events, 10.5 us)
Async XLA Ops:
  1.2 6.1 %copy-start = (bf16[512,4096]{1,0:T(8,128)(2,1)S(1)}, bf16[512,4096]{1,0:T(8,128)(2,1)}, u32[]{:S(2)}) copy-start(bf16[512,4096]{1,0:T(8,128)(2,1)} %own_w_ref.5) | copy-start | bytes 12582916
  1.3 1.1 %copy-start.1 = (bf16[512,2,128]{2,1,0:T(2,128)(2,1)S(1)}, bf16[512,2,128]{2,1,0:T(2,128)(2,1)}, u32[]{:S(2)}) copy-start(bf16[512,2,128]{2,1,0:T(2,128)(2,1)} %param.7) | copy-start | bytes 786436
  7.4 39.0 %copy-start.2 = (bf16[512,2,128]{2,1,0:T(2,128)(2,1)S(1)}, bf16[512,2,128]{2,1,0:T(2,128)(2,1)}, u32[]{:S(2)}) copy-start(bf16[512,2,128]{2,1,0:T(2,128)(2,1)} %param.6) | copy-start | bytes 786436
  7.4 52.3 %collective-permute-start.18 = (bf16[512,4096]{1,0:T(8,128)(2,1)S(1)}, bf16[512,4096]{1,0:T(8,128)(2,1)S(1)}, u32[]{:S(2)}, u32[]{:S(2)}) collective-permute-start(bf16[512,4096]{1,0:T(8,128)(2,1)S(1)} %copy-done), channel_id=1, source_target_pairs={{0,1},{1,0},{2,3},{3,2},{4,5},{5,4},{6,7},{7,6},{8,9},{9,8},{10,11... | collective-permute-start | bytes 12582920 | tf_op jit(solution)/shard_map/ppermute | solution.py:294
  7.5 13.0 %collective-permute-start.3 = (bf16[128,384]{1,0:T(8,128)(2,1)S(1)}, bf16[128,384]{1,0:T(8,128)(2,1)S(1)}, u32[]{:S(2)}, u32[]{:S(2)}) collective-permute-start(bf16[128,384]{1,0:T(8,128)(2,1)S(1)} %get-tuple-element.41.refs_0_), channel_id=1, source_target_pairs={{0,8},{8,16},{16,24},{24,32},{32,40},{40,48},{48,56},{56,0},{64,72... | collective-permute-start | bytes 294920 | tf_op jit(solution)/shard_map/ppermute | solution.py:301
  14.4 7.1 %collective-permute-start.7 = (bf16[128,384]{1,0:T(8,128)(2,1)S(1)}, bf16[128,384]{1,0:T(8,128)(2,1)S(1)}, u32[]{:S(2)}, u32[]{:S(2)}) collective-permute-start(bf16[128,384]{1,0:T(8,128)(2,1)S(1)} %get-tuple-element.44.refs_0_), channel_id=1, source_target_pairs={{0,56},{8,0},{16,8},{24,16},{32,24},{40,32},{48,40},{56,48},{64,12... | collective-permute-start | bytes 294920 | tf_op jit(solution)/shard_map/ppermute | solution.py:302
  18.4 6.8 %collective-permute-start = (bf16[128,384]{1,0:T(8,128)(2,1)S(1)}, bf16[128,384]{1,0:T(8,128)(2,1)S(1)}, u32[]{:S(2)}, u32[]{:S(2)}) collective-permute-start(bf16[128,384]{1,0:T(8,128)(2,1)S(1)} %get-tuple-element.41.refs_0_), channel_id=1, source_target_pairs={{0,56},{8,0},{16,8},{24,16},{32,24},{40,32},{48,40},{56,48},{64,12... | collective-permute-start | bytes 294920 | tf_op jit(solution)/shard_map/ppermute | solution.py:302
  20.5 6.6 %collective-permute-start.4 = (bf16[128,384]{1,0:T(8,128)(2,1)S(1)}, bf16[128,384]{1,0:T(8,128)(2,1)S(1)}, u32[]{:S(2)}, u32[]{:S(2)}) collective-permute-start(bf16[128,384]{1,0:T(8,128)(2,1)S(1)} %collective-permute-done.3.refs_7_), channel_id=1, source_target_pairs={{0,8},{8,16},{16,24},{24,32},{32,40},{40,48},{48,56},{56,0},{64,72... | collective-permute-start | bytes 294920 | tf_op jit(solution)/shard_map/ppermute | solution.py:301
  20.5 7.6 %collective-permute-start.11 = (bf16[128,384]{1,0:T(8,128)(2,1)S(1)}, bf16[128,384]{1,0:T(8,128)(2,1)S(1)}, u32[]{:S(2)}, u32[]{:S(2)}) collective-permute-start(bf16[128,384]{1,0:T(8,128)(2,1)S(1)} %get-tuple-element.44.refs_0_), channel_id=1, source_target_pairs={{0,8},{8,16},{16,24},{24,32},{32,40},{40,48},{48,56},{56,0},{64,72... | collective-permute-start | bytes 294920 | tf_op jit(solution)/shard_map/ppermute | solution.py:301
  21.6 6.6 %collective-permute-start.8 = (bf16[128,384]{1,0:T(8,128)(2,1)S(1)}, bf16[128,384]{1,0:T(8,128)(2,1)S(1)}, u32[]{:S(2)}, u32[]{:S(2)}) collective-permute-start(bf16[128,384]{1,0:T(8,128)(2,1)S(1)} %collective-permute-done.7.refs_1_), channel_id=1, source_target_pairs={{0,56},{8,0},{16,8},{24,16},{32,24},{40,32},{48,40},{56,48},{64,12... | collective-permute-start | bytes 294920 | tf_op jit(solution)/shard_map/ppermute | solution.py:302
  25.3 6.6 %collective-permute-start.1 = (bf16[128,384]{1,0:T(8,128)(2,1)S(1)}, bf16[128,384]{1,0:T(8,128)(2,1)S(1)}, u32[]{:S(2)}, u32[]{:S(2)}) collective-permute-start(bf16[128,384]{1,0:T(8,128)(2,1)S(1)} %collective-permute-done.refs_1_), channel_id=1, source_target_pairs={{0,56},{8,0},{16,8},{24,16},{32,24},{40,32},{48,40},{56,48},{64,12... | collective-permute-start | bytes 294920 | tf_op jit(solution)/shard_map/ppermute | solution.py:302
  27.0 6.2 %collective-permute-start.5 = (bf16[128,384]{1,0:T(8,128)(2,1)S(1)}, bf16[128,384]{1,0:T(8,128)(2,1)S(1)}, u32[]{:S(2)}, u32[]{:S(2)}) collective-permute-start(bf16[128,384]{1,0:T(8,128)(2,1)S(1)} %collective-permute-done.4.refs_6_), channel_id=1, source_target_pairs={{0,8},{8,16},{16,24},{24,32},{32,40},{40,48},{48,56},{56,0},{64,72... | collective-permute-start | bytes 294920 | tf_op jit(solution)/shard_map/ppermute | solution.py:301
  28.1 6.2 %collective-permute-start.12 = (bf16[128,384]{1,0:T(8,128)(2,1)S(1)}, bf16[128,384]{1,0:T(8,128)(2,1)S(1)}, u32[]{:S(2)}, u32[]{:S(2)}) collective-permute-start(bf16[128,384]{1,0:T(8,128)(2,1)S(1)} %collective-permute-done.11.refs_7_), channel_id=1, source_target_pairs={{0,8},{8,16},{16,24},{24,32},{32,40},{40,48},{48,56},{56,0},{64,72... | collective-permute-start | bytes 294920 | tf_op jit(solution)/shard_map/ppermute | solution.py:301
  28.1 6.6 %collective-permute-start.9 = (bf16[128,384]{1,0:T(8,128)(2,1)S(1)}, bf16[128,384]{1,0:T(8,128)(2,1)S(1)}, u32[]{:S(2)}, u32[]{:S(2)}) collective-permute-start(bf16[128,384]{1,0:T(8,128)(2,1)S(1)} %collective-permute-done.8.refs_2_), channel_id=1, source_target_pairs={{0,56},{8,0},{16,8},{24,16},{32,24},{40,32},{48,40},{56,48},{64,12... | collective-permute-start | bytes 294920 | tf_op jit(solution)/shard_map/ppermute | solution.py:302
  31.8 6.6 %collective-permute-start.2 = (bf16[128,384]{1,0:T(8,128)(2,1)S(1)}, bf16[128,384]{1,0:T(8,128)(2,1)S(1)}, u32[]{:S(2)}, u32[]{:S(2)}) collective-permute-start(bf16[128,384]{1,0:T(8,128)(2,1)S(1)} %collective-permute-done.1.refs_2_), channel_id=1, source_target_pairs={{0,56},{8,0},{16,8},{24,16},{32,24},{40,32},{48,40},{56,48},{64,12... | collective-permute-start | bytes 294920 | tf_op jit(solution)/shard_map/ppermute | solution.py:302
  33.2 6.0 %collective-permute-start.6 = (bf16[128,384]{1,0:T(8,128)(2,1)S(1)}, bf16[128,384]{1,0:T(8,128)(2,1)S(1)}, u32[]{:S(2)}, u32[]{:S(2)}) collective-permute-start(bf16[128,384]{1,0:T(8,128)(2,1)S(1)} %collective-permute-done.5.refs_5_), channel_id=1, source_target_pairs={{0,8},{8,16},{16,24},{24,32},{32,40},{40,48},{48,56},{56,0},{64,72... | collective-permute-start | bytes 294920 | tf_op jit(solution)/shard_map/ppermute | solution.py:304
  34.3 6.6 %collective-permute-start.13 = (bf16[128,384]{1,0:T(8,128)(2,1)S(1)}, bf16[128,384]{1,0:T(8,128)(2,1)S(1)}, u32[]{:S(2)}, u32[]{:S(2)}) collective-permute-start(bf16[128,384]{1,0:T(8,128)(2,1)S(1)} %collective-permute-done.12.refs_6_), channel_id=1, source_target_pairs={{0,8},{8,16},{16,24},{24,32},{32,40},{40,48},{48,56},{56,0},{64,72... | collective-permute-start | bytes 294920 | tf_op jit(solution)/shard_map/ppermute | solution.py:301
  34.8 6.1 %collective-permute-start.10 = (bf16[128,384]{1,0:T(8,128)(2,1)S(1)}, bf16[128,384]{1,0:T(8,128)(2,1)S(1)}, u32[]{:S(2)}, u32[]{:S(2)}) collective-permute-start(bf16[128,384]{1,0:T(8,128)(2,1)S(1)} %collective-permute-done.9.refs_3_), channel_id=1, source_target_pairs={{0,56},{8,0},{16,8},{24,16},{32,24},{40,32},{48,40},{56,48},{64,12... | collective-permute-start | bytes 294920 | tf_op jit(solution)/shard_map/ppermute | solution.py:305
  42.5 7.6 %collective-permute-start.16 = (bf16[2,128,384]{2,1,0:T(8,128)(2,1)S(1)}, bf16[2,128,384]{2,1,0:T(8,128)(2,1)S(1)}, u32[]{:S(2)}, u32[]{:S(2)}) collective-permute-start(bf16[2,128,384]{2,1,0:T(8,128)(2,1)S(1)} %pad_maximum_fusion), channel_id=1, source_target_pairs={{0,64},{8,72},{16,80},{24,88},{32,96},{40,104},{48,112},{56,120},{... | collective-permute-start | bytes 589832 | tf_op jit(solution)/shard_map/ppermute | solution.py:319
  43.8 9.2 %collective-permute-start.15 = (bf16[2,128,384]{2,1,0:T(8,128)(2,1)S(1)}, bf16[2,128,384]{2,1,0:T(8,128)(2,1)S(1)}, u32[]{:S(2)}, u32[]{:S(2)}) collective-permute-start(bf16[2,128,384]{2,1,0:T(8,128)(2,1)S(1)} %pad_maximum_fusion), channel_id=1, source_target_pairs={{0,128},{8,136},{16,144},{24,152},{32,160},{40,168},{48,176},{56,1... | collective-permute-start | bytes 589832 | tf_op jit(solution)/shard_map/ppermute | solution.py:319
  45.1 11.5 %collective-permute-start.14 = (bf16[2,128,384]{2,1,0:T(8,128)(2,1)S(1)}, bf16[2,128,384]{2,1,0:T(8,128)(2,1)S(1)}, u32[]{:S(2)}, u32[]{:S(2)}) collective-permute-start(bf16[2,128,384]{2,1,0:T(8,128)(2,1)S(1)} %pad_maximum_fusion), channel_id=1, source_target_pairs={{0,192},{8,200},{16,208},{24,216},{32,224},{40,232},{48,240},{56,2... | collective-permute-start | bytes 589832 | tf_op jit(solution)/shard_map/ppermute | solution.py:319
  57.8 1.8 %collective-permute-start.17 = (bf16[256,512]{1,0:T(8,128)(2,1)S(1)}, bf16[256,512]{1,0:T(8,128)(2,1)S(1)}, u32[]{:S(2)}, u32[]{:S(2)}) collective-permute-start(bf16[256,512]{1,0:T(8,128)(2,1)S(1)} %get-tuple-element.61), channel_id=1, source_target_pairs={{0,1},{1,0},{2,3},{3,2},{4,5},{5,4},{6,7},{7,6},{8,9},{9,8},{10,11... | collective-permute-start | bytes 786440 | tf_op jit(solution)/shard_map/ppermute | solution.py:339
  60.4 9.2 %collective-permute-start.19 = (bf16[128,1024]{1,0:T(8,128)(2,1)S(1)}, bf16[128,1024]{1,0:T(8,128)(2,1)S(1)}, u32[]{:S(2)}, u32[]{:S(2)}) collective-permute-start(bf16[128,1024]{1,0:T(8,128)(2,1)S(1)} %get-tuple-element.70), channel_id=1, source_target_pairs={{0,2},{1,3},{2,0},{3,1},{4,6},{5,7},{6,4},{7,5},{8,10},{9,11},{10,... | collective-permute-start | bytes 786440 | tf_op jit(solution)/shard_map/ppermute | solution.py:351
  62.0 10.7 %collective-permute-start.21 = (bf16[128,1024]{1,0:T(8,128)(2,1)S(1)}, bf16[128,1024]{1,0:T(8,128)(2,1)S(1)}, u32[]{:S(2)}, u32[]{:S(2)}) collective-permute-start(bf16[128,1024]{1,0:T(8,128)(2,1)S(1)} %get-tuple-element.72), channel_id=1, source_target_pairs={{0,6},{1,7},{2,4},{3,5},{4,2},{5,3},{6,0},{7,1},{8,14},{9,15},{10,... | collective-permute-start | bytes 786440 | tf_op jit(solution)/shard_map/ppermute | solution.py:352
  64.9 10.1 %collective-permute-start.20 = (bf16[128,1024]{1,0:T(8,128)(2,1)S(1)}, bf16[128,1024]{1,0:T(8,128)(2,1)S(1)}, u32[]{:S(2)}, u32[]{:S(2)}) collective-permute-start(bf16[128,1024]{1,0:T(8,128)(2,1)S(1)} %get-tuple-element.71), channel_id=1, source_target_pairs={{0,2},{1,3},{2,0},{3,1},{4,6},{5,7},{6,4},{7,5},{8,10},{9,11},{10,... | collective-permute-start | bytes 786440 | tf_op jit(solution)/shard_map/ppermute | solution.py:351
  65.7 12.7 %collective-permute-start.22 = (bf16[128,1024]{1,0:T(8,128)(2,1)S(1)}, bf16[128,1024]{1,0:T(8,128)(2,1)S(1)}, u32[]{:S(2)}, u32[]{:S(2)}) collective-permute-start(bf16[128,1024]{1,0:T(8,128)(2,1)S(1)} %get-tuple-element.73), channel_id=1, source_target_pairs={{0,6},{1,7},{2,4},{3,5},{4,2},{5,3},{6,0},{7,1},{8,14},{9,15},{10,... | collective-permute-start | bytes 786440 | tf_op jit(solution)/shard_map/ppermute | solution.py:352
  69.6 11.2 %collective-permute-start.23 = (bf16[64,1024]{1,0:T(8,128)(2,1)S(1)}, bf16[64,1024]{1,0:T(8,128)(2,1)S(1)}, u32[]{:S(2)}, u32[]{:S(2)}) collective-permute-start(bf16[64,1024]{1,0:T(8,128)(2,1)S(1)} %shard_map.74), channel_id=1, source_target_pairs={{0,6},{1,7},{2,4},{3,5},{4,2},{5,3},{6,0},{7,1},{8,14},{9,15},{10,... | collective-permute-start | bytes 393224 | tf_op jit(solution)/shard_map/ppermute | solution.py:364
  72.8 8.1 %collective-permute-start.25 = (bf16[64,1024]{1,0:T(8,128)(2,1)S(1)}, bf16[64,1024]{1,0:T(8,128)(2,1)S(1)}, u32[]{:S(2)}, u32[]{:S(2)}) collective-permute-start(bf16[64,1024]{1,0:T(8,128)(2,1)S(1)} %shard_map.76), channel_id=1, source_target_pairs={{0,2},{1,3},{2,0},{3,1},{4,6},{5,7},{6,4},{7,5},{8,10},{9,11},{10,... | collective-permute-start | bytes 393224 | tf_op jit(solution)/shard_map/ppermute | solution.py:364
  75.1 7.4 %collective-permute-start.24 = (bf16[64,1024]{1,0:T(8,128)(2,1)S(1)}, bf16[64,1024]{1,0:T(8,128)(2,1)S(1)}, u32[]{:S(2)}, u32[]{:S(2)}) collective-permute-start(bf16[64,1024]{1,0:T(8,128)(2,1)S(1)} %shard_map.75), channel_id=1, source_target_pairs={{0,6},{1,7},{2,4},{3,5},{4,2},{5,3},{6,0},{7,1},{8,14},{9,15},{10,... | collective-permute-start | bytes 393224 | tf_op jit(solution)/shard_map/ppermute | solution.py:364
  78.4 5.1 %collective-permute-start.26 = (bf16[64,1024]{1,0:T(8,128)(2,1)S(1)}, bf16[64,1024]{1,0:T(8,128)(2,1)S(1)}, u32[]{:S(2)}, u32[]{:S(2)}) collective-permute-start(bf16[64,1024]{1,0:T(8,128)(2,1)S(1)} %shard_map.77), channel_id=1, source_target_pairs={{0,2},{1,3},{2,0},{3,1},{4,6},{5,7},{6,4},{7,5},{8,10},{9,11},{10,... | collective-permute-start | bytes 393224 | tf_op jit(solution)/shard_map/ppermute | solution.py:364

commit v5 on v3

--- a/solution.py
+++ b/solution.py
@@ -35,8 +35,11 @@
 def dot3(a, b):
     a_high, a_low = split(a)
     b_high, b_low = split(b)
-    both = dot(jnp.concatenate([a_high, a_low], 1), jnp.concatenate([b_high, b_high], 0))
-    return both + dot(a_high, b_low)
+    left = jnp.concatenate([a_high, a_low], 1)
+    right = jnp.concatenate([b_high, b_low], 1)
+    both = dot(left, jnp.concatenate([right, right], 0))
+    width = b.shape[1]
+    return both[:, :width] + both[:, width:]
 
 
 def dot2_right(a, b):
@@ -53,25 +56,44 @@
     return lax.broadcasted_iota(jnp.int32, (n, n), 0), lax.broadcasted_iota(jnp.int32, (n, n), 1)
 
 
-def terms_kernel(
-    resets_hbm, beta_hbm, k_ref, v_ref, wu_ref, prefix_ref, scale_ref, carry_ref, resets, beta_ref, sems
-):
+def head_rows(rows, width, place):
+    row = lax.broadcasted_iota(jnp.int32, (BLOCK, width * BLOCK), 0)
+    col = lax.broadcasted_iota(jnp.int32, (BLOCK, width * BLOCK), 1)
+    chosen = jnp.where(col == width * row + place, 1.0, 0.0).astype(BF16)
+    return dot(chosen, rows).astype(BF16)
+
+
+CELLS = [(b, h) for b in range(4) for h in range(2)]
+
+
+def after_map(first, second):
+    added = jnp.concatenate([jnp.zeros((BLOCK, 128), F32), second[:, 128:]], 1)
+    return dot3(second[:, :128], first) + added
+
+
+def terms_kernel(resets_hbm, beta_hbm, k_hbm, v_ref, *refs):
+    wu_ref, prefix_ref, scale_ref, rows_ref, carry_ref = refs[:5]
+    resets, beta_ref, k_ref, sems = refs[5:]
+    k_copy = pltpu.make_async_copy(k_hbm, k_ref, sems.at[2])
     resets_copy = pltpu.make_async_copy(resets_hbm, resets, sems.at[0])
     beta_copy = pltpu.make_async_copy(beta_hbm, beta_ref, sems.at[1])
+    k_copy.start()
     beta_copy.start()
     resets_copy.start()
     row, col = square_ids(BLOCK)
     eye = row == col
     identity = jnp.where(eye, 1.0, 0.0).astype(F32)
-    cells = [(b, h) for b in range(4) for h in range(2)]
     ks, vs, grams = {}, {}, {}
-    for b, h in cells:
-        ks[b, h] = k_ref[b * BLOCK : (b + 1) * BLOCK, h * 128 : (h + 1) * 128]
+    k_copy.wait()
+    for b, h in CELLS:
+        ks[b, h] = head_rows(k_ref[b * 2 * BLOCK : (b + 1) * 2 * BLOCK], 2, h)
         vs[b, h] = v_ref[b * BLOCK : (b + 1) * BLOCK, h * 256 : (h + 1) * 256]
-        grams[b, h] = dot_nt(ks[b, h], ks[b, h])
+        rows_ref[b * 2 + h] = ks[b, h]
+    for cell in CELLS:
+        grams[cell] = dot_nt(ks[cell], ks[cell])
     beta_copy.wait()
     lower, inv, r_cols, beta_rows, c_rows = {}, {}, {}, {}, {}
-    for b, h in cells:
+    for b, h in CELLS:
         gram = grams[b, h]
         diagonal = jnp.where(eye, gram, 0.0)
         r_col = lax.rsqrt(jnp.sum(diagonal, axis=1, keepdims=True) + 1e-06)
@@ -87,62 +109,59 @@
         scale_ref[b * 2 + h : b * 2 + h + 1, :] = r_row
     size = 2
     while size < BLOCK:
-        joined = (row // (2 * size) == col // (2 * size)) & (row // size != col // size)
-        half = {}
-        for cell in cells:
-            half[cell] = dot3(jnp.where(joined, lower[cell], 0.0), inv[cell])
-        for cell in cells:
-            inv[cell] = inv[cell] - dot3(inv[cell], half[cell])
-        size *= 2
-    steps = {}
-    for b, h in cells:
+        joined = (row // (4 * size) == col // (4 * size)) & (row // size != col // size)
+        links, squares, odds = {}, {}, {}
+        for cell in CELLS:
+            links[cell] = dot3(inv[cell], jnp.where(joined, lower[cell], 0.0))
+        for cell in CELLS:
+            squares[cell] = dot3(links[cell], links[cell])
+            odds[cell] = inv[cell] - dot3(links[cell], inv[cell])
+        for cell in CELLS:
+            inv[cell] = odds[cell] + dot3(squares[cell], odds[cell])
+        size *= 4
+    resets_copy.wait()
+    maps = {}
+    kept = []
+    for b in range(4):
+        starts = (resets[0, 0] == b) | (resets[0, 1] == b)
+        kept.append(jnp.where(starts, 0.0, 1.0).astype(F32))
+    for b, h in CELLS:
         cell = (b, h)
         decay = dot2_left(inv[cell] * c_rows[cell], ks[cell])
         update = dot2_left(inv[cell] * beta_rows[cell], vs[cell])
         wu = jnp.concatenate([decay, update], 1)
         wu_ref[b * 2 + h] = wu
         high, low = split(wu * r_cols[cell])
-        steps[cell] = dot_t(
-            jnp.concatenate([ks[cell], ks[cell]], 0), jnp.concatenate([high, low], 0)
-        )
+        step = dot_t(jnp.concatenate([ks[cell], ks[cell]], 0), jnp.concatenate([high, low], 0))
+        maps[cell] = jnp.concatenate([(identity - step[:, :128]) * kept[b], step[:, 128:]], 1)
     zeros = jnp.zeros((BLOCK, 256), F32)
-    state = {h: jnp.concatenate([identity, zeros], 1) for h in range(2)}
-    resets_copy.wait()
-    for b in range(4):
-        starts = (resets[0, 0] == b) | (resets[0, 1] == b)
-        kept = jnp.where(starts, 0.0, 1.0).astype(F32)
-        for h in range(2):
-            before = state[h] * kept
-            prefix_ref[b * 2 + h] = before
-            step = steps[b, h]
-            added = jnp.concatenate([jnp.zeros((BLOCK, 128), F32), step[:, 128:]], 1)
-            if b == 0:
-                moved = jnp.concatenate([step[:, :128] * kept, zeros], 1)
-            else:
-                moved = dot3(step[:, :128], before)
-            state[h] = before - moved + added
     for h in range(2):
+        first = after_map(maps[0, h], maps[1, h])
+        last = after_map(maps[2, h], maps[3, h])
+        whole = after_map(first, last)
         carry_ref[h] = jnp.concatenate(
-            [state[h][:, :128] - identity, state[h][:, 128:]], 1
+            [whole[:, :128] - identity, whole[:, 128:]], 1
         ).astype(BF16)
+        prefix_ref[h] = jnp.concatenate([identity, zeros], 1) * kept[0]
+        prefix_ref[2 + h] = maps[0, h] * kept[1]
+        prefix_ref[4 + h] = first * kept[2]
+        prefix_ref[6 + h] = after_map(first, maps[2, h]) * kept[3]
 
 
 def response_kernel(q_ref, k_ref, scale_ref, wu_ref, prefix_ref, r_ref, o_ref):
     row, col = square_ids(BLOCK)
     causal = row >= col
-    for b in range(4):
-        for h in range(2):
-            cell = b * 2 + h
-            q = q_ref[b * BLOCK : (b + 1) * BLOCK, h * 128 : (h + 1) * 128]
-            k = k_ref[b * BLOCK : (b + 1) * BLOCK, h * 128 : (h + 1) * 128]
-            qf = q.astype(F32)
-            rq = lax.rsqrt(jnp.sum(qf * qf, axis=1, keepdims=True) + 1e-06)
-            scores = jnp.where(causal, rq * dot_nt(q, k) * scale_ref[cell : cell + 1, :], 0.0)
-            local = dot3(scores, wu_ref[cell])
-            reach = qf * rq - local[:, :128]
-            out = dot3(reach, prefix_ref[cell])
-            r_ref[cell] = out[:, :128].astype(BF16)
-            o_ref[cell] = out[:, 128:] + local[:, 128:]
+    for b, h in CELLS:
+        cell = b * 2 + h
+        q = head_rows(q_ref[b * 2 * BLOCK : (b + 1) * 2 * BLOCK], 2, h)
+        qf = q.astype(F32)
+        rq = lax.rsqrt(jnp.sum(qf * qf, axis=1, keepdims=True) + 1e-06)
+        scores = rq * dot_nt(q, k_ref[cell]) * scale_ref[cell : cell + 1, :]
+        local = dot3(jnp.where(causal, scores, 0.0), wu_ref[cell])
+        reach = qf * rq - local[:, :128]
+        out = dot3(reach, prefix_ref[cell])
+        r_ref[cell] = out[:, :128].astype(BF16)
+        o_ref[cell] = out[:, 128:] + local[:, 128:]
 
 
 def follow(state, element):
@@ -184,14 +203,22 @@
         ).astype(BF16)
 
 
-def output_kernel(far_ref, mid_ref, near_ref, before_ref, r_ref, o_ref, keep_ref, send_ref):
+def pass_kernel(own_ref, peer_ref, out_ref):
+    odd = (lax.axis_index("seq") // 8) % 2 == 1
+    for h in range(2):
+        early = jnp.where(odd, peer_ref[h], own_ref[h])
+        late = jnp.where(odd, own_ref[h], peer_ref[h])
+        out_ref[h] = follow(early[:, 128:].astype(F32), late).astype(BF16)
+
+
+def output_kernel(peer_ref, passed_ref, before_ref, r_ref, o_ref, keep_ref, send_ref):
     head = lax.axis_index("head")
     y, core = head // 2, head % 2
+    odd = (lax.axis_index("seq") // 8) % 2 == 1
     states = []
     for h in range(2):
-        state = far_ref[h][:, 128:].astype(F32)
-        state = follow(state, mid_ref[h])
-        state = follow(state, near_ref[h])
+        state = passed_ref[h].astype(F32)
+        state = jnp.where(odd, follow(state, peer_ref[h]), state)
         before = before_ref[h]
         states.append(state + dot3(before[:, :128], state) + before[:, 128:])
     for b in range(4):
@@ -269,36 +296,32 @@
 
 
 def body(queries, keys, values, beta, reset_blocks, out_weight):
-    k = keys.reshape(512, 256)
+    q = queries.reshape(1024, 128)
+    k = keys.reshape(1024, 128)
     v = values.reshape(512, 512)
 
     across = [(i, i ^ 1) for i in range(8)]
     other_weight = lax.ppermute(out_weight, "head", across)
 
     shaped = jax.ShapeDtypeStruct
-    wu, prefix, scale, carry = call(
+    wu, prefix, scale, rows, carry = call(
         terms_kernel,
         [
             shaped((8, 128, 384), F32),
             shaped((8, 128, 384), F32),
             shaped((8, 128), F32),
+            shaped((8, 128, 128), BF16),
             shaped((2, 128, 384), BF16),
         ],
-        [k, v],
+        [v],
         3_000_000_000,
-        in_hbm=[reset_blocks, beta],
+        in_hbm=[reset_blocks, beta, k],
         scratch=[
             pltpu.SMEM((1, 2), jnp.int32),
             pltpu.VMEM((2, 512), F32),
-            pltpu.SemaphoreType.DMA((2,)),
+            pltpu.VMEM((1024, 128), BF16),
+            pltpu.SemaphoreType.DMA((3,)),
         ],
-    )
-    queries, carry = lax.optimization_barrier((queries, carry))
-    response, own_out = call(
-        response_kernel,
-        [shaped((8, 128, 128), BF16), shaped((8, 128, 256), F32)],
-        [queries.reshape(512, 256), k, scale, wu, prefix],
-        2_000_000_000,
     )
     up = [(i, i - i % 8 + (i + 1) % 8) for i in range(32)]
     down = [(i, i - i % 8 + (i + 7) % 8) for i in range(32)]
@@ -306,10 +329,6 @@
     for step in range(3):
         below.append(lax.ppermute(below[-1], "seq", up))
         above.append(lax.ppermute(above[-1], "seq", down))
-        if step == 0:
-            below[1], above[1], response, own_out = lax.optimization_barrier(
-                (below[1], above[1], response, own_out)
-            )
     opposite = [
         lax.ppermute(below[3][0], "seq", up),
         lax.ppermute(above[3][1], "seq", down),
@@ -320,14 +339,22 @@
         above + opposite + below[:0:-1],
         1_000_000_000,
     )
-    received = [
-        lax.ppermute(total, "seq", [(i, i + 8 * d) for i in range(32) if i + 8 * d < 32])
-        for d in (3, 2, 1)
-    ]
+    peer = lax.ppermute(total, "seq", [(i, i ^ 8) for i in range(32)])
+    response, own_out = call(
+        response_kernel,
+        [shaped((8, 128, 128), BF16), shaped((8, 128, 256), F32)],
+        [q, rows, scale, wu, prefix],
+        2_000_000_000,
+    )
+    peer, response, own_out = lax.optimization_barrier((peer, response, own_out))
+    (joint,) = call(pass_kernel, [shaped((2, 128, 256), BF16)], [total, peer], 100_000_000)
+    passed = lax.ppermute(
+        joint, "seq", [(z + 8 * x, z + 8 * (3 - x)) for x in (0, 1) for z in range(8)]
+    )
     keep, send = call(
         output_kernel,
         [shaped((256, 512), BF16), shaped((256, 512), BF16)],
-        received + [before, response, own_out],
+        [peer, passed, before, response, own_out],
         500_000_000,
     )
     joined = lax.ppermute(send, "head", across)

time: 86.6 us -> 83.4 us (0.963)
  waiting for transfers between devices: 36.2 us -> 33.1 us
  local copies, waits for them, and re-layouts: 2.18 us -> 1.16 us
    ppermute x3, waiting for transfers between devices: 3.42 us -> 14 us  [body(): below.append(lax.ppermute(below[-1], 'seq', up))]
    ppermute x3, waiting for transfers between devices: 9.38 us -> 0.01 us  [body(): above.append(lax.ppermute(above[-1], 'seq', down))]
    ppermute x3, starting transfers between devices: 8.03 us -> 10.5 us  [body(): above.append(lax.ppermute(above[-1], 'seq', down))]
    ppermute x3 -> x2, starting transfers between devices: 5.05 us -> 2.61 us  [the longest x1 1.31 us: body(): peer = lax.ppermute(total, 'seq', [(i, i ^ 8) for i in range(32)])]
    ppermute x1, waiting for transfers between devices: 2.1 us -> 0.01 us  [body(): lax.ppermute(above[3][1], 'seq', down)]
    ppermute x1, waiting for transfers between devices: 3.71 us -> 2.32 us  [body(): lax.ppermute(below[3][0], 'seq', up)]
    unnamed x7 -> x5, local copies, waits for them, and re-layouts: 2.16 us -> 1.13 us
    ppermute x3 -> x2, waiting for transfers between devices: 7.09 us -> 6.42 us  [the longest x1 5.56 us: body(): lax.ppermute(joint, 'seq', [(z + 8 * x, z + 8 * (3 - x)) for x in (0, 1)...]
  transfers between devices with their start and end apart: 21 -> 20, of which waited for: 14 -> 12; matrix products, arithmetic and copies ran while one was open for 3% -> 1% of each run, Pallas kernels for 17% -> 18%
where the time goes in v5:
time: 83.4 us; the launch traced here: 82 us
  waiting for transfers between devices  33.1 us (40%)
  starting transfers between devices  30.9 us (37%)
  Pallas kernels  16.7 us (20%)
  local copies, waits for them, and re-layouts  1.16 us (1%)
    pallas_call x13, Pallas kernels, call(): pl.pallas_call(kernel, out_shape=[jax.ShapeDtypeStruct(a.shape, a.dtype)...  16.7 us
    ppermute x3, waiting for transfers between devices, body(): below.append(lax.ppermute(below[-1], 'seq', up))  14 us
    ppermute x3, starting transfers between devices, body(): above.append(lax.ppermute(above[-1], 'seq', down))  10.5 us
    ppermute x4, starting transfers between devices, body(): received[part] = lax.ppermute(summed, 'head', routes[3 - part])  6.87 us
    ppermute x1, waiting for transfers between devices, body(): lax.ppermute(joint, 'seq', [(z + 8 * x, z + 8 * (3 - x)) for x in (0, 1)...  5.56 us
    ppermute x4, waiting for transfers between devices, body(): received[part] = lax.ppermute(summed, 'head', routes[3 - part])  4.83 us
    ppermute x2, waiting for transfers between devices, body(): sent[part] = lax.ppermute(to_near, 'head', near)  4.03 us
    ppermute x1, starting transfers between devices, body(): lax.ppermute(above[3][1], 'seq', down)  3.47 us
  transfers between devices with their start and end apart: 20, of which 12 were waited for; matrix products, arithmetic and copies ran while one was open for 1% of the time, Pallas kernels for 18%

profile of v5, /device:TPU:4, one launch (start us, length us, event | category | flops | bytes accessed | tf_op | source)
XLA Modules:
  0.0 82.0 jit_solution(3303259199193388758)
XLA Ops:
  0.0 1.1 %copy.7 = bf16[64,8,2,256]{3,1,2,0:T(8,128)(2,1)S(1)} copy(bf16[64,8,2,256]{3,2,1,0:T(2,128)(2,1)} %bitcast.10) | data formatting | bytes 1048576
  1.1 6.3 %shard_map.64 = (f32[8,128,384]{2,1,0:T(8,128)S(1)}, f32[8,128,384]{2,1,0:T(8,128)S(1)}, f32[8,128]{1,0:T(8,128)S(1)}, bf16[8,128,128]{2,1,0:T(8,128)(2,1)S(1)}, bf16[2,128,384]{2,1,0:T(8,128)(2,1)S(1)}) custom-call(s32[1,2]{1,0:T(1,128)} %resets_hbm.1, f32[2,512]{1,0:T(2,128)} %beta_hbm.1, bf16[1024,128]{1,0:T(8,128)(2,1)} %bitcast.11, ...), custom_call_target="tpu_custom_call" | custom-call | flops 3000000000 | bytes 4399112 | tf_op jit(solution)/shard_map/pallas_call | solution.py:244
  7.5 2.0 %collective-permute-start.3 = (bf16[2,128,384]{2,1,0:T(8,128)(2,1)S(1)}, bf16[2,128,384]{2,1,0:T(8,128)(2,1)S(1)}, u32[]{:S(2)}, u32[]{:S(2)}) collective-permute-start(bf16[2,128,384]{2,1,0:T(8,128)(2,1)S(1)} %get-tuple-element.31.refs_0_), channel_id=1, source_target_pairs={{0,8},{8,16},{16,24},{24,32},{32,40},{40,48},{48,56},{56,0},{64,72... | collective-permute-start | bytes 589832 | tf_op jit(solution)/shard_map/ppermute | solution.py:330
  9.5 4.0 %collective-permute-start = (bf16[2,128,384]{2,1,0:T(8,128)(2,1)S(1)}, bf16[2,128,384]{2,1,0:T(8,128)(2,1)S(1)}, u32[]{:S(2)}, u32[]{:S(2)}) collective-permute-start(bf16[2,128,384]{2,1,0:T(8,128)(2,1)S(1)} %get-tuple-element.31.refs_0_), channel_id=1, source_target_pairs={{0,56},{8,0},{16,8},{24,16},{32,24},{40,32},{48,40},{56,48},{64,12... | collective-permute-start | bytes 589832 | tf_op jit(solution)/shard_map/ppermute | solution.py:331
  13.5 5.5 %collective-permute-done.3.refs_8_ = bf16[2,128,384]{2,1,0:T(8,128)(2,1)S(1)} collective-permute-done((bf16[2,128,384]{2,1,0:T(8,128)(2,1)S(1)}, bf16[2,128,384]{2,1,0:T(8,128)(2,1)S(1)}, u32[]{:S(2)}, u32[]{:S(2)}) %collective-permute-start.3) | collective-permute-done | bytes 196640 | tf_op jit(solution)/shard_map/ppermute | solution.py:330
  19.0 3.2 %collective-permute-start.1 = (bf16[2,128,384]{2,1,0:T(8,128)(2,1)S(1)}, bf16[2,128,384]{2,1,0:T(8,128)(2,1)S(1)}, u32[]{:S(2)}, u32[]{:S(2)}) collective-permute-start(bf16[2,128,384]{2,1,0:T(8,128)(2,1)S(1)} %collective-permute-done.refs_1_), channel_id=1, source_target_pairs={{0,56},{8,0},{16,8},{24,16},{32,24},{40,32},{48,40},{56,48},{64,12... | collective-permute-start | bytes 589832 | tf_op jit(solution)/shard_map/ppermute | solution.py:331
  22.2 4.7 %collective-permute-done.4.refs_7_ = bf16[2,128,384]{2,1,0:T(8,128)(2,1)S(1)} collective-permute-done((bf16[2,128,384]{2,1,0:T(8,128)(2,1)S(1)}, bf16[2,128,384]{2,1,0:T(8,128)(2,1)S(1)}, u32[]{:S(2)}, u32[]{:S(2)}) %collective-permute-start.4) | collective-permute-done | bytes 196640 | tf_op jit(solution)/shard_map/ppermute | solution.py:330
  26.9 3.2 %collective-permute-start.2 = (bf16[2,128,384]{2,1,0:T(8,128)(2,1)S(1)}, bf16[2,128,384]{2,1,0:T(8,128)(2,1)S(1)}, u32[]{:S(2)}, u32[]{:S(2)}) collective-permute-start(bf16[2,128,384]{2,1,0:T(8,128)(2,1)S(1)} %collective-permute-done.1.refs_2_), channel_id=1, source_target_pairs={{0,56},{8,0},{16,8},{24,16},{32,24},{40,32},{48,40},{56,48},{64,12... | collective-permute-start | bytes 589832 | tf_op jit(solution)/shard_map/ppermute | solution.py:331
  30.2 3.8 %collective-permute-done.5.refs_6_ = bf16[2,128,384]{2,1,0:T(8,128)(2,1)S(1)} collective-permute-done((bf16[2,128,384]{2,1,0:T(8,128)(2,1)S(1)}, bf16[2,128,384]{2,1,0:T(8,128)(2,1)S(1)}, u32[]{:S(2)}, u32[]{:S(2)}) %collective-permute-start.5) | collective-permute-done | bytes 196640 | tf_op jit(solution)/shard_map/ppermute | solution.py:330
  34.1 3.5 %collective-permute-start.7 = (bf16[128,384]{1,0:T(8,128)(2,1)S(1)}, bf16[128,384]{1,0:T(8,128)(2,1)S(1)}, u32[]{:S(2)}, u32[]{:S(2)}) collective-permute-start(bf16[128,384]{1,0:T(8,128)(2,1)S(1)} %slice_bitcast_fusion), channel_id=1, source_target_pairs={{0,56},{8,0},{16,8},{24,16},{32,24},{40,32},{48,40},{56,48},{64,12... | collective-permute-start | bytes 294920 | tf_op jit(solution)/shard_map/ppermute | solution.py:334
  37.6 2.3 %collective-permute-done.6.refs_4_ = bf16[128,384]{1,0:T(8,128)(2,1)S(1)} collective-permute-done((bf16[128,384]{1,0:T(8,128)(2,1)S(1)}, bf16[128,384]{1,0:T(8,128)(2,1)S(1)}, u32[]{:S(2)}, u32[]{:S(2)}) %collective-permute-start.6) | collective-permute-done | bytes 98336 | tf_op jit(solution)/shard_map/ppermute | solution.py:333
  39.9 1.9 %shard_map.65 = (f32[2,128,384]{2,1,0:T(8,128)S(1)}, bf16[2,128,384]{2,1,0:T(8,128)(2,1)S(1)}) custom-call(bf16[2,128,384]{2,1,0:T(8,128)(2,1)S(1)} %get-tuple-element.31.refs_0_, bf16[2,128,384]{2,1,0:T(8,128)(2,1)S(1)} %collective-permute-done.refs_1_, bf16[2,128,384]{2,1,0:T(8,128)(2,1)S(1)} %collective-permute-done.1.refs_2_, ...), custom_call_target="tpu_custom_call" | custom-call | flops 1000000000 | bytes 2162688 | tf_op jit(solution)/shard_map/pallas_call | solution.py:244
  41.8 1.3 %collective-permute-start.8 = (bf16[2,128,384]{2,1,0:T(8,128)(2,1)S(1)}, bf16[2,128,384]{2,1,0:T(8,128)(2,1)S(1)}, u32[]{:S(2)}, u32[]{:S(2)}) collective-permute-start(bf16[2,128,384]{2,1,0:T(8,128)(2,1)S(1)} %get-tuple-element.32.own_ref), channel_id=1, source_target_pairs={{0,64},{8,72},{16,80},{24,88},{32,96},{40,104},{48,112},{56,120},{... | collective-permute-start | bytes 589832 | tf_op jit(solution)/shard_map/ppermute | solution.py:342
  43.1 3.6 %shard_map.66 = (bf16[8,128,128]{2,1,0:T(8,128)(2,1)S(1)}, f32[8,128,256]{2,1,0:T(8,128)S(1)}) custom-call(bf16[1024,128]{1,0:T(8,128)(2,1)S(1)} %bitcast.9, bf16[8,128,128]{2,1,0:T(8,128)(2,1)S(1)} %get-tuple-element.33.k_ref, f32[8,128]{1,0:T(8,128)S(1)} %get-tuple-element.34.scale_ref, f32[8,128,384]{2,1,0:T(8,128)S(1)} %get-tuple-element.35.wu_ref, ...), custom_call_target="tpu_custom_call" | custom-call | flops 2000000000 | bytes 4984832 | tf_op jit(solution)/shard_map/pallas_call | solution.py:244
  46.7 0.9 %collective-permute-done.8.peer_ref = bf16[2,128,384]{2,1,0:T(8,128)(2,1)S(1)} collective-permute-done((bf16[2,128,384]{2,1,0:T(8,128)(2,1)S(1)}, bf16[2,128,384]{2,1,0:T(8,128)(2,1)S(1)}, u32[]{:S(2)}, u32[]{:S(2)}) %collective-permute-start.8) | collective-permute-done | bytes 196640 | tf_op jit(solution)/shard_map/ppermute | solution.py:342
  47.8 1.3 %collective-permute-start.9 = (bf16[2,128,256]{2,1,0:T(8,128)(2,1)S(1)}, bf16[2,128,256]{2,1,0:T(8,128)(2,1)S(1)}, u32[]{:S(2)}, u32[]{:S(2)}) collective-permute-start(bf16[2,128,256]{2,1,0:T(8,128)(2,1)S(1)} %shard_map.67), channel_id=1, source_target_pairs={{0,192},{8,200},{16,208},{24,216},{32,224},{40,232},{48,240},{56,2... | collective-permute-start | bytes 393224 | tf_op jit(solution)/shard_map/ppermute | solution.py:351
  49.1 5.6 %collective-permute-done.9.passed_ref = bf16[2,128,256]{2,1,0:T(8,128)(2,1)S(1)} collective-permute-done((bf16[2,128,256]{2,1,0:T(8,128)(2,1)S(1)}, bf16[2,128,256]{2,1,0:T(8,128)(2,1)S(1)}, u32[]{:S(2)}, u32[]{:S(2)}) %collective-permute-start.9) | collective-permute-done | bytes 131104 | tf_op jit(solution)/shard_map/ppermute | solution.py:351
  54.7 0.8 %shard_map.68 = (bf16[256,512]{1,0:T(8,128)(2,1)S(1)}, bf16[256,512]{1,0:T(8,128)(2,1)S(1)}) custom-call(bf16[2,128,384]{2,1,0:T(8,128)(2,1)S(1)} %collective-permute-done.8.peer_ref, bf16[2,128,256]{2,1,0:T(8,128)(2,1)S(1)} %collective-permute-done.9.passed_ref, f32[2,128,384]{2,1,0:T(8,128)S(1)} %get-tuple-element.40.before_ref, ...), custom_call_target="tpu_custom_call" | custom-call | flops 500000000 | bytes 2555904 | tf_op jit(solution)/shard_map/pallas_call | solution.py:244
  55.6 1.5 %collective-permute-done.10.joined_ref = bf16[256,512]{1,0:T(8,128)(2,1)S(1)} collective-permute-done((bf16[256,512]{1,0:T(8,128)(2,1)S(1)}, bf16[256,512]{1,0:T(8,128)(2,1)S(1)}, u32[]{:S(2)}, u32[]{:S(2)}) %collective-permute-start.10) | collective-permute-done | bytes 262176 | tf_op jit(solution)/shard_map/ppermute | solution.py:360
  57.2 0.7 shard_map.69
  57.9 1.7 %collective-permute-start.12 = (bf16[128,1024]{1,0:T(8,128)(2,1)S(1)}, bf16[128,1024]{1,0:T(8,128)(2,1)S(1)}, u32[]{:S(2)}, u32[]{:S(2)}) collective-permute-start(bf16[128,1024]{1,0:T(8,128)(2,1)S(1)} %get-tuple-element.52), channel_id=1, source_target_pairs={{0,2},{1,3},{2,0},{3,1},{4,6},{5,7},{6,4},{7,5},{8,10},{9,11},{10,... | collective-permute-start | bytes 786440 | tf_op jit(solution)/shard_map/ppermute | solution.py:372
  59.6 2.2 %collective-permute-start.14 = (bf16[128,1024]{1,0:T(8,128)(2,1)S(1)}, bf16[128,1024]{1,0:T(8,128)(2,1)S(1)}, u32[]{:S(2)}, u32[]{:S(2)}) collective-permute-start(bf16[128,1024]{1,0:T(8,128)(2,1)S(1)} %get-tuple-element.54), channel_id=1, source_target_pairs={{0,6},{1,7},{2,4},{3,5},{4,2},{5,3},{6,0},{7,1},{8,14},{9,15},{10,... | collective-permute-start | bytes 786440 | tf_op jit(solution)/shard_map/ppermute | solution.py:373
  62.5 0.8 collective-permute-start.13
  63.9 1.3 %shard_map.71 = (bf16[64,4096]{1,0:T(8,128)(2,1)S(1)}, bf16[64,4096]{1,0:T(8,128)(2,1)S(1)}) custom-call(bf16[256,512]{1,0:T(8,128)(2,1)S(1)} %get-tuple-element.50.keep_ref, bf16[256,512]{1,0:T(8,128)(2,1)S(1)} %collective-permute-done.10.joined_ref, bf16[512,4096]{1,0:T(8,128)(2,1)S(1)} %copy-done, bf16[512,4096]{1,0:T(8,128)(2,1)S(1)} %collective-permute-done.11.other_w_ref), custom_call_target="tpu_custom_call" | custom-call | flops 1000000000 | bytes 9961472 | tf_op jit(solution)/shard_map/pallas_call | solution.py:244
  65.1 2.0 %collective-permute-done.12.sent_ref.refs_1_ = bf16[128,1024]{1,0:T(8,128)(2,1)S(1)} collective-permute-done((bf16[128,1024]{1,0:T(8,128)(2,1)S(1)}, bf16[128,1024]{1,0:T(8,128)(2,1)S(1)}, u32[]{:S(2)}, u32[]{:S(2)}) %collective-permute-start.12) | collective-permute-done | bytes 262176 | tf_op jit(solution)/shard_map/ppermute | solution.py:372
  67.2 3.1 %collective-permute-start.16 = (bf16[64,1024]{1,0:T(8,128)(2,1)S(1)}, bf16[64,1024]{1,0:T(8,128)(2,1)S(1)}, u32[]{:S(2)}, u32[]{:S(2)}) collective-permute-start(bf16[64,1024]{1,0:T(8,128)(2,1)S(1)} %shard_map.72), channel_id=1, source_target_pairs={{0,6},{1,7},{2,4},{3,5},{4,2},{5,3},{6,0},{7,1},{8,14},{9,15},{10,... | collective-permute-start | bytes 393224 | tf_op jit(solution)/shard_map/ppermute | solution.py:385
  70.6 2.0 %collective-permute-done.13.sent_ref.refs_2_ = bf16[128,1024]{1,0:T(8,128)(2,1)S(1)} collective-permute-done((bf16[128,1024]{1,0:T(8,128)(2,1)S(1)}, bf16[128,1024]{1,0:T(8,128)(2,1)S(1)}, u32[]{:S(2)}, u32[]{:S(2)}) %collective-permute-start.13) | collective-permute-done | bytes 262176 | tf_op jit(solution)/shard_map/ppermute | solution.py:372
  72.6 3.3 %collective-permute-start.17 = (bf16[64,1024]{1,0:T(8,128)(2,1)S(1)}, bf16[64,1024]{1,0:T(8,128)(2,1)S(1)}, u32[]{:S(2)}, u32[]{:S(2)}) collective-permute-start(bf16[64,1024]{1,0:T(8,128)(2,1)S(1)} %shard_map.73), channel_id=1, source_target_pairs={{0,6},{1,7},{2,4},{3,5},{4,2},{5,3},{6,0},{7,1},{8,14},{9,15},{10,... | collective-permute-start | bytes 393224 | tf_op jit(solution)/shard_map/ppermute | solution.py:385
  76.2 2.2 %collective-permute-done.16.refs_5_ = bf16[64,1024]{1,0:T(8,128)(2,1)S(1)} collective-permute-done((bf16[64,1024]{1,0:T(8,128)(2,1)S(1)}, bf16[64,1024]{1,0:T(8,128)(2,1)S(1)}, u32[]{:S(2)}, u32[]{:S(2)}) %collective-permute-start.16) | collective-permute-done | bytes 131104 | tf_op jit(solution)/shard_map/ppermute | solution.py:385
  78.4 1.7 %collective-permute-done.17.refs_6_ = bf16[64,1024]{1,0:T(8,128)(2,1)S(1)} collective-permute-done((bf16[64,1024]{1,0:T(8,128)(2,1)S(1)}, bf16[64,1024]{1,0:T(8,128)(2,1)S(1)}, u32[]{:S(2)}, u32[]{:S(2)}) %collective-permute-start.17) | collective-permute-done | bytes 131104 | tf_op jit(solution)/shard_map/ppermute | solution.py:385
  80.1 0.9 %collective-permute-done.19.refs_8_ = bf16[64,1024]{1,0:T(8,128)(2,1)S(1)} collective-permute-done((bf16[64,1024]{1,0:T(8,128)(2,1)S(1)}, bf16[64,1024]{1,0:T(8,128)(2,1)S(1)}, u32[]{:S(2)}, u32[]{:S(2)}) %collective-permute-start.19) | collective-permute-done | bytes 131104 | tf_op jit(solution)/shard_map/ppermute | solution.py:385
  81.0 1.0 %shard_map.76 = bf16[64,4096]{1,0:T(8,128)(2,1)} custom-call(bf16[64,4096]{1,0:T(8,128)(2,1)S(1)} %get-tuple-element.51.refs_0_, bf16[128,1024]{1,0:T(8,128)(2,1)S(1)} %collective-permute-done.12.sent_ref.refs_1_, bf16[128,1024]{1,0:T(8,128)(2,1)S(1)} %collective-permute-done.13.sent_ref.refs_2_, ...), custom_call_target="tpu_custom_call" | custom-call | flops 1000000 | bytes 2621440 | tf_op jit(solution)/shard_map/pallas_call | solution.py:244
  (28 shorter events, 2.4 us)
Async XLA Ops:
  0.0 57.2 %collective-permute-start.11 = (bf16[512,4096]{1,0:T(8,128)(2,1)}, bf16[512,4096]{1,0:T(8,128)(2,1)S(1)}, u32[]{:S(2)}, u32[]{:S(2)}) collective-permute-start(bf16[512,4096]{1,0:T(8,128)(2,1)} %own_w_ref.5), channel_id=1, source_target_pairs={{0,1},{1,0},{2,3},{3,2},{4,5},{5,4},{6,7},{7,6},{8,9},{9,8},{10,11... | collective-permute-start | bytes 12582920 | tf_op jit(solution)/shard_map/ppermute | solution.py:304
  1.1 42.0 %copy-start.1 = (bf16[512,2,128]{2,1,0:T(2,128)(2,1)S(1)}, bf16[512,2,128]{2,1,0:T(2,128)(2,1)}, u32[]{:S(2)}) copy-start(bf16[512,2,128]{2,1,0:T(2,128)(2,1)} %param.6) | copy-start | bytes 786436
  7.5 11.5 %collective-permute-start.3 = (bf16[2,128,384]{2,1,0:T(8,128)(2,1)S(1)}, bf16[2,128,384]{2,1,0:T(8,128)(2,1)S(1)}, u32[]{:S(2)}, u32[]{:S(2)}) collective-permute-start(bf16[2,128,384]{2,1,0:T(8,128)(2,1)S(1)} %get-tuple-element.31.refs_0_), channel_id=1, source_target_pairs={{0,8},{8,16},{16,24},{24,32},{32,40},{40,48},{48,56},{56,0},{64,72... | collective-permute-start | bytes 589832 | tf_op jit(solution)/shard_map/ppermute | solution.py:330
  9.5 9.5 %collective-permute-start = (bf16[2,128,384]{2,1,0:T(8,128)(2,1)S(1)}, bf16[2,128,384]{2,1,0:T(8,128)(2,1)S(1)}, u32[]{:S(2)}, u32[]{:S(2)}) collective-permute-start(bf16[2,128,384]{2,1,0:T(8,128)(2,1)S(1)} %get-tuple-element.31.refs_0_), channel_id=1, source_target_pairs={{0,56},{8,0},{16,8},{24,16},{32,24},{40,32},{48,40},{56,48},{64,12... | collective-permute-start | bytes 589832 | tf_op jit(solution)/shard_map/ppermute | solution.py:331
  19.0 7.9 %collective-permute-start.4 = (bf16[2,128,384]{2,1,0:T(8,128)(2,1)S(1)}, bf16[2,128,384]{2,1,0:T(8,128)(2,1)S(1)}, u32[]{:S(2)}, u32[]{:S(2)}) collective-permute-start(bf16[2,128,384]{2,1,0:T(8,128)(2,1)S(1)} %collective-permute-done.3.refs_8_), channel_id=1, source_target_pairs={{0,8},{8,16},{16,24},{24,32},{32,40},{40,48},{48,56},{56,0},{64,72... | collective-permute-start | bytes 589832 | tf_op jit(solution)/shard_map/ppermute | solution.py:330
  19.0 7.9 %collective-permute-start.1 = (bf16[2,128,384]{2,1,0:T(8,128)(2,1)S(1)}, bf16[2,128,384]{2,1,0:T(8,128)(2,1)S(1)}, u32[]{:S(2)}, u32[]{:S(2)}) collective-permute-start(bf16[2,128,384]{2,1,0:T(8,128)(2,1)S(1)} %collective-permute-done.refs_1_), channel_id=1, source_target_pairs={{0,56},{8,0},{16,8},{24,16},{32,24},{40,32},{48,40},{56,48},{64,12... | collective-permute-start | bytes 589832 | tf_op jit(solution)/shard_map/ppermute | solution.py:331
  26.9 7.1 %collective-permute-start.5 = (bf16[2,128,384]{2,1,0:T(8,128)(2,1)S(1)}, bf16[2,128,384]{2,1,0:T(8,128)(2,1)S(1)}, u32[]{:S(2)}, u32[]{:S(2)}) collective-permute-start(bf16[2,128,384]{2,1,0:T(8,128)(2,1)S(1)} %collective-permute-done.4.refs_7_), channel_id=1, source_target_pairs={{0,8},{8,16},{16,24},{24,32},{32,40},{40,48},{48,56},{56,0},{64,72... | collective-permute-start | bytes 589832 | tf_op jit(solution)/shard_map/ppermute | solution.py:330
  26.9 7.2 %collective-permute-start.2 = (bf16[2,128,384]{2,1,0:T(8,128)(2,1)S(1)}, bf16[2,128,384]{2,1,0:T(8,128)(2,1)S(1)}, u32[]{:S(2)}, u32[]{:S(2)}) collective-permute-start(bf16[2,128,384]{2,1,0:T(8,128)(2,1)S(1)} %collective-permute-done.1.refs_2_), channel_id=1, source_target_pairs={{0,56},{8,0},{16,8},{24,16},{32,24},{40,32},{48,40},{56,48},{64,12... | collective-permute-start | bytes 589832 | tf_op jit(solution)/shard_map/ppermute | solution.py:331
  34.0 5.9 %collective-permute-start.6 = (bf16[128,384]{1,0:T(8,128)(2,1)S(1)}, bf16[128,384]{1,0:T(8,128)(2,1)S(1)}, u32[]{:S(2)}, u32[]{:S(2)}) collective-permute-start(bf16[128,384]{1,0:T(8,128)(2,1)S(1)} %slice_bitcast_fusion.1), channel_id=1, source_target_pairs={{0,8},{8,16},{16,24},{24,32},{32,40},{40,48},{48,56},{56,0},{64,72... | collective-permute-start | bytes 294920 | tf_op jit(solution)/shard_map/ppermute | solution.py:333
  34.1 5.8 %collective-permute-start.7 = (bf16[128,384]{1,0:T(8,128)(2,1)S(1)}, bf16[128,384]{1,0:T(8,128)(2,1)S(1)}, u32[]{:S(2)}, u32[]{:S(2)}) collective-permute-start(bf16[128,384]{1,0:T(8,128)(2,1)S(1)} %slice_bitcast_fusion), channel_id=1, source_target_pairs={{0,56},{8,0},{16,8},{24,16},{32,24},{40,32},{48,40},{56,48},{64,12... | collective-permute-start | bytes 294920 | tf_op jit(solution)/shard_map/ppermute | solution.py:334
  41.8 5.8 %collective-permute-start.8 = (bf16[2,128,384]{2,1,0:T(8,128)(2,1)S(1)}, bf16[2,128,384]{2,1,0:T(8,128)(2,1)S(1)}, u32[]{:S(2)}, u32[]{:S(2)}) collective-permute-start(bf16[2,128,384]{2,1,0:T(8,128)(2,1)S(1)} %get-tuple-element.32.own_ref), channel_id=1, source_target_pairs={{0,64},{8,72},{16,80},{24,88},{32,96},{40,104},{48,112},{56,120},{... | collective-permute-start | bytes 589832 | tf_op jit(solution)/shard_map/ppermute | solution.py:342
  43.1 14.0 %copy-start = (bf16[512,4096]{1,0:T(8,128)(2,1)S(1)}, bf16[512,4096]{1,0:T(8,128)(2,1)}, u32[]{:S(2)}) copy-start(bf16[512,4096]{1,0:T(8,128)(2,1)} %own_w_ref.5) | copy-start | bytes 12582916
  47.8 6.9 %collective-permute-start.9 = (bf16[2,128,256]{2,1,0:T(8,128)(2,1)S(1)}, bf16[2,128,256]{2,1,0:T(8,128)(2,1)S(1)}, u32[]{:S(2)}, u32[]{:S(2)}) collective-permute-start(bf16[2,128,256]{2,1,0:T(8,128)(2,1)S(1)} %shard_map.67), channel_id=1, source_target_pairs={{0,192},{8,200},{16,208},{24,216},{32,224},{40,232},{48,240},{56,2... | collective-permute-start | bytes 393224 | tf_op jit(solution)/shard_map/ppermute | solution.py:351
  55.5 1.6 %collective-permute-start.10 = (bf16[256,512]{1,0:T(8,128)(2,1)S(1)}, bf16[256,512]{1,0:T(8,128)(2,1)S(1)}, u32[]{:S(2)}, u32[]{:S(2)}) collective-permute-start(bf16[256,512]{1,0:T(8,128)(2,1)S(1)} %get-tuple-element.44), channel_id=1, source_target_pairs={{0,1},{1,0},{2,3},{3,2},{4,5},{5,4},{6,7},{7,6},{8,9},{9,8},{10,11... | collective-permute-start | bytes 786440 | tf_op jit(solution)/shard_map/ppermute | solution.py:360
  57.9 9.2 %collective-permute-start.12 = (bf16[128,1024]{1,0:T(8,128)(2,1)S(1)}, bf16[128,1024]{1,0:T(8,128)(2,1)S(1)}, u32[]{:S(2)}, u32[]{:S(2)}) collective-permute-start(bf16[128,1024]{1,0:T(8,128)(2,1)S(1)} %get-tuple-element.52), channel_id=1, source_target_pairs={{0,2},{1,3},{2,0},{3,1},{4,6},{5,7},{6,4},{7,5},{8,10},{9,11},{10,... | collective-permute-start | bytes 786440 | tf_op jit(solution)/shard_map/ppermute | solution.py:372
  59.6 10.7 %collective-permute-start.14 = (bf16[128,1024]{1,0:T(8,128)(2,1)S(1)}, bf16[128,1024]{1,0:T(8,128)(2,1)S(1)}, u32[]{:S(2)}, u32[]{:S(2)}) collective-permute-start(bf16[128,1024]{1,0:T(8,128)(2,1)S(1)} %get-tuple-element.54), channel_id=1, source_target_pairs={{0,6},{1,7},{2,4},{3,5},{4,2},{5,3},{6,0},{7,1},{8,14},{9,15},{10,... | collective-permute-start | bytes 786440 | tf_op jit(solution)/shard_map/ppermute | solution.py:373
  62.5 10.1 %collective-permute-start.13 = (bf16[128,1024]{1,0:T(8,128)(2,1)S(1)}, bf16[128,1024]{1,0:T(8,128)(2,1)S(1)}, u32[]{:S(2)}, u32[]{:S(2)}) collective-permute-start(bf16[128,1024]{1,0:T(8,128)(2,1)S(1)} %get-tuple-element.53), channel_id=1, source_target_pairs={{0,2},{1,3},{2,0},{3,1},{4,6},{5,7},{6,4},{7,5},{8,10},{9,11},{10,... | collective-permute-start | bytes 786440 | tf_op jit(solution)/shard_map/ppermute | solution.py:372
  63.3 12.7 %collective-permute-start.15 = (bf16[128,1024]{1,0:T(8,128)(2,1)S(1)}, bf16[128,1024]{1,0:T(8,128)(2,1)S(1)}, u32[]{:S(2)}, u32[]{:S(2)}) collective-permute-start(bf16[128,1024]{1,0:T(8,128)(2,1)S(1)} %get-tuple-element.55), channel_id=1, source_target_pairs={{0,6},{1,7},{2,4},{3,5},{4,2},{5,3},{6,0},{7,1},{8,14},{9,15},{10,... | collective-permute-start | bytes 786440 | tf_op jit(solution)/shard_map/ppermute | solution.py:373
  67.2 11.2 %collective-permute-start.16 = (bf16[64,1024]{1,0:T(8,128)(2,1)S(1)}, bf16[64,1024]{1,0:T(8,128)(2,1)S(1)}, u32[]{:S(2)}, u32[]{:S(2)}) collective-permute-start(bf16[64,1024]{1,0:T(8,128)(2,1)S(1)} %shard_map.72), channel_id=1, source_target_pairs={{0,6},{1,7},{2,4},{3,5},{4,2},{5,3},{6,0},{7,1},{8,14},{9,15},{10,... | collective-permute-start | bytes 393224 | tf_op jit(solution)/shard_map/ppermute | solution.py:385
  70.3 8.1 %collective-permute-start.18 = (bf16[64,1024]{1,0:T(8,128)(2,1)S(1)}, bf16[64,1024]{1,0:T(8,128)(2,1)S(1)}, u32[]{:S(2)}, u32[]{:S(2)}) collective-permute-start(bf16[64,1024]{1,0:T(8,128)(2,1)S(1)} %shard_map.74), channel_id=1, source_target_pairs={{0,2},{1,3},{2,0},{3,1},{4,6},{5,7},{6,4},{7,5},{8,10},{9,11},{10,... | collective-permute-start | bytes 393224 | tf_op jit(solution)/shard_map/ppermute | solution.py:385
  72.6 7.5 %collective-permute-start.17 = (bf16[64,1024]{1,0:T(8,128)(2,1)S(1)}, bf16[64,1024]{1,0:T(8,128)(2,1)S(1)}, u32[]{:S(2)}, u32[]{:S(2)}) collective-permute-start(bf16[64,1024]{1,0:T(8,128)(2,1)S(1)} %shard_map.73), channel_id=1, source_target_pairs={{0,6},{1,7},{2,4},{3,5},{4,2},{5,3},{6,0},{7,1},{8,14},{9,15},{10,... | collective-permute-start | bytes 393224 | tf_op jit(solution)/shard_map/ppermute | solution.py:385
  76.0 5.1 %collective-permute-start.19 = (bf16[64,1024]{1,0:T(8,128)(2,1)S(1)}, bf16[64,1024]{1,0:T(8,128)(2,1)S(1)}, u32[]{:S(2)}, u32[]{:S(2)}) collective-permute-start(bf16[64,1024]{1,0:T(8,128)(2,1)S(1)} %shard_map.75), channel_id=1, source_target_pairs={{0,2},{1,3},{2,0},{3,1},{4,6},{5,7},{6,4},{7,5},{8,10},{9,11},{10,... | collective-permute-start | bytes 393224 | tf_op jit(solution)/shard_map/ppermute | solution.py:385

commit v6 on v5

--- a/solution.py
+++ b/solution.py
@@ -175,31 +175,46 @@
     return state + moved + added
 
 
-def group_kernel(*refs):
-    refs, (before_ref, total_ref) = refs[:9], refs[9:]
-    elements = [(ref.at[0], ref.at[1]) for ref in refs[:4] + refs[6:]]
-    elements.insert(4, refs[4:6])
+def whole_map(element, identity):
+    element = element.astype(F32)
+    return jnp.concatenate([element[:, :128] + identity, element[:, 128:]], 1)
+
+
+def pair_map_kernel(own_ref, peer_ref, out_ref):
+    row, col = square_ids(BLOCK)
+    identity = jnp.where(row == col, 1.0, 0.0).astype(F32)
+    upper = lax.axis_index("seq") % 2 == 1
+    for h in range(2):
+        early = jnp.where(upper, peer_ref[h], own_ref[h])
+        late = jnp.where(upper, own_ref[h], peer_ref[h])
+        both = follow(whole_map(early, identity), late)
+        out_ref[h] = jnp.concatenate([both[:, :128] - identity, both[:, 128:]], 1).astype(BF16)
+
+
+def group_kernel(peer_ref, pair_ref, first_ref, second_ref, far_ref, before_ref, total_ref):
     row, col = square_ids(BLOCK)
     identity = jnp.where(row == col, 1.0, 0.0).astype(F32)
     empty = jnp.concatenate([identity, jnp.zeros((BLOCK, 256), F32)], 1)
     z = lax.axis_index("seq") % 8
-    state = {h: empty for h in range(2)}
-    after = {h: empty for h in range(2)}
-    for step in range(1, 8):
-        wraps = z + step == 8
-        for h in range(2):
+    place, upper = z // 2, z % 2 == 1
+    for h in range(2):
+        below = jnp.where(upper, second_ref[h], first_ref[h])
+        above = jnp.where(upper, first_ref[h], second_ref[h])
+        state = after = empty
+        for step, element in ((1, above), (2, far_ref[h]), (3, below)):
+            wraps = place + step == 4
             if step > 1:
-                after[h] = jnp.where(wraps, state[h], after[h])
-                state[h] = jnp.where(wraps, empty, state[h])
-            state[h] = follow(state[h], elements[step][h][...])
-    for h in range(2):
-        after[h] = jnp.where(z == 0, state[h], after[h])
-        state[h] = jnp.where(z == 0, empty, state[h])
-        before_ref[h] = jnp.concatenate([state[h][:, :128] - identity, state[h][:, 128:]], 1)
-        through = follow(state[h], elements[0][h][...])
-        total = dot3(after[h][:, :128], through)
+                after = jnp.where(wraps, state, after)
+                state = jnp.where(wraps, empty, state)
+            state = follow(state, element)
+        after = jnp.where(place == 0, state, after)
+        state = jnp.where(place == 0, empty, state)
+        before = jnp.where(upper, follow(state, peer_ref[h]), state)
+        before_ref[h] = jnp.concatenate([before[:, :128] - identity, before[:, 128:]], 1)
+        through = follow(state, pair_ref[h])
+        total = dot3(after[:, :128], through)
         total_ref[h] = jnp.concatenate(
-            [total[:, :128] - identity, total[:, 128:] + after[h][:, 128:]], 1
+            [total[:, :128] - identity, total[:, 128:] + after[:, 128:]], 1
         ).astype(BF16)
 
 
@@ -323,21 +338,20 @@
             pltpu.SemaphoreType.DMA((3,)),
         ],
     )
-    up = [(i, i - i % 8 + (i + 1) % 8) for i in range(32)]
-    down = [(i, i - i % 8 + (i + 7) % 8) for i in range(32)]
-    below, above = [carry], [carry]
-    for step in range(3):
-        below.append(lax.ppermute(below[-1], "seq", up))
-        above.append(lax.ppermute(above[-1], "seq", down))
-    opposite = [
-        lax.ppermute(below[3][0], "seq", up),
-        lax.ppermute(above[3][1], "seq", down),
-    ]
+    inside = [(i, i ^ 1) for i in range(32)]
+    outward = [(i, i - i % 8 + (i % 8 + (1 if i % 2 else 7)) % 8) for i in range(32)]
+    neighbour = lax.ppermute(carry, "seq", inside)
+    (pair,) = call(
+        pair_map_kernel, [shaped((2, 128, 384), BF16)], [carry, neighbour], 100_000_000
+    )
+    first = lax.ppermute(pair, "seq", outward)
+    second = lax.ppermute(first, "seq", inside)
+    farthest = lax.ppermute(second, "seq", outward)
     before, total = call(
         group_kernel,
         [shaped((2, 128, 384), F32), shaped((2, 128, 384), BF16)],
-        above + opposite + below[:0:-1],
-        1_000_000_000,
+        [neighbour, pair, first, second, farthest],
+        600_000_000,
     )
     peer = lax.ppermute(total, "seq", [(i, i ^ 8) for i in range(32)])
     response, own_out = call(

time: 83.4 us -> 82 us (0.983)
  starting transfers between devices: 30.9 us -> 25.5 us
  waiting for transfers between devices: 33.1 us -> 37.1 us
    ppermute x8 -> x4, starting transfers between devices: 16.1 us -> 10.4 us  [the longest x1 5.77 us: body(): first = lax.ppermute(pair, 'seq', outward)]
    ppermute x8 -> x4, waiting for transfers between devices: 16.3 us -> 20.5 us  [the longest x1 5.95 us: body(): second = lax.ppermute(first, 'seq', inside)]
    pallas_call x13 -> x14, Pallas kernels: 16.7 us -> 16.8 us  [call(): pl.pallas_call(kernel, out_shape=[jax.ShapeDtypeStruct(a.shape, a.dtype)...]
  transfers between devices with their start and end apart: 20 -> 16, of which waited for: 12 -> 12; matrix products, arithmetic and copies ran while one was open for 1% -> 1% of each run, Pallas kernels for 18% -> 19%
where the time goes in v6:
time: 82 us; the launch traced here: 80.6 us
  waiting for transfers between devices  37.1 us (45%)
  starting transfers between devices  25.5 us (31%)
  Pallas kernels  16.8 us (20%)
  local copies, waits for them, and re-layouts  1.13 us (1%)
    pallas_call x14, Pallas kernels, call(): pl.pallas_call(kernel, out_shape=[jax.ShapeDtypeStruct(a.shape, a.dtype)...  16.8 us
    ppermute x4, starting transfers between devices, body(): received[part] = lax.ppermute(summed, 'head', routes[3 - part])  6.88 us
    ppermute x1, waiting for transfers between devices, body(): second = lax.ppermute(first, 'seq', inside)  5.95 us
    ppermute x1, starting transfers between devices, body(): first = lax.ppermute(pair, 'seq', outward)  5.77 us
    ppermute x1, waiting for transfers between devices, body(): neighbour = lax.ppermute(carry, 'seq', inside)  5.57 us
    ppermute x1, waiting for transfers between devices, body(): lax.ppermute(joint, 'seq', [(z + 8 * x, z + 8 * (3 - x)) for x in (0, 1)...  5.38 us
    ppermute x4, waiting for transfers between devices, body(): received[part] = lax.ppermute(summed, 'head', routes[3 - part])  4.83 us
    ppermute x1, waiting for transfers between devices, body(): first = lax.ppermute(pair, 'seq', outward)  4.79 us
  transfers between devices with their start and end apart: 16, of which 12 were waited for; matrix products, arithmetic and copies ran while one was open for 1% of the time, Pallas kernels for 19%

profile of v6, /device:TPU:4, one launch (start us, length us, event | category | flops | bytes accessed | tf_op | source)
XLA Modules:
  0.0 80.6 jit_solution(327390701894279276)
XLA Ops:
  0.0 1.1 %copy.7 = bf16[64,8,2,256]{3,1,2,0:T(8,128)(2,1)S(1)} copy(bf16[64,8,2,256]{3,2,1,0:T(2,128)(2,1)} %bitcast.6) | data formatting | bytes 1048576
  1.1 6.3 %shard_map.64 = (f32[8,128,384]{2,1,0:T(8,128)S(1)}, f32[8,128,384]{2,1,0:T(8,128)S(1)}, f32[8,128]{1,0:T(8,128)S(1)}, bf16[8,128,128]{2,1,0:T(8,128)(2,1)S(1)}, bf16[2,128,384]{2,1,0:T(8,128)(2,1)S(1)}) custom-call(s32[1,2]{1,0:T(1,128)} %resets_hbm.1, f32[2,512]{1,0:T(2,128)} %beta_hbm.1, bf16[1024,128]{1,0:T(8,128)(2,1)} %bitcast.7, ...), custom_call_target="tpu_custom_call" | custom-call | flops 3000000000 | bytes 4399112 | tf_op jit(solution)/shard_map/pallas_call | solution.py:259
  7.5 2.0 %collective-permute-start = (bf16[2,128,384]{2,1,0:T(8,128)(2,1)S(1)}, bf16[2,128,384]{2,1,0:T(8,128)(2,1)S(1)}, u32[]{:S(2)}, u32[]{:S(2)}) collective-permute-start(bf16[2,128,384]{2,1,0:T(8,128)(2,1)S(1)} %get-tuple-element.31.own_ref), channel_id=1, source_target_pairs={{0,8},{8,0},{16,24},{24,16},{32,40},{40,32},{48,56},{56,48},{64,72... | collective-permute-start | bytes 589832 | tf_op jit(solution)/shard_map/ppermute | solution.py:343
  9.5 5.6 %collective-permute-done.peer_ref = bf16[2,128,384]{2,1,0:T(8,128)(2,1)S(1)} collective-permute-done((bf16[2,128,384]{2,1,0:T(8,128)(2,1)S(1)}, bf16[2,128,384]{2,1,0:T(8,128)(2,1)S(1)}, u32[]{:S(2)}, u32[]{:S(2)}) %collective-permute-start) | collective-permute-done | bytes 196640 | tf_op jit(solution)/shard_map/ppermute | solution.py:343
  15.3 5.8 %collective-permute-start.1 = (bf16[2,128,384]{2,1,0:T(8,128)(2,1)S(1)}, bf16[2,128,384]{2,1,0:T(8,128)(2,1)S(1)}, u32[]{:S(2)}, u32[]{:S(2)}) collective-permute-start(bf16[2,128,384]{2,1,0:T(8,128)(2,1)S(1)} %shard_map.65.pair_ref), channel_id=1, source_target_pairs={{0,56},{8,16},{16,8},{24,32},{32,24},{40,48},{48,40},{56,0},{64,12... | collective-permute-start | bytes 589832 | tf_op jit(solution)/shard_map/ppermute | solution.py:347
  21.1 4.8 %collective-permute-done.1.first_ref = bf16[2,128,384]{2,1,0:T(8,128)(2,1)S(1)} collective-permute-done((bf16[2,128,384]{2,1,0:T(8,128)(2,1)S(1)}, bf16[2,128,384]{2,1,0:T(8,128)(2,1)S(1)}, u32[]{:S(2)}, u32[]{:S(2)}) %collective-permute-start.1) | collective-permute-done | bytes 196640 | tf_op jit(solution)/shard_map/ppermute | solution.py:347
  25.9 6.0 %collective-permute-done.2.second_ref = bf16[2,128,384]{2,1,0:T(8,128)(2,1)S(1)} collective-permute-done((bf16[2,128,384]{2,1,0:T(8,128)(2,1)S(1)}, bf16[2,128,384]{2,1,0:T(8,128)(2,1)S(1)}, u32[]{:S(2)}, u32[]{:S(2)}) %collective-permute-start.2) | collective-permute-done | bytes 196640 | tf_op jit(solution)/shard_map/ppermute | solution.py:348
  31.8 2.7 %collective-permute-start.3 = (bf16[2,128,384]{2,1,0:T(8,128)(2,1)S(1)}, bf16[2,128,384]{2,1,0:T(8,128)(2,1)S(1)}, u32[]{:S(2)}, u32[]{:S(2)}) collective-permute-start(bf16[2,128,384]{2,1,0:T(8,128)(2,1)S(1)} %collective-permute-done.2.second_ref), channel_id=1, source_target_pairs={{0,56},{8,16},{16,8},{24,32},{32,24},{40,48},{48,40},{56,0},{64,12... | collective-permute-start | bytes 589832 | tf_op jit(solution)/shard_map/ppermute | solution.py:349
  34.5 4.2 %collective-permute-done.3.far_ref = bf16[2,128,384]{2,1,0:T(8,128)(2,1)S(1)} collective-permute-done((bf16[2,128,384]{2,1,0:T(8,128)(2,1)S(1)}, bf16[2,128,384]{2,1,0:T(8,128)(2,1)S(1)}, u32[]{:S(2)}, u32[]{:S(2)}) %collective-permute-start.3) | collective-permute-done | bytes 196640 | tf_op jit(solution)/shard_map/ppermute | solution.py:349
  38.7 1.8 %shard_map.66 = (f32[2,128,384]{2,1,0:T(8,128)S(1)}, bf16[2,128,384]{2,1,0:T(8,128)(2,1)S(1)}) custom-call(bf16[2,128,384]{2,1,0:T(8,128)(2,1)S(1)} %collective-permute-done.peer_ref, bf16[2,128,384]{2,1,0:T(8,128)(2,1)S(1)} %shard_map.65.pair_ref, bf16[2,128,384]{2,1,0:T(8,128)(2,1)S(1)} %collective-permute-done.1.first_ref, ...), custom_call_target="tpu_custom_call" | custom-call | flops 600000000 | bytes 1572864 | tf_op jit(solution)/shard_map/pallas_call | solution.py:259
  40.5 1.3 %collective-permute-start.4 = (bf16[2,128,384]{2,1,0:T(8,128)(2,1)S(1)}, bf16[2,128,384]{2,1,0:T(8,128)(2,1)S(1)}, u32[]{:S(2)}, u32[]{:S(2)}) collective-permute-start(bf16[2,128,384]{2,1,0:T(8,128)(2,1)S(1)} %get-tuple-element.32.own_ref), channel_id=1, source_target_pairs={{0,64},{8,72},{16,80},{24,88},{32,96},{40,104},{48,112},{56,120},{... | collective-permute-start | bytes 589832 | tf_op jit(solution)/shard_map/ppermute | solution.py:356
  41.8 3.6 %shard_map.67 = (bf16[8,128,128]{2,1,0:T(8,128)(2,1)S(1)}, f32[8,128,256]{2,1,0:T(8,128)S(1)}) custom-call(bf16[1024,128]{1,0:T(8,128)(2,1)S(1)} %bitcast.5, bf16[8,128,128]{2,1,0:T(8,128)(2,1)S(1)} %get-tuple-element.33.k_ref, f32[8,128]{1,0:T(8,128)S(1)} %get-tuple-element.34.scale_ref, f32[8,128,384]{2,1,0:T(8,128)S(1)} %get-tuple-element.35.wu_ref, ...), custom_call_target="tpu_custom_call" | custom-call | flops 2000000000 | bytes 4984832 | tf_op jit(solution)/shard_map/pallas_call | solution.py:259
  45.4 0.9 %collective-permute-done.4.peer_ref = bf16[2,128,384]{2,1,0:T(8,128)(2,1)S(1)} collective-permute-done((bf16[2,128,384]{2,1,0:T(8,128)(2,1)S(1)}, bf16[2,128,384]{2,1,0:T(8,128)(2,1)S(1)}, u32[]{:S(2)}, u32[]{:S(2)}) %collective-permute-start.4) | collective-permute-done | bytes 196640 | tf_op jit(solution)/shard_map/ppermute | solution.py:356
  46.5 1.5 %collective-permute-start.5 = (bf16[2,128,256]{2,1,0:T(8,128)(2,1)S(1)}, bf16[2,128,256]{2,1,0:T(8,128)(2,1)S(1)}, u32[]{:S(2)}, u32[]{:S(2)}) collective-permute-start(bf16[2,128,256]{2,1,0:T(8,128)(2,1)S(1)} %shard_map.68), channel_id=1, source_target_pairs={{0,192},{8,200},{16,208},{24,216},{32,224},{40,232},{48,240},{56,2... | collective-permute-start | bytes 393224 | tf_op jit(solution)/shard_map/ppermute | solution.py:365
  47.9 5.4 %collective-permute-done.5.passed_ref = bf16[2,128,256]{2,1,0:T(8,128)(2,1)S(1)} collective-permute-done((bf16[2,128,256]{2,1,0:T(8,128)(2,1)S(1)}, bf16[2,128,256]{2,1,0:T(8,128)(2,1)S(1)}, u32[]{:S(2)}, u32[]{:S(2)}) %collective-permute-start.5) | collective-permute-done | bytes 131104 | tf_op jit(solution)/shard_map/ppermute | solution.py:365
  53.3 0.8 %shard_map.69 = (bf16[256,512]{1,0:T(8,128)(2,1)S(1)}, bf16[256,512]{1,0:T(8,128)(2,1)S(1)}) custom-call(bf16[2,128,384]{2,1,0:T(8,128)(2,1)S(1)} %collective-permute-done.4.peer_ref, bf16[2,128,256]{2,1,0:T(8,128)(2,1)S(1)} %collective-permute-done.5.passed_ref, f32[2,128,384]{2,1,0:T(8,128)S(1)} %get-tuple-element.40.before_ref, ...), custom_call_target="tpu_custom_call" | custom-call | flops 500000000 | bytes 2555904 | tf_op jit(solution)/shard_map/pallas_call | solution.py:259
  54.3 1.5 %collective-permute-done.6.joined_ref = bf16[256,512]{1,0:T(8,128)(2,1)S(1)} collective-permute-done((bf16[256,512]{1,0:T(8,128)(2,1)S(1)}, bf16[256,512]{1,0:T(8,128)(2,1)S(1)}, u32[]{:S(2)}, u32[]{:S(2)}) %collective-permute-start.6) | collective-permute-done | bytes 262176 | tf_op jit(solution)/shard_map/ppermute | solution.py:374
  55.8 0.7 shard_map.70
  56.5 1.7 %collective-permute-start.8 = (bf16[128,1024]{1,0:T(8,128)(2,1)S(1)}, bf16[128,1024]{1,0:T(8,128)(2,1)S(1)}, u32[]{:S(2)}, u32[]{:S(2)}) collective-permute-start(bf16[128,1024]{1,0:T(8,128)(2,1)S(1)} %get-tuple-element.52), channel_id=1, source_target_pairs={{0,2},{1,3},{2,0},{3,1},{4,6},{5,7},{6,4},{7,5},{8,10},{9,11},{10,... | collective-permute-start | bytes 786440 | tf_op jit(solution)/shard_map/ppermute | solution.py:386
  58.2 2.2 %collective-permute-start.10 = (bf16[128,1024]{1,0:T(8,128)(2,1)S(1)}, bf16[128,1024]{1,0:T(8,128)(2,1)S(1)}, u32[]{:S(2)}, u32[]{:S(2)}) collective-permute-start(bf16[128,1024]{1,0:T(8,128)(2,1)S(1)} %get-tuple-element.54), channel_id=1, source_target_pairs={{0,6},{1,7},{2,4},{3,5},{4,2},{5,3},{6,0},{7,1},{8,14},{9,15},{10,... | collective-permute-start | bytes 786440 | tf_op jit(solution)/shard_map/ppermute | solution.py:387
  60.4 0.7 shard_map.71
  61.1 0.8 collective-permute-start.9
  61.9 0.6 collective-permute-start.11
  62.5 1.3 %shard_map.72 = (bf16[64,4096]{1,0:T(8,128)(2,1)S(1)}, bf16[64,4096]{1,0:T(8,128)(2,1)S(1)}) custom-call(bf16[256,512]{1,0:T(8,128)(2,1)S(1)} %get-tuple-element.50.keep_ref, bf16[256,512]{1,0:T(8,128)(2,1)S(1)} %collective-permute-done.6.joined_ref, bf16[512,4096]{1,0:T(8,128)(2,1)S(1)} %copy-done, bf16[512,4096]{1,0:T(8,128)(2,1)S(1)} %collective-permute-done.7.other_w_ref), custom_call_target="tpu_custom_call" | custom-call | flops 1000000000 | bytes 9961472 | tf_op jit(solution)/shard_map/pallas_call | solution.py:259
  63.8 2.0 %collective-permute-done.8.sent_ref.refs_1_ = bf16[128,1024]{1,0:T(8,128)(2,1)S(1)} collective-permute-done((bf16[128,1024]{1,0:T(8,128)(2,1)S(1)}, bf16[128,1024]{1,0:T(8,128)(2,1)S(1)}, u32[]{:S(2)}, u32[]{:S(2)}) %collective-permute-start.8) | collective-permute-done | bytes 262176 | tf_op jit(solution)/shard_map/ppermute | solution.py:386
  65.8 3.1 %collective-permute-start.12 = (bf16[64,1024]{1,0:T(8,128)(2,1)S(1)}, bf16[64,1024]{1,0:T(8,128)(2,1)S(1)}, u32[]{:S(2)}, u32[]{:S(2)}) collective-permute-start(bf16[64,1024]{1,0:T(8,128)(2,1)S(1)} %shard_map.73), channel_id=1, source_target_pairs={{0,6},{1,7},{2,4},{3,5},{4,2},{5,3},{6,0},{7,1},{8,14},{9,15},{10,... | collective-permute-start | bytes 393224 | tf_op jit(solution)/shard_map/ppermute | solution.py:399
  69.2 2.0 %collective-permute-done.9.sent_ref.refs_2_ = bf16[128,1024]{1,0:T(8,128)(2,1)S(1)} collective-permute-done((bf16[128,1024]{1,0:T(8,128)(2,1)S(1)}, bf16[128,1024]{1,0:T(8,128)(2,1)S(1)}, u32[]{:S(2)}, u32[]{:S(2)}) %collective-permute-start.9) | collective-permute-done | bytes 262176 | tf_op jit(solution)/shard_map/ppermute | solution.py:386
  71.3 3.3 %collective-permute-start.13 = (bf16[64,1024]{1,0:T(8,128)(2,1)S(1)}, bf16[64,1024]{1,0:T(8,128)(2,1)S(1)}, u32[]{:S(2)}, u32[]{:S(2)}) collective-permute-start(bf16[64,1024]{1,0:T(8,128)(2,1)S(1)} %shard_map.74), channel_id=1, source_target_pairs={{0,6},{1,7},{2,4},{3,5},{4,2},{5,3},{6,0},{7,1},{8,14},{9,15},{10,... | collective-permute-start | bytes 393224 | tf_op jit(solution)/shard_map/ppermute | solution.py:399
  74.8 2.2 %collective-permute-done.12.refs_5_ = bf16[64,1024]{1,0:T(8,128)(2,1)S(1)} collective-permute-done((bf16[64,1024]{1,0:T(8,128)(2,1)S(1)}, bf16[64,1024]{1,0:T(8,128)(2,1)S(1)}, u32[]{:S(2)}, u32[]{:S(2)}) %collective-permute-start.12) | collective-permute-done | bytes 131104 | tf_op jit(solution)/shard_map/ppermute | solution.py:399
  77.1 1.7 %collective-permute-done.13.refs_6_ = bf16[64,1024]{1,0:T(8,128)(2,1)S(1)} collective-permute-done((bf16[64,1024]{1,0:T(8,128)(2,1)S(1)}, bf16[64,1024]{1,0:T(8,128)(2,1)S(1)}, u32[]{:S(2)}, u32[]{:S(2)}) %collective-permute-start.13) | collective-permute-done | bytes 131104 | tf_op jit(solution)/shard_map/ppermute | solution.py:399
  78.7 0.9 %collective-permute-done.15.refs_8_ = bf16[64,1024]{1,0:T(8,128)(2,1)S(1)} collective-permute-done((bf16[64,1024]{1,0:T(8,128)(2,1)S(1)}, bf16[64,1024]{1,0:T(8,128)(2,1)S(1)}, u32[]{:S(2)}, u32[]{:S(2)}) %collective-permute-start.15) | collective-permute-done | bytes 131104 | tf_op jit(solution)/shard_map/ppermute | solution.py:399
  79.7 1.0 %shard_map.77 = bf16[64,4096]{1,0:T(8,128)(2,1)} custom-call(bf16[64,4096]{1,0:T(8,128)(2,1)S(1)} %get-tuple-element.51.refs_0_, bf16[128,1024]{1,0:T(8,128)(2,1)S(1)} %collective-permute-done.8.sent_ref.refs_1_, bf16[128,1024]{1,0:T(8,128)(2,1)S(1)} %collective-permute-done.9.sent_ref.refs_2_, ...), custom_call_target="tpu_custom_call" | custom-call | flops 1000000 | bytes 2621440 | tf_op jit(solution)/shard_map/pallas_call | solution.py:259
  (19 shorter events, 1.2 us)
Async XLA Ops:
  0.0 55.8 %collective-permute-start.7 = (bf16[512,4096]{1,0:T(8,128)(2,1)}, bf16[512,4096]{1,0:T(8,128)(2,1)S(1)}, u32[]{:S(2)}, u32[]{:S(2)}) collective-permute-start(bf16[512,4096]{1,0:T(8,128)(2,1)} %own_w_ref.5), channel_id=1, source_target_pairs={{0,1},{1,0},{2,3},{3,2},{4,5},{5,4},{6,7},{7,6},{8,9},{9,8},{10,11... | collective-permute-start | bytes 12582920 | tf_op jit(solution)/shard_map/ppermute | solution.py:319
  1.1 40.7 %copy-start.1 = (bf16[512,2,128]{2,1,0:T(2,128)(2,1)S(1)}, bf16[512,2,128]{2,1,0:T(2,128)(2,1)}, u32[]{:S(2)}) copy-start(bf16[512,2,128]{2,1,0:T(2,128)(2,1)} %param.6) | copy-start | bytes 786436
  7.5 7.6 %collective-permute-start = (bf16[2,128,384]{2,1,0:T(8,128)(2,1)S(1)}, bf16[2,128,384]{2,1,0:T(8,128)(2,1)S(1)}, u32[]{:S(2)}, u32[]{:S(2)}) collective-permute-start(bf16[2,128,384]{2,1,0:T(8,128)(2,1)S(1)} %get-tuple-element.31.own_ref), channel_id=1, source_target_pairs={{0,8},{8,0},{16,24},{24,16},{32,40},{40,32},{48,56},{56,48},{64,72... | collective-permute-start | bytes 589832 | tf_op jit(solution)/shard_map/ppermute | solution.py:343
  15.3 10.6 %collective-permute-start.1 = (bf16[2,128,384]{2,1,0:T(8,128)(2,1)S(1)}, bf16[2,128,384]{2,1,0:T(8,128)(2,1)S(1)}, u32[]{:S(2)}, u32[]{:S(2)}) collective-permute-start(bf16[2,128,384]{2,1,0:T(8,128)(2,1)S(1)} %shard_map.65.pair_ref), channel_id=1, source_target_pairs={{0,56},{8,16},{16,8},{24,32},{32,24},{40,48},{48,40},{56,0},{64,12... | collective-permute-start | bytes 589832 | tf_op jit(solution)/shard_map/ppermute | solution.py:347
  25.9 6.0 %collective-permute-start.2 = (bf16[2,128,384]{2,1,0:T(8,128)(2,1)S(1)}, bf16[2,128,384]{2,1,0:T(8,128)(2,1)S(1)}, u32[]{:S(2)}, u32[]{:S(2)}) collective-permute-start(bf16[2,128,384]{2,1,0:T(8,128)(2,1)S(1)} %collective-permute-done.1.first_ref), channel_id=1, source_target_pairs={{0,8},{8,0},{16,24},{24,16},{32,40},{40,32},{48,56},{56,48},{64,72... | collective-permute-start | bytes 589832 | tf_op jit(solution)/shard_map/ppermute | solution.py:348
  31.8 6.9 %collective-permute-start.3 = (bf16[2,128,384]{2,1,0:T(8,128)(2,1)S(1)}, bf16[2,128,384]{2,1,0:T(8,128)(2,1)S(1)}, u32[]{:S(2)}, u32[]{:S(2)}) collective-permute-start(bf16[2,128,384]{2,1,0:T(8,128)(2,1)S(1)} %collective-permute-done.2.second_ref), channel_id=1, source_target_pairs={{0,56},{8,16},{16,8},{24,32},{32,24},{40,48},{48,40},{56,0},{64,12... | collective-permute-start | bytes 589832 | tf_op jit(solution)/shard_map/ppermute | solution.py:349
  40.5 5.8 %collective-permute-start.4 = (bf16[2,128,384]{2,1,0:T(8,128)(2,1)S(1)}, bf16[2,128,384]{2,1,0:T(8,128)(2,1)S(1)}, u32[]{:S(2)}, u32[]{:S(2)}) collective-permute-start(bf16[2,128,384]{2,1,0:T(8,128)(2,1)S(1)} %get-tuple-element.32.own_ref), channel_id=1, source_target_pairs={{0,64},{8,72},{16,80},{24,88},{32,96},{40,104},{48,112},{56,120},{... | collective-permute-start | bytes 589832 | tf_op jit(solution)/shard_map/ppermute | solution.py:356
  41.8 14.0 %copy-start = (bf16[512,4096]{1,0:T(8,128)(2,1)S(1)}, bf16[512,4096]{1,0:T(8,128)(2,1)}, u32[]{:S(2)}) copy-start(bf16[512,4096]{1,0:T(8,128)(2,1)} %own_w_ref.5) | copy-start | bytes 12582916
  46.5 6.9 %collective-permute-start.5 = (bf16[2,128,256]{2,1,0:T(8,128)(2,1)S(1)}, bf16[2,128,256]{2,1,0:T(8,128)(2,1)S(1)}, u32[]{:S(2)}, u32[]{:S(2)}) collective-permute-start(bf16[2,128,256]{2,1,0:T(8,128)(2,1)S(1)} %shard_map.68), channel_id=1, source_target_pairs={{0,192},{8,200},{16,208},{24,216},{32,224},{40,232},{48,240},{56,2... | collective-permute-start | bytes 393224 | tf_op jit(solution)/shard_map/ppermute | solution.py:365
  54.2 1.6 %collective-permute-start.6 = (bf16[256,512]{1,0:T(8,128)(2,1)S(1)}, bf16[256,512]{1,0:T(8,128)(2,1)S(1)}, u32[]{:S(2)}, u32[]{:S(2)}) collective-permute-start(bf16[256,512]{1,0:T(8,128)(2,1)S(1)} %get-tuple-element.44), channel_id=1, source_target_pairs={{0,1},{1,0},{2,3},{3,2},{4,5},{5,4},{6,7},{7,6},{8,9},{9,8},{10,11... | collective-permute-start | bytes 786440 | tf_op jit(solution)/shard_map/ppermute | solution.py:374
  56.5 9.2 %collective-permute-start.8 = (bf16[128,1024]{1,0:T(8,128)(2,1)S(1)}, bf16[128,1024]{1,0:T(8,128)(2,1)S(1)}, u32[]{:S(2)}, u32[]{:S(2)}) collective-permute-start(bf16[128,1024]{1,0:T(8,128)(2,1)S(1)} %get-tuple-element.52), channel_id=1, source_target_pairs={{0,2},{1,3},{2,0},{3,1},{4,6},{5,7},{6,4},{7,5},{8,10},{9,11},{10,... | collective-permute-start | bytes 786440 | tf_op jit(solution)/shard_map/ppermute | solution.py:386
  58.2 10.7 %collective-permute-start.10 = (bf16[128,1024]{1,0:T(8,128)(2,1)S(1)}, bf16[128,1024]{1,0:T(8,128)(2,1)S(1)}, u32[]{:S(2)}, u32[]{:S(2)}) collective-permute-start(bf16[128,1024]{1,0:T(8,128)(2,1)S(1)} %get-tuple-element.54), channel_id=1, source_target_pairs={{0,6},{1,7},{2,4},{3,5},{4,2},{5,3},{6,0},{7,1},{8,14},{9,15},{10,... | collective-permute-start | bytes 786440 | tf_op jit(solution)/shard_map/ppermute | solution.py:387
  61.1 10.1 %collective-permute-start.9 = (bf16[128,1024]{1,0:T(8,128)(2,1)S(1)}, bf16[128,1024]{1,0:T(8,128)(2,1)S(1)}, u32[]{:S(2)}, u32[]{:S(2)}) collective-permute-start(bf16[128,1024]{1,0:T(8,128)(2,1)S(1)} %get-tuple-element.53), channel_id=1, source_target_pairs={{0,2},{1,3},{2,0},{3,1},{4,6},{5,7},{6,4},{7,5},{8,10},{9,11},{10,... | collective-permute-start | bytes 786440 | tf_op jit(solution)/shard_map/ppermute | solution.py:386
  61.9 12.7 %collective-permute-start.11 = (bf16[128,1024]{1,0:T(8,128)(2,1)S(1)}, bf16[128,1024]{1,0:T(8,128)(2,1)S(1)}, u32[]{:S(2)}, u32[]{:S(2)}) collective-permute-start(bf16[128,1024]{1,0:T(8,128)(2,1)S(1)} %get-tuple-element.55), channel_id=1, source_target_pairs={{0,6},{1,7},{2,4},{3,5},{4,2},{5,3},{6,0},{7,1},{8,14},{9,15},{10,... | collective-permute-start | bytes 786440 | tf_op jit(solution)/shard_map/ppermute | solution.py:387
  65.8 11.2 %collective-permute-start.12 = (bf16[64,1024]{1,0:T(8,128)(2,1)S(1)}, bf16[64,1024]{1,0:T(8,128)(2,1)S(1)}, u32[]{:S(2)}, u32[]{:S(2)}) collective-permute-start(bf16[64,1024]{1,0:T(8,128)(2,1)S(1)} %shard_map.73), channel_id=1, source_target_pairs={{0,6},{1,7},{2,4},{3,5},{4,2},{5,3},{6,0},{7,1},{8,14},{9,15},{10,... | collective-permute-start | bytes 393224 | tf_op jit(solution)/shard_map/ppermute | solution.py:399
  69.0 8.1 %collective-permute-start.14 = (bf16[64,1024]{1,0:T(8,128)(2,1)S(1)}, bf16[64,1024]{1,0:T(8,128)(2,1)S(1)}, u32[]{:S(2)}, u32[]{:S(2)}) collective-permute-start(bf16[64,1024]{1,0:T(8,128)(2,1)S(1)} %shard_map.75), channel_id=1, source_target_pairs={{0,2},{1,3},{2,0},{3,1},{4,6},{5,7},{6,4},{7,5},{8,10},{9,11},{10,... | collective-permute-start | bytes 393224 | tf_op jit(solution)/shard_map/ppermute | solution.py:399
  71.3 7.5 %collective-permute-start.13 = (bf16[64,1024]{1,0:T(8,128)(2,1)S(1)}, bf16[64,1024]{1,0:T(8,128)(2,1)S(1)}, u32[]{:S(2)}, u32[]{:S(2)}) collective-permute-start(bf16[64,1024]{1,0:T(8,128)(2,1)S(1)} %shard_map.74), channel_id=1, source_target_pairs={{0,6},{1,7},{2,4},{3,5},{4,2},{5,3},{6,0},{7,1},{8,14},{9,15},{10,... | collective-permute-start | bytes 393224 | tf_op jit(solution)/shard_map/ppermute | solution.py:399
  74.6 5.1 %collective-permute-start.15 = (bf16[64,1024]{1,0:T(8,128)(2,1)S(1)}, bf16[64,1024]{1,0:T(8,128)(2,1)S(1)}, u32[]{:S(2)}, u32[]{:S(2)}) collective-permute-start(bf16[64,1024]{1,0:T(8,128)(2,1)S(1)} %shard_map.76), channel_id=1, source_target_pairs={{0,2},{1,3},{2,0},{3,1},{4,6},{5,7},{6,4},{7,5},{8,10},{9,11},{10,... | collective-permute-start | bytes 393224 | tf_op jit(solution)/shard_map/ppermute | solution.py:399

commit v7 on v6

--- a/solution.py
+++ b/solution.py
@@ -72,8 +72,9 @@
 
 
 def terms_kernel(resets_hbm, beta_hbm, k_hbm, v_ref, *refs):
-    wu_ref, prefix_ref, scale_ref, rows_ref, carry_ref = refs[:5]
-    resets, beta_ref, k_ref, sems = refs[5:]
+    wu_ref, prefix_ref, scale_ref, rows_ref = refs[:4]
+    carry_refs = refs[4:6]
+    resets, beta_ref, k_ref, sems = refs[6:]
     k_copy = pltpu.make_async_copy(k_hbm, k_ref, sems.at[2])
     resets_copy = pltpu.make_async_copy(resets_hbm, resets, sems.at[0])
     beta_copy = pltpu.make_async_copy(beta_hbm, beta_ref, sems.at[1])
@@ -139,7 +140,7 @@
         first = after_map(maps[0, h], maps[1, h])
         last = after_map(maps[2, h], maps[3, h])
         whole = after_map(first, last)
-        carry_ref[h] = jnp.concatenate(
+        carry_refs[h][...] = jnp.concatenate(
             [whole[:, :128] - identity, whole[:, 128:]], 1
         ).astype(BF16)
         prefix_ref[h] = jnp.concatenate([identity, zeros], 1) * kept[0]
@@ -184,24 +185,25 @@
     row, col = square_ids(BLOCK)
     identity = jnp.where(row == col, 1.0, 0.0).astype(F32)
     upper = lax.axis_index("seq") % 2 == 1
-    for h in range(2):
-        early = jnp.where(upper, peer_ref[h], own_ref[h])
-        late = jnp.where(upper, own_ref[h], peer_ref[h])
-        both = follow(whole_map(early, identity), late)
-        out_ref[h] = jnp.concatenate([both[:, :128] - identity, both[:, 128:]], 1).astype(BF16)
-
-
-def group_kernel(peer_ref, pair_ref, first_ref, second_ref, far_ref, before_ref, total_ref):
+    early = jnp.where(upper, peer_ref[...], own_ref[...])
+    late = jnp.where(upper, own_ref[...], peer_ref[...])
+    both = follow(whole_map(early, identity), late)
+    out_ref[...] = jnp.concatenate([both[:, :128] - identity, both[:, 128:]], 1).astype(BF16)
+
+
+def group_kernel(*refs):
+    before_ref, total_ref = refs[10:]
     row, col = square_ids(BLOCK)
     identity = jnp.where(row == col, 1.0, 0.0).astype(F32)
     empty = jnp.concatenate([identity, jnp.zeros((BLOCK, 256), F32)], 1)
     z = lax.axis_index("seq") % 8
     place, upper = z // 2, z % 2 == 1
     for h in range(2):
-        below = jnp.where(upper, second_ref[h], first_ref[h])
-        above = jnp.where(upper, first_ref[h], second_ref[h])
+        peer, pair, first, second, far = (ref[...] for ref in refs[5 * h : 5 * h + 5])
+        below = jnp.where(upper, second, first)
+        above = jnp.where(upper, first, second)
         state = after = empty
-        for step, element in ((1, above), (2, far_ref[h]), (3, below)):
+        for step, element in ((1, above), (2, far), (3, below)):
             wraps = place + step == 4
             if step > 1:
                 after = jnp.where(wraps, state, after)
@@ -209,9 +211,9 @@
             state = follow(state, element)
         after = jnp.where(place == 0, state, after)
         state = jnp.where(place == 0, empty, state)
-        before = jnp.where(upper, follow(state, peer_ref[h]), state)
+        before = jnp.where(upper, follow(state, peer), state)
         before_ref[h] = jnp.concatenate([before[:, :128] - identity, before[:, 128:]], 1)
-        through = follow(state, pair_ref[h])
+        through = follow(state, pair)
         total = dot3(after[:, :128], through)
         total_ref[h] = jnp.concatenate(
             [total[:, :128] - identity, total[:, 128:] + after[:, 128:]], 1
@@ -319,14 +321,15 @@
     other_weight = lax.ppermute(out_weight, "head", across)
 
     shaped = jax.ShapeDtypeStruct
-    wu, prefix, scale, rows, carry = call(
+    wu, prefix, scale, rows, *carries = call(
         terms_kernel,
         [
             shaped((8, 128, 384), F32),
             shaped((8, 128, 384), F32),
             shaped((8, 128), F32),
             shaped((8, 128, 128), BF16),
-            shaped((2, 128, 384), BF16),
+            shaped((128, 384), BF16),
+            shaped((128, 384), BF16),
         ],
         [v],
         3_000_000_000,
@@ -340,17 +343,20 @@
     )
     inside = [(i, i ^ 1) for i in range(32)]
     outward = [(i, i - i % 8 + (i % 8 + (1 if i % 2 else 7)) % 8) for i in range(32)]
-    neighbour = lax.ppermute(carry, "seq", inside)
-    (pair,) = call(
-        pair_map_kernel, [shaped((2, 128, 384), BF16)], [carry, neighbour], 100_000_000
-    )
-    first = lax.ppermute(pair, "seq", outward)
-    second = lax.ppermute(first, "seq", inside)
-    farthest = lax.ppermute(second, "seq", outward)
+    gathered = []
+    for carry in carries:
+        neighbour = lax.ppermute(carry, "seq", inside)
+        (pair,) = call(
+            pair_map_kernel, [shaped((128, 384), BF16)], [carry, neighbour], 100_000_000
+        )
+        first = lax.ppermute(pair, "seq", outward)
+        second = lax.ppermute(first, "seq", inside)
+        farthest = lax.ppermute(second, "seq", outward)
+        gathered += [neighbour, pair, first, second, farthest]
     before, total = call(
         group_kernel,
         [shaped((2, 128, 384), F32), shaped((2, 128, 384), BF16)],
-        [neighbour, pair, first, second, farthest],
+        gathered,
         600_000_000,
     )
     peer = lax.ppermute(total, "seq", [(i, i ^ 8) for i in range(32)])

time: 82 us -> 80.7 us (0.984)
  waiting for transfers between devices: 37.1 us -> 31.8 us
  starting transfers between devices: 25.5 us -> 29.2 us
    ppermute x1 -> x2, waiting for transfers between devices: 5.95 us -> 2.05 us  [body(): second = lax.ppermute(first, 'seq', inside)]
    ppermute x1 -> x2, starting transfers between devices: 2.66 us -> 4.91 us  [body(): farthest = lax.ppermute(second, 'seq', outward)]
    ppermute x1 -> x2, waiting for transfers between devices: 5.57 us -> 3.64 us  [body(): neighbour = lax.ppermute(carry, 'seq', inside)]
    ppermute x1 -> x2, starting transfers between devices: 5.77 us -> 7.36 us  [body(): first = lax.ppermute(pair, 'seq', outward)]
    ppermute x1 -> x2, waiting for transfers between devices: 4.22 us -> 4.78 us  [body(): farthest = lax.ppermute(second, 'seq', outward)]
    ppermute x1 -> x2, waiting for transfers between devices: 4.79 us -> 4.42 us  [body(): first = lax.ppermute(pair, 'seq', outward)]
    pallas_call x14 -> x15, Pallas kernels: 16.8 us -> 17 us  [call(): pl.pallas_call(kernel, out_shape=[jax.ShapeDtypeStruct(a.shape, a.dtype)...]
    ppermute x1 -> x2, starting transfers between devices: 2.01 us -> 2.11 us  [body(): neighbour = lax.ppermute(carry, 'seq', inside)]
  transfers between devices with their start and end apart: 16 -> 20, of which waited for: 12 -> 14; matrix products, arithmetic and copies ran while one was open for 1% -> 1% of each run, Pallas kernels for 19% -> 19%
where the time goes in v7:
time: 80.7 us; the launch traced here: 79.3 us
  waiting for transfers between devices  31.8 us (39%)
  starting transfers between devices  29.2 us (36%)
  Pallas kernels  17 us (21%)
  local copies, waits for them, and re-layouts  1.13 us (1%)
    pallas_call x15, Pallas kernels, call(): pl.pallas_call(kernel, out_shape=[jax.ShapeDtypeStruct(a.shape, a.dtype)...  17 us
    ppermute x2, starting transfers between devices, body(): first = lax.ppermute(pair, 'seq', outward)  7.36 us
    ppermute x4, starting transfers between devices, body(): received[part] = lax.ppermute(summed, 'head', routes[3 - part])  6.76 us
    ppermute x1, waiting for transfers between devices, body(): lax.ppermute(joint, 'seq', [(z + 8 * x, z + 8 * (3 - x)) for x in (0, 1)...  5.56 us
    ppermute x2, starting transfers between devices, body(): farthest = lax.ppermute(second, 'seq', outward)  4.91 us
    ppermute x4, waiting for transfers between devices, body(): received[part] = lax.ppermute(summed, 'head', routes[3 - part])  4.83 us
    ppermute x2, waiting for transfers between devices, body(): farthest = lax.ppermute(second, 'seq', outward)  4.78 us
    ppermute x2, waiting for transfers between devices, body(): first = lax.ppermute(pair, 'seq', outward)  4.42 us
  transfers between devices with their start and end apart: 20, of which 14 were waited for; matrix products, arithmetic and copies ran while one was open for 1% of the time, Pallas kernels for 19%

profile of v7, /device:TPU:4, one launch (start us, length us, event | category | flops | bytes accessed | tf_op | source)
XLA Modules:
  0.0 79.3 jit_solution(15639760428214546558)
XLA Ops:
  0.0 1.1 %copy.7 = bf16[64,8,2,256]{3,1,2,0:T(8,128)(2,1)S(1)} copy(bf16[64,8,2,256]{3,2,1,0:T(2,128)(2,1)} %bitcast.6) | data formatting | bytes 1048576
  1.1 6.3 %shard_map.64 = (f32[8,128,384]{2,1,0:T(8,128)S(1)}, f32[8,128,384]{2,1,0:T(8,128)S(1)}, f32[8,128]{1,0:T(8,128)S(1)}, bf16[8,128,128]{2,1,0:T(8,128)(2,1)S(1)},...) custom-call(s32[1,2]{1,0:T(1,128)} %resets_hbm.1, f32[2,512]{1,0:T(2,128)} %beta_hbm.1, ...), custom_call_target="tpu_custom_call" | custom-call | flops 3000000000 | bytes 4399112 | tf_op jit(solution)/shard_map/pallas_call | solution.py:261
  7.5 2.0 %collective-permute-start = (bf16[128,384]{1,0:T(8,128)(2,1)S(1)}, bf16[128,384]{1,0:T(8,128)(2,1)S(1)}, u32[]{:S(2)}, u32[]{:S(2)}) collective-permute-start(bf16[128,384]{1,0:T(8,128)(2,1)S(1)} %get-tuple-element.32.own_ref), channel_id=1, source_target_pairs={{0,8},{8,0},{16,24},{24,16},{32,40},{40,32},{48,56},{56,48},{64,72... | collective-permute-start | bytes 294920 | tf_op jit(solution)/shard_map/ppermute | solution.py:348
  9.6 3.6 %collective-permute-done.peer_ref.refs_0_ = bf16[128,384]{1,0:T(8,128)(2,1)S(1)} collective-permute-done((bf16[128,384]{1,0:T(8,128)(2,1)S(1)}, bf16[128,384]{1,0:T(8,128)(2,1)S(1)}, u32[]{:S(2)}, u32[]{:S(2)}) %collective-permute-start) | collective-permute-done | bytes 98336 | tf_op jit(solution)/shard_map/ppermute | solution.py:348
  13.4 5.9 %collective-permute-start.1 = (bf16[128,384]{1,0:T(8,128)(2,1)S(1)}, bf16[128,384]{1,0:T(8,128)(2,1)S(1)}, u32[]{:S(2)}, u32[]{:S(2)}) collective-permute-start(bf16[128,384]{1,0:T(8,128)(2,1)S(1)} %shard_map.65.refs_1_), channel_id=1, source_target_pairs={{0,56},{8,16},{16,8},{24,32},{32,24},{40,48},{48,40},{56,0},{64,12... | collective-permute-start | bytes 294920 | tf_op jit(solution)/shard_map/ppermute | solution.py:352
  19.5 1.5 %collective-permute-start.5 = (bf16[128,384]{1,0:T(8,128)(2,1)S(1)}, bf16[128,384]{1,0:T(8,128)(2,1)S(1)}, u32[]{:S(2)}, u32[]{:S(2)}) collective-permute-start(bf16[128,384]{1,0:T(8,128)(2,1)S(1)} %shard_map.66.refs_6_), channel_id=1, source_target_pairs={{0,56},{8,16},{16,8},{24,32},{32,24},{40,48},{48,40},{56,0},{64,12... | collective-permute-start | bytes 294920 | tf_op jit(solution)/shard_map/ppermute | solution.py:352
  21.0 1.1 %collective-permute-done.1.refs_2_ = bf16[128,384]{1,0:T(8,128)(2,1)S(1)} collective-permute-done((bf16[128,384]{1,0:T(8,128)(2,1)S(1)}, bf16[128,384]{1,0:T(8,128)(2,1)S(1)}, u32[]{:S(2)}, u32[]{:S(2)}) %collective-permute-start.1) | collective-permute-done | bytes 98336 | tf_op jit(solution)/shard_map/ppermute | solution.py:352
  22.1 3.3 %collective-permute-done.5.refs_7_ = bf16[128,384]{1,0:T(8,128)(2,1)S(1)} collective-permute-done((bf16[128,384]{1,0:T(8,128)(2,1)S(1)}, bf16[128,384]{1,0:T(8,128)(2,1)S(1)}, u32[]{:S(2)}, u32[]{:S(2)}) %collective-permute-start.5) | collective-permute-done | bytes 98336 | tf_op jit(solution)/shard_map/ppermute | solution.py:352
  25.5 2.0 %collective-permute-done.2.refs_3_ = bf16[128,384]{1,0:T(8,128)(2,1)S(1)} collective-permute-done((bf16[128,384]{1,0:T(8,128)(2,1)S(1)}, bf16[128,384]{1,0:T(8,128)(2,1)S(1)}, u32[]{:S(2)}, u32[]{:S(2)}) %collective-permute-start.2) | collective-permute-done | bytes 98336 | tf_op jit(solution)/shard_map/ppermute | solution.py:353
  27.5 3.9 %collective-permute-start.3 = (bf16[128,384]{1,0:T(8,128)(2,1)S(1)}, bf16[128,384]{1,0:T(8,128)(2,1)S(1)}, u32[]{:S(2)}, u32[]{:S(2)}) collective-permute-start(bf16[128,384]{1,0:T(8,128)(2,1)S(1)} %collective-permute-done.2.refs_3_), channel_id=1, source_target_pairs={{0,56},{8,16},{16,8},{24,32},{32,24},{40,48},{48,40},{56,0},{64,12... | collective-permute-start | bytes 294920 | tf_op jit(solution)/shard_map/ppermute | solution.py:354
  31.4 1.0 %collective-permute-start.7 = (bf16[128,384]{1,0:T(8,128)(2,1)S(1)}, bf16[128,384]{1,0:T(8,128)(2,1)S(1)}, u32[]{:S(2)}, u32[]{:S(2)}) collective-permute-start(bf16[128,384]{1,0:T(8,128)(2,1)S(1)} %collective-permute-done.6.refs_8_), channel_id=1, source_target_pairs={{0,56},{8,16},{16,8},{24,32},{32,24},{40,48},{48,40},{56,0},{64,12... | collective-permute-start | bytes 294920 | tf_op jit(solution)/shard_map/ppermute | solution.py:354
  32.4 1.9 %collective-permute-done.3.refs_4_ = bf16[128,384]{1,0:T(8,128)(2,1)S(1)} collective-permute-done((bf16[128,384]{1,0:T(8,128)(2,1)S(1)}, bf16[128,384]{1,0:T(8,128)(2,1)S(1)}, u32[]{:S(2)}, u32[]{:S(2)}) %collective-permute-start.3) | collective-permute-done | bytes 98336 | tf_op jit(solution)/shard_map/ppermute | solution.py:354
  34.3 2.9 %collective-permute-done.7.refs_9_ = bf16[128,384]{1,0:T(8,128)(2,1)S(1)} collective-permute-done((bf16[128,384]{1,0:T(8,128)(2,1)S(1)}, bf16[128,384]{1,0:T(8,128)(2,1)S(1)}, u32[]{:S(2)}, u32[]{:S(2)}) %collective-permute-start.7) | collective-permute-done | bytes 98336 | tf_op jit(solution)/shard_map/ppermute | solution.py:354
  37.2 1.8 %shard_map.67 = (f32[2,128,384]{2,1,0:T(8,128)S(1)}, bf16[2,128,384]{2,1,0:T(8,128)(2,1)S(1)}) custom-call(bf16[128,384]{1,0:T(8,128)(2,1)S(1)} %collective-permute-done.peer_ref.refs_0_, bf16[128,384]{1,0:T(8,128)(2,1)S(1)} %shard_map.65.refs_1_, bf16[128,384]{1,0:T(8,128)(2,1)S(1)} %collective-permute-done.1.refs_2_, ...), custom_call_target="tpu_custom_call" | custom-call | flops 600000000 | bytes 1572864 | tf_op jit(solution)/shard_map/pallas_call | solution.py:261
  39.0 1.5 %collective-permute-start.8 = (bf16[2,128,384]{2,1,0:T(8,128)(2,1)S(1)}, bf16[2,128,384]{2,1,0:T(8,128)(2,1)S(1)}, u32[]{:S(2)}, u32[]{:S(2)}) collective-permute-start(bf16[2,128,384]{2,1,0:T(8,128)(2,1)S(1)} %get-tuple-element.34.own_ref), channel_id=1, source_target_pairs={{0,64},{8,72},{16,80},{24,88},{32,96},{40,104},{48,112},{56,120},{... | collective-permute-start | bytes 589832 | tf_op jit(solution)/shard_map/ppermute | solution.py:362
  40.4 3.6 %shard_map.68 = (bf16[8,128,128]{2,1,0:T(8,128)(2,1)S(1)}, f32[8,128,256]{2,1,0:T(8,128)S(1)}) custom-call(bf16[1024,128]{1,0:T(8,128)(2,1)S(1)} %bitcast.5, bf16[8,128,128]{2,1,0:T(8,128)(2,1)S(1)} %get-tuple-element.35.k_ref, f32[8,128]{1,0:T(8,128)S(1)} %get-tuple-element.36.scale_ref, f32[8,128,384]{2,1,0:T(8,128)S(1)} %get-tuple-element.37.wu_ref, ...), custom_call_target="tpu_custom_call" | custom-call | flops 2000000000 | bytes 4984832 | tf_op jit(solution)/shard_map/pallas_call | solution.py:261
  44.0 0.9 %collective-permute-done.8.peer_ref = bf16[2,128,384]{2,1,0:T(8,128)(2,1)S(1)} collective-permute-done((bf16[2,128,384]{2,1,0:T(8,128)(2,1)S(1)}, bf16[2,128,384]{2,1,0:T(8,128)(2,1)S(1)}, u32[]{:S(2)}, u32[]{:S(2)}) %collective-permute-start.8) | collective-permute-done | bytes 196640 | tf_op jit(solution)/shard_map/ppermute | solution.py:362
  45.1 1.3 %collective-permute-start.9 = (bf16[2,128,256]{2,1,0:T(8,128)(2,1)S(1)}, bf16[2,128,256]{2,1,0:T(8,128)(2,1)S(1)}, u32[]{:S(2)}, u32[]{:S(2)}) collective-permute-start(bf16[2,128,256]{2,1,0:T(8,128)(2,1)S(1)} %shard_map.69), channel_id=1, source_target_pairs={{0,192},{8,200},{16,208},{24,216},{32,224},{40,232},{48,240},{56,2... | collective-permute-start | bytes 393224 | tf_op jit(solution)/shard_map/ppermute | solution.py:371
  46.4 5.6 %collective-permute-done.9.passed_ref = bf16[2,128,256]{2,1,0:T(8,128)(2,1)S(1)} collective-permute-done((bf16[2,128,256]{2,1,0:T(8,128)(2,1)S(1)}, bf16[2,128,256]{2,1,0:T(8,128)(2,1)S(1)}, u32[]{:S(2)}, u32[]{:S(2)}) %collective-permute-start.9) | collective-permute-done | bytes 131104 | tf_op jit(solution)/shard_map/ppermute | solution.py:371
  52.0 0.8 %shard_map.70 = (bf16[256,512]{1,0:T(8,128)(2,1)S(1)}, bf16[256,512]{1,0:T(8,128)(2,1)S(1)}) custom-call(bf16[2,128,384]{2,1,0:T(8,128)(2,1)S(1)} %collective-permute-done.8.peer_ref, bf16[2,128,256]{2,1,0:T(8,128)(2,1)S(1)} %collective-permute-done.9.passed_ref, f32[2,128,384]{2,1,0:T(8,128)S(1)} %get-tuple-element.42.before_ref, ...), custom_call_target="tpu_custom_call" | custom-call | flops 500000000 | bytes 2555904 | tf_op jit(solution)/shard_map/pallas_call | solution.py:261
  53.0 1.5 %collective-permute-done.10.joined_ref = bf16[256,512]{1,0:T(8,128)(2,1)S(1)} collective-permute-done((bf16[256,512]{1,0:T(8,128)(2,1)S(1)}, bf16[256,512]{1,0:T(8,128)(2,1)S(1)}, u32[]{:S(2)}, u32[]{:S(2)}) %collective-permute-start.10) | collective-permute-done | bytes 262176 | tf_op jit(solution)/shard_map/ppermute | solution.py:380
  55.2 1.7 %collective-permute-start.12 = (bf16[128,1024]{1,0:T(8,128)(2,1)S(1)}, bf16[128,1024]{1,0:T(8,128)(2,1)S(1)}, u32[]{:S(2)}, u32[]{:S(2)}) collective-permute-start(bf16[128,1024]{1,0:T(8,128)(2,1)S(1)} %get-tuple-element.54), channel_id=1, source_target_pairs={{0,2},{1,3},{2,0},{3,1},{4,6},{5,7},{6,4},{7,5},{8,10},{9,11},{10,... | collective-permute-start | bytes 786440 | tf_op jit(solution)/shard_map/ppermute | solution.py:392
  56.9 2.2 %collective-permute-start.14 = (bf16[128,1024]{1,0:T(8,128)(2,1)S(1)}, bf16[128,1024]{1,0:T(8,128)(2,1)S(1)}, u32[]{:S(2)}, u32[]{:S(2)}) collective-permute-start(bf16[128,1024]{1,0:T(8,128)(2,1)S(1)} %get-tuple-element.56), channel_id=1, source_target_pairs={{0,6},{1,7},{2,4},{3,5},{4,2},{5,3},{6,0},{7,1},{8,14},{9,15},{10,... | collective-permute-start | bytes 786440 | tf_op jit(solution)/shard_map/ppermute | solution.py:393
  61.2 1.3 %shard_map.73 = (bf16[64,4096]{1,0:T(8,128)(2,1)S(1)}, bf16[64,4096]{1,0:T(8,128)(2,1)S(1)}) custom-call(bf16[256,512]{1,0:T(8,128)(2,1)S(1)} %get-tuple-element.52.keep_ref, bf16[256,512]{1,0:T(8,128)(2,1)S(1)} %collective-permute-done.10.joined_ref, bf16[512,4096]{1,0:T(8,128)(2,1)S(1)} %copy-done, bf16[512,4096]{1,0:T(8,128)(2,1)S(1)} %collective-permute-done.11.other_w_ref), custom_call_target="tpu_custom_call" | custom-call | flops 1000000000 | bytes 9961472 | tf_op jit(solution)/shard_map/pallas_call | solution.py:261
  62.4 2.0 %collective-permute-done.12.sent_ref.refs_1_ = bf16[128,1024]{1,0:T(8,128)(2,1)S(1)} collective-permute-done((bf16[128,1024]{1,0:T(8,128)(2,1)S(1)}, bf16[128,1024]{1,0:T(8,128)(2,1)S(1)}, u32[]{:S(2)}, u32[]{:S(2)}) %collective-permute-start.12) | collective-permute-done | bytes 262176 | tf_op jit(solution)/shard_map/ppermute | solution.py:392
  64.5 3.1 %collective-permute-start.16 = (bf16[64,1024]{1,0:T(8,128)(2,1)S(1)}, bf16[64,1024]{1,0:T(8,128)(2,1)S(1)}, u32[]{:S(2)}, u32[]{:S(2)}) collective-permute-start(bf16[64,1024]{1,0:T(8,128)(2,1)S(1)} %shard_map.74), channel_id=1, source_target_pairs={{0,6},{1,7},{2,4},{3,5},{4,2},{5,3},{6,0},{7,1},{8,14},{9,15},{10,... | collective-permute-start | bytes 393224 | tf_op jit(solution)/shard_map/ppermute | solution.py:405
  67.9 2.1 %collective-permute-done.13.sent_ref.refs_2_ = bf16[128,1024]{1,0:T(8,128)(2,1)S(1)} collective-permute-done((bf16[128,1024]{1,0:T(8,128)(2,1)S(1)}, bf16[128,1024]{1,0:T(8,128)(2,1)S(1)}, u32[]{:S(2)}, u32[]{:S(2)}) %collective-permute-start.13) | collective-permute-done | bytes 262176 | tf_op jit(solution)/shard_map/ppermute | solution.py:392
  70.0 3.2 %collective-permute-start.17 = (bf16[64,1024]{1,0:T(8,128)(2,1)S(1)}, bf16[64,1024]{1,0:T(8,128)(2,1)S(1)}, u32[]{:S(2)}, u32[]{:S(2)}) collective-permute-start(bf16[64,1024]{1,0:T(8,128)(2,1)S(1)} %shard_map.75), channel_id=1, source_target_pairs={{0,6},{1,7},{2,4},{3,5},{4,2},{5,3},{6,0},{7,1},{8,14},{9,15},{10,... | collective-permute-start | bytes 393224 | tf_op jit(solution)/shard_map/ppermute | solution.py:405
  73.5 2.2 %collective-permute-done.16.refs_5_ = bf16[64,1024]{1,0:T(8,128)(2,1)S(1)} collective-permute-done((bf16[64,1024]{1,0:T(8,128)(2,1)S(1)}, bf16[64,1024]{1,0:T(8,128)(2,1)S(1)}, u32[]{:S(2)}, u32[]{:S(2)}) %collective-permute-start.16) | collective-permute-done | bytes 131104 | tf_op jit(solution)/shard_map/ppermute | solution.py:405
  75.7 1.7 %collective-permute-done.17.refs_6_ = bf16[64,1024]{1,0:T(8,128)(2,1)S(1)} collective-permute-done((bf16[64,1024]{1,0:T(8,128)(2,1)S(1)}, bf16[64,1024]{1,0:T(8,128)(2,1)S(1)}, u32[]{:S(2)}, u32[]{:S(2)}) %collective-permute-start.17) | collective-permute-done | bytes 131104 | tf_op jit(solution)/shard_map/ppermute | solution.py:405
  77.4 0.9 %collective-permute-done.19.refs_8_ = bf16[64,1024]{1,0:T(8,128)(2,1)S(1)} collective-permute-done((bf16[64,1024]{1,0:T(8,128)(2,1)S(1)}, bf16[64,1024]{1,0:T(8,128)(2,1)S(1)}, u32[]{:S(2)}, u32[]{:S(2)}) %collective-permute-start.19) | collective-permute-done | bytes 131104 | tf_op jit(solution)/shard_map/ppermute | solution.py:405
  78.3 1.0 %shard_map.78 = bf16[64,4096]{1,0:T(8,128)(2,1)} custom-call(bf16[64,4096]{1,0:T(8,128)(2,1)S(1)} %get-tuple-element.53.refs_0_, bf16[128,1024]{1,0:T(8,128)(2,1)S(1)} %collective-permute-done.12.sent_ref.refs_1_, bf16[128,1024]{1,0:T(8,128)(2,1)S(1)} %collective-permute-done.13.sent_ref.refs_2_, ...), custom_call_target="tpu_custom_call" | custom-call | flops 1000000 | bytes 2621440 | tf_op jit(solution)/shard_map/pallas_call | solution.py:261
  (28 shorter events, 4.3 us)
Async XLA Ops:
  0.0 54.5 %collective-permute-start.11 = (bf16[512,4096]{1,0:T(8,128)(2,1)}, bf16[512,4096]{1,0:T(8,128)(2,1)S(1)}, u32[]{:S(2)}, u32[]{:S(2)}) collective-permute-start(bf16[512,4096]{1,0:T(8,128)(2,1)} %own_w_ref.5), channel_id=1, source_target_pairs={{0,1},{1,0},{2,3},{3,2},{4,5},{5,4},{6,7},{7,6},{8,9},{9,8},{10,11... | collective-permute-start | bytes 12582920 | tf_op jit(solution)/shard_map/ppermute | solution.py:321
  1.1 39.3 %copy-start.1 = (bf16[512,2,128]{2,1,0:T(2,128)(2,1)S(1)}, bf16[512,2,128]{2,1,0:T(2,128)(2,1)}, u32[]{:S(2)}) copy-start(bf16[512,2,128]{2,1,0:T(2,128)(2,1)} %param.6) | copy-start | bytes 786436
  7.5 5.8 %collective-permute-start = (bf16[128,384]{1,0:T(8,128)(2,1)S(1)}, bf16[128,384]{1,0:T(8,128)(2,1)S(1)}, u32[]{:S(2)}, u32[]{:S(2)}) collective-permute-start(bf16[128,384]{1,0:T(8,128)(2,1)S(1)} %get-tuple-element.32.own_ref), channel_id=1, source_target_pairs={{0,8},{8,0},{16,24},{24,16},{32,40},{40,32},{48,56},{56,48},{64,72... | collective-permute-start | bytes 294920 | tf_op jit(solution)/shard_map/ppermute | solution.py:348
  9.5 9.8 %collective-permute-start.4 = (bf16[128,384]{1,0:T(8,128)(2,1)S(1)}, bf16[128,384]{1,0:T(8,128)(2,1)S(1)}, u32[]{:S(2)}, u32[]{:S(2)}) collective-permute-start(bf16[128,384]{1,0:T(8,128)(2,1)S(1)} %get-tuple-element.33.own_ref), channel_id=1, source_target_pairs={{0,8},{8,0},{16,24},{24,16},{32,40},{40,32},{48,56},{56,48},{64,72... | collective-permute-start | bytes 294920 | tf_op jit(solution)/shard_map/ppermute | solution.py:348
  13.4 8.7 %collective-permute-start.1 = (bf16[128,384]{1,0:T(8,128)(2,1)S(1)}, bf16[128,384]{1,0:T(8,128)(2,1)S(1)}, u32[]{:S(2)}, u32[]{:S(2)}) collective-permute-start(bf16[128,384]{1,0:T(8,128)(2,1)S(1)} %shard_map.65.refs_1_), channel_id=1, source_target_pairs={{0,56},{8,16},{16,8},{24,32},{32,24},{40,48},{48,40},{56,0},{64,12... | collective-permute-start | bytes 294920 | tf_op jit(solution)/shard_map/ppermute | solution.py:352
  19.5 5.9 %collective-permute-start.5 = (bf16[128,384]{1,0:T(8,128)(2,1)S(1)}, bf16[128,384]{1,0:T(8,128)(2,1)S(1)}, u32[]{:S(2)}, u32[]{:S(2)}) collective-permute-start(bf16[128,384]{1,0:T(8,128)(2,1)S(1)} %shard_map.66.refs_6_), channel_id=1, source_target_pairs={{0,56},{8,16},{16,8},{24,32},{32,24},{40,48},{48,40},{56,0},{64,12... | collective-permute-start | bytes 294920 | tf_op jit(solution)/shard_map/ppermute | solution.py:352
  22.1 5.4 %collective-permute-start.2 = (bf16[128,384]{1,0:T(8,128)(2,1)S(1)}, bf16[128,384]{1,0:T(8,128)(2,1)S(1)}, u32[]{:S(2)}, u32[]{:S(2)}) collective-permute-start(bf16[128,384]{1,0:T(8,128)(2,1)S(1)} %collective-permute-done.1.refs_2_), channel_id=1, source_target_pairs={{0,8},{8,0},{16,24},{24,16},{32,40},{40,32},{48,56},{56,48},{64,72... | collective-permute-start | bytes 294920 | tf_op jit(solution)/shard_map/ppermute | solution.py:353
  25.5 5.9 %collective-permute-start.6 = (bf16[128,384]{1,0:T(8,128)(2,1)S(1)}, bf16[128,384]{1,0:T(8,128)(2,1)S(1)}, u32[]{:S(2)}, u32[]{:S(2)}) collective-permute-start(bf16[128,384]{1,0:T(8,128)(2,1)S(1)} %collective-permute-done.5.refs_7_), channel_id=1, source_target_pairs={{0,8},{8,0},{16,24},{24,16},{32,40},{40,32},{48,56},{56,48},{64,72... | collective-permute-start | bytes 294920 | tf_op jit(solution)/shard_map/ppermute | solution.py:353
  27.5 6.8 %collective-permute-start.3 = (bf16[128,384]{1,0:T(8,128)(2,1)S(1)}, bf16[128,384]{1,0:T(8,128)(2,1)S(1)}, u32[]{:S(2)}, u32[]{:S(2)}) collective-permute-start(bf16[128,384]{1,0:T(8,128)(2,1)S(1)} %collective-permute-done.2.refs_3_), channel_id=1, source_target_pairs={{0,56},{8,16},{16,8},{24,32},{32,24},{40,48},{48,40},{56,0},{64,12... | collective-permute-start | bytes 294920 | tf_op jit(solution)/shard_map/ppermute | solution.py:354
  31.4 5.8 %collective-permute-start.7 = (bf16[128,384]{1,0:T(8,128)(2,1)S(1)}, bf16[128,384]{1,0:T(8,128)(2,1)S(1)}, u32[]{:S(2)}, u32[]{:S(2)}) collective-permute-start(bf16[128,384]{1,0:T(8,128)(2,1)S(1)} %collective-permute-done.6.refs_8_), channel_id=1, source_target_pairs={{0,56},{8,16},{16,8},{24,32},{32,24},{40,48},{48,40},{56,0},{64,12... | collective-permute-start | bytes 294920 | tf_op jit(solution)/shard_map/ppermute | solution.py:354
  39.0 5.9 %collective-permute-start.8 = (bf16[2,128,384]{2,1,0:T(8,128)(2,1)S(1)}, bf16[2,128,384]{2,1,0:T(8,128)(2,1)S(1)}, u32[]{:S(2)}, u32[]{:S(2)}) collective-permute-start(bf16[2,128,384]{2,1,0:T(8,128)(2,1)S(1)} %get-tuple-element.34.own_ref), channel_id=1, source_target_pairs={{0,64},{8,72},{16,80},{24,88},{32,96},{40,104},{48,112},{56,120},{... | collective-permute-start | bytes 589832 | tf_op jit(solution)/shard_map/ppermute | solution.py:362
  40.4 14.1 %copy-start = (bf16[512,4096]{1,0:T(8,128)(2,1)S(1)}, bf16[512,4096]{1,0:T(8,128)(2,1)}, u32[]{:S(2)}) copy-start(bf16[512,4096]{1,0:T(8,128)(2,1)} %own_w_ref.5) | copy-start | bytes 12582916
  45.1 6.9 %collective-permute-start.9 = (bf16[2,128,256]{2,1,0:T(8,128)(2,1)S(1)}, bf16[2,128,256]{2,1,0:T(8,128)(2,1)S(1)}, u32[]{:S(2)}, u32[]{:S(2)}) collective-permute-start(bf16[2,128,256]{2,1,0:T(8,128)(2,1)S(1)} %shard_map.69), channel_id=1, source_target_pairs={{0,192},{8,200},{16,208},{24,216},{32,224},{40,232},{48,240},{56,2... | collective-permute-start | bytes 393224 | tf_op jit(solution)/shard_map/ppermute | solution.py:371
  52.9 1.6 %collective-permute-start.10 = (bf16[256,512]{1,0:T(8,128)(2,1)S(1)}, bf16[256,512]{1,0:T(8,128)(2,1)S(1)}, u32[]{:S(2)}, u32[]{:S(2)}) collective-permute-start(bf16[256,512]{1,0:T(8,128)(2,1)S(1)} %get-tuple-element.46), channel_id=1, source_target_pairs={{0,1},{1,0},{2,3},{3,2},{4,5},{5,4},{6,7},{7,6},{8,9},{9,8},{10,11... | collective-permute-start | bytes 786440 | tf_op jit(solution)/shard_map/ppermute | solution.py:380
  55.2 9.2 %collective-permute-start.12 = (bf16[128,1024]{1,0:T(8,128)(2,1)S(1)}, bf16[128,1024]{1,0:T(8,128)(2,1)S(1)}, u32[]{:S(2)}, u32[]{:S(2)}) collective-permute-start(bf16[128,1024]{1,0:T(8,128)(2,1)S(1)} %get-tuple-element.54), channel_id=1, source_target_pairs={{0,2},{1,3},{2,0},{3,1},{4,6},{5,7},{6,4},{7,5},{8,10},{9,11},{10,... | collective-permute-start | bytes 786440 | tf_op jit(solution)/shard_map/ppermute | solution.py:392
  56.9 10.7 %collective-permute-start.14 = (bf16[128,1024]{1,0:T(8,128)(2,1)S(1)}, bf16[128,1024]{1,0:T(8,128)(2,1)S(1)}, u32[]{:S(2)}, u32[]{:S(2)}) collective-permute-start(bf16[128,1024]{1,0:T(8,128)(2,1)S(1)} %get-tuple-element.56), channel_id=1, source_target_pairs={{0,6},{1,7},{2,4},{3,5},{4,2},{5,3},{6,0},{7,1},{8,14},{9,15},{10,... | collective-permute-start | bytes 786440 | tf_op jit(solution)/shard_map/ppermute | solution.py:393
  59.8 10.2 %collective-permute-start.13 = (bf16[128,1024]{1,0:T(8,128)(2,1)S(1)}, bf16[128,1024]{1,0:T(8,128)(2,1)S(1)}, u32[]{:S(2)}, u32[]{:S(2)}) collective-permute-start(bf16[128,1024]{1,0:T(8,128)(2,1)S(1)} %get-tuple-element.55), channel_id=1, source_target_pairs={{0,2},{1,3},{2,0},{3,1},{4,6},{5,7},{6,4},{7,5},{8,10},{9,11},{10,... | collective-permute-start | bytes 786440 | tf_op jit(solution)/shard_map/ppermute | solution.py:392
  60.5 12.7 %collective-permute-start.15 = (bf16[128,1024]{1,0:T(8,128)(2,1)S(1)}, bf16[128,1024]{1,0:T(8,128)(2,1)S(1)}, u32[]{:S(2)}, u32[]{:S(2)}) collective-permute-start(bf16[128,1024]{1,0:T(8,128)(2,1)S(1)} %get-tuple-element.57), channel_id=1, source_target_pairs={{0,6},{1,7},{2,4},{3,5},{4,2},{5,3},{6,0},{7,1},{8,14},{9,15},{10,... | collective-permute-start | bytes 786440 | tf_op jit(solution)/shard_map/ppermute | solution.py:393
  64.5 11.2 %collective-permute-start.16 = (bf16[64,1024]{1,0:T(8,128)(2,1)S(1)}, bf16[64,1024]{1,0:T(8,128)(2,1)S(1)}, u32[]{:S(2)}, u32[]{:S(2)}) collective-permute-start(bf16[64,1024]{1,0:T(8,128)(2,1)S(1)} %shard_map.74), channel_id=1, source_target_pairs={{0,6},{1,7},{2,4},{3,5},{4,2},{5,3},{6,0},{7,1},{8,14},{9,15},{10,... | collective-permute-start | bytes 393224 | tf_op jit(solution)/shard_map/ppermute | solution.py:405
  67.6 8.1 %collective-permute-start.18 = (bf16[64,1024]{1,0:T(8,128)(2,1)S(1)}, bf16[64,1024]{1,0:T(8,128)(2,1)S(1)}, u32[]{:S(2)}, u32[]{:S(2)}) collective-permute-start(bf16[64,1024]{1,0:T(8,128)(2,1)S(1)} %shard_map.76), channel_id=1, source_target_pairs={{0,2},{1,3},{2,0},{3,1},{4,6},{5,7},{6,4},{7,5},{8,10},{9,11},{10,... | collective-permute-start | bytes 393224 | tf_op jit(solution)/shard_map/ppermute | solution.py:405
  70.0 7.4 %collective-permute-start.17 = (bf16[64,1024]{1,0:T(8,128)(2,1)S(1)}, bf16[64,1024]{1,0:T(8,128)(2,1)S(1)}, u32[]{:S(2)}, u32[]{:S(2)}) collective-permute-start(bf16[64,1024]{1,0:T(8,128)(2,1)S(1)} %shard_map.75), channel_id=1, source_target_pairs={{0,6},{1,7},{2,4},{3,5},{4,2},{5,3},{6,0},{7,1},{8,14},{9,15},{10,... | collective-permute-start | bytes 393224 | tf_op jit(solution)/shard_map/ppermute | solution.py:405
  73.2 5.1 %collective-permute-start.19 = (bf16[64,1024]{1,0:T(8,128)(2,1)S(1)}, bf16[64,1024]{1,0:T(8,128)(2,1)S(1)}, u32[]{:S(2)}, u32[]{:S(2)}) collective-permute-start(bf16[64,1024]{1,0:T(8,128)(2,1)S(1)} %shard_map.77), channel_id=1, source_target_pairs={{0,2},{1,3},{2,0},{3,1},{4,6},{5,7},{6,4},{7,5},{8,10},{9,11},{10,... | collective-permute-start | bytes 393224 | tf_op jit(solution)/shard_map/ppermute | solution.py:405
